TPU v7x, 32 devices: a whole 2x2x4 slice. The times are simulated.
32 devices in a mesh: seq: 32 (over z, y, x, core), tp: 1.
Axes of the slice: x: 2, y: 2, z: 4, core: 2. Of those that a mesh axis runs over, the one named last changes fastest.
Arguments:
- queries: bfloat16 [4096, 4096], P('seq', 'tp'), may hold values from -128 to 128
- rotated_keys: bfloat16 [4096, 1024], P('seq', 'tp'), may hold values from -4.5 to 4.5
- values: bfloat16 [4096, 1024], P('seq', 'tp'), may hold values from -64 to 64
- decay_rates: float32 [64], P('tp'), may hold values from 2e-06 to 0.016
- decay_codes: int32 [4096, 64], P('seq', 'tp'), may hold values from 1 to 4096
- gate_input: bfloat16 [4096, 4096], P('seq', 'tp'), may hold values from -64 to 64
- norm_gain: float32 [4096], P('tp'), may hold values from 0.1 to 1.9
- bc_weight: bfloat16 [4096, 256], P('tp'), may hold values from -0.09375 to 0.09375
Outputs:
- first_pass: float32 [4096, 4096], P('seq', 'tp')
- second_pass: float32 [4096, 4096], P('seq', 'tp')
All inputs are finite; a program needn't handle non-finite values.
Results may differ from a plain program's by a relative error of at most 0.017.
Values may be sent and summed in bfloat16 or wider, within the bound.
No kernel may reach another device: no remote copies, remote signals or barrier semaphores. Data moves between devices by JAX's collectives and lax.ppermute only.
A program may use at most 128 MiB of HBM per device.

v0:
```python
import math

import jax
import jax.numpy as jnp
from jax import lax
from jax.sharding import PartitionSpec as P

QUERY_HEADS = 32
KEY_VALUE_HEADS = 8
HEAD_SIZE = 128
SH = 64
SP = 64
NS = 128
WINDOW_LENGTH = 2048
STRETCH = 128


EPSILON = 1e-05


def shifted(block, axis, distance):
    devices = range(lax.axis_size(axis))
    route = [(i - distance, i) for i in devices if i - distance in devices]
    return lax.ppermute(block, axis, route)


def prefix(x, axis, combine, identity):
    peers, index = (lax.axis_size(axis), lax.axis_index(axis))
    everything = jax.tree.map(lambda part: lax.all_gather(part, axis), x)
    start = jax.tree.map(
        lambda part, zero: jnp.broadcast_to(jnp.asarray(zero, part.dtype), part.shape), x, identity
    )

    def step(k, before):
        reached = k < index
        new = combine(before, jax.tree.map(lambda part: part[k], everything))
        return jax.tree.map(lambda a, b: jnp.where(reached, a, b), new, before)

    return lax.fori_loop(0, peers, step, start)


def combine_states(earlier, later):
    return (earlier[0] * later[0], later[0][..., None, None] * earlier[1] + later[1])


def attention(queries, rotated_keys, values):
    tok_rows = queries.shape[0]
    seq_index = lax.axis_index("seq")
    reach = WINDOW_LENGTH // tok_rows
    kv_local = rotated_keys.shape[1] // HEAD_SIZE
    group_length = QUERY_HEADS // KEY_VALUE_HEADS
    paired = jnp.stack([rotated_keys, values], 0)
    moving = paired
    arrived = []
    for counter in range(reach):
        moving = shifted(moving, "seq", 1)
        arrived.append(moving)
    kv_blocks = arrived[::-1]
    window_kv = jnp.concatenate(kv_blocks + [paired], 1)
    grouped = queries.reshape(tok_rows, kv_local, group_length, HEAD_SIZE)
    score_scale = 1.0 / math.sqrt(HEAD_SIZE)
    query_pos = seq_index * tok_rows + jnp.arange(tok_rows, dtype=jnp.int32)
    base_pos = (seq_index - reach) * tok_rows

    def block_scores(key_block):
        key_row_block = lax.dynamic_slice_in_dim(
            window_kv[0], key_block * tok_rows, tok_rows, 0
        ).reshape(tok_rows, kv_local, HEAD_SIZE)
        scores = (
            jnp.einsum("tkgd,skd->kgts", grouped, key_row_block, preferred_element_type=jnp.float32)
            * score_scale
        )
        key_pos = base_pos + key_block * tok_rows + jnp.arange(tok_rows, dtype=jnp.int32)
        allowed = (
            (key_pos[None, :] <= query_pos[:, None])
            & (key_pos[None, :] > query_pos[:, None] - WINDOW_LENGTH)
            & (key_pos[None, :] >= 0)
        )
        return jnp.where(allowed[None, None], scores, -jnp.inf)

    def visit_order(counter):
        return (counter + reach) % (reach + 1)

    def totals(counter, running):
        row_max, row_sum = running
        scores = block_scores(visit_order(counter))
        new_max = jnp.maximum(row_max, jnp.max(scores, axis=3))
        rescale = jnp.exp(row_max - new_max)
        row_sum = row_sum * rescale + jnp.sum(jnp.exp(scores - new_max[..., None]), axis=3)
        return (new_max, row_sum)

    max_init = jnp.full((kv_local, group_length, tok_rows), -jnp.inf, jnp.float32)
    row_max, row_sum = lax.fori_loop(0, reach + 1, totals, (max_init, jnp.zeros_like(max_init)))

    def weighted(counter, accumulated):
        key_block = visit_order(counter)
        scores = block_scores(key_block)
        value_row_block = lax.dynamic_slice_in_dim(
            window_kv[1], key_block * tok_rows, tok_rows, 0
        ).reshape(tok_rows, kv_local, HEAD_SIZE)
        probs = (jnp.exp(scores - row_max[..., None]) / row_sum[..., None]).astype(jnp.bfloat16)
        return accumulated + jnp.einsum(
            "kgts,skd->kgtd", probs, value_row_block, preferred_element_type=jnp.float32
        )

    acc_init = jnp.zeros((kv_local, group_length, tok_rows, HEAD_SIZE), jnp.float32)
    accumulated = lax.fori_loop(0, reach + 1, weighted, acc_init)
    mixed_rows = jnp.transpose(accumulated, (2, 0, 1, 3))
    return mixed_rows.astype(jnp.bfloat16).reshape(tok_rows, kv_local * group_length * HEAD_SIZE)


def core(inputs, decay_rates, decay_codes, gate_input, norm_gain, bc_weight):
    tok_rows = inputs.shape[0]
    head_count = decay_rates.shape[0]
    channels = SH * SP
    as_float = inputs.astype(jnp.float32)
    own_squares = jnp.sum(as_float * as_float, axis=1)
    partial_value = jnp.dot(inputs, bc_weight, preferred_element_type=jnp.float32)
    total_squares = lax.psum(own_squares, "tp")
    spread = jnp.sqrt(total_squares / channels + EPSILON)[:, None]
    projected = lax.psum(partial_value / spread, "tp")
    normed = (as_float / spread).astype(jnp.bfloat16)
    projected = projected.astype(jnp.bfloat16)
    stretch_count = tok_rows // STRETCH
    x_stretches = normed.reshape(stretch_count, STRETCH, head_count, SP)
    b_stretches = projected[:, :NS].reshape(stretch_count, STRETCH, NS)
    c_stretches = projected[:, NS:].reshape(stretch_count, STRETCH, NS)
    summed_codes = jnp.cumsum(
        decay_codes.reshape(stretch_count, STRETCH, head_count), axis=1, dtype=jnp.int32
    )
    log_decay = -decay_rates * summed_codes.astype(jnp.float32)
    decay_by_head = jnp.transpose(log_decay, (0, 2, 1))
    gram_matrix = jnp.einsum(
        "ctn,csn->cts", c_stretches, b_stretches, preferred_element_type=jnp.float32
    )
    lower_mask = jnp.arange(STRETCH)[:, None] >= jnp.arange(STRETCH)[None, :]
    decay_gaps = jnp.where(
        lower_mask, decay_by_head[..., :, None] - decay_by_head[..., None, :], 0.0
    )
    mixing = jnp.where(lower_mask, gram_matrix[:, None] * jnp.exp(decay_gaps), 0.0).astype(
        jnp.bfloat16
    )
    y_local = jnp.einsum("chts,cshp->cthp", mixing, x_stretches, preferred_element_type=jnp.float32)
    tail_decay = jnp.exp(decay_by_head[..., -1:] - decay_by_head)
    b_weighted = (b_stretches.astype(jnp.float32)[:, None] * tail_decay[..., None]).astype(
        jnp.bfloat16
    )
    contrib = jnp.einsum(
        "chsn,cshp->chnp", b_weighted, x_stretches, preferred_element_type=jnp.float32
    )
    stretch_decay = jnp.exp(decay_by_head[..., -1])
    carried_decay = jnp.ones((head_count,), jnp.float32)
    carried_state = jnp.zeros((head_count, NS, SP), jnp.float32)
    carried_state = stretch_decay[0][:, None, None] * carried_state + contrib[0]
    carried_decay = carried_decay * stretch_decay[0]
    unused_decay, entering = prefix(
        (carried_decay, carried_state),
        "seq",
        combine_states,
        (jnp.ones_like(carried_decay), jnp.zeros_like(carried_state)),
    )
    states = [entering]
    stacked = jnp.stack(states, 0)
    c_weighted = c_stretches.astype(jnp.float32)[:, None] * jnp.exp(decay_by_head)[..., None]
    y_carried = jnp.einsum(
        "chtn,chnp->cthp",
        c_weighted,
        stacked,
        precision=lax.Precision.HIGHEST,
        preferred_element_type=jnp.float32,
    )
    outputs = (y_local + y_carried).reshape(tok_rows, head_count * SP)
    gated_out = outputs * jax.nn.silu(gate_input.astype(jnp.float32))
    gate_squares = lax.psum(jnp.sum(gated_out * gated_out, axis=1), "tp")
    out_scale = jnp.sqrt(gate_squares / channels + EPSILON)[:, None]
    return gated_out / out_scale * norm_gain


def on_device(
    queries, rotated_keys, values, decay_rates, decay_codes, gate_input, norm_gain, bc_weight
):
    attended = attention(queries, rotated_keys, values)
    first_pass = core(attended, decay_rates, decay_codes, gate_input, norm_gain, bc_weight)
    pass_input = first_pass.astype(jnp.bfloat16)
    second_pass = core(pass_input, decay_rates, decay_codes, gate_input, norm_gain, bc_weight)
    return (first_pass, second_pass)


def solution(mesh):
    return jax.shard_map(
        on_device,
        mesh=mesh,
        in_specs=(
            P("seq", "tp"),
            P("seq", "tp"),
            P("seq", "tp"),
            P("tp"),
            P("seq", "tp"),
            P("seq", "tp"),
            P("tp"),
            P("tp", None),
        ),
        out_specs=(P("seq", "tp"), P("seq", "tp")),
        check_vma=False,
    )
```

profile of v0, /device:TPU:0, one launch (start us, length us, event | category | flops | bytes accessed | tf_op | source)
XLA Modules:
  0.0 2111.0 jit_solution(12588788853938628870)
XLA Ops:
  13.6 9.1 collective-permute-start.1
  25.0 9.0 collective-permute-start.2
  36.3 9.0 collective-permute-start.3
  47.6 9.0 collective-permute-start.4
  58.9 9.0 collective-permute-start.5
  70.2 9.0 collective-permute-start.6
  81.5 9.0 collective-permute-start.7
  92.8 9.0 collective-permute-start.8
  104.1 9.0 collective-permute-start.9
  115.3 9.0 collective-permute-start.10
  126.6 9.0 collective-permute-start.11
  137.9 9.1 collective-permute-start.12
  149.4 10.7 collective-permute-start.13
  160.9 10.6 collective-permute-start.14
  172.5 10.8 collective-permute-start.15
  203.0 114.7 %while.62 = (s32[]{:T(128)}, f32[8,4,128]{2,1,0:T(4,128)S(1)}, f32[8,4,128]{2,1,0:T(4,128)S(1)}, s32[]{:T(128)}, bf16[2,2176,1024]{1,2,0:T(8,128)(2,1)}, /*index...) while((s32[]{:T(128)}, f32[8,4,128]{2,1,0:T(4,128)S(1)}, ...), condition=%wide.region_3.4_spmd.clone, body=%wide.region_0.3_spmd.clone.sunk | while | flops 137974416 | bytes 15207960 | solution.py:93
  317.7 178.7 %while.63 = (s32[]{:T(128)}, f32[8,4,128,128]{3,2,1,0:T(8,128)}, s32[]{:T(128)}, bf16[2,2176,1024]{1,2,0:T(8,128)(2,1)}, bf16[128,8,4,128]{3,0,2,1:T(8,128)(2,1)...) while((s32[]{:T(128)}, f32[8,4,128,128]{3,2,1,0:T(8,128)}, ...), condition=%wide.region_5.6_spmd.clone, body=%wide.region_4.5_spmd.clone.sunk | while | flops 272171648 | bytes 33099344 | solution.py:107
  505.0 60.6 %all-gather = f32[32,64,1]{1,2,0:T(1,128)S(1)} all-gather(f32[1,64,1]{1,2,0:T(1,128)} %get-tuple-element.811), channel_id=2, replica_groups=mesh['seq'=32,'tp'=1] {'seq'}, dimensions={0}, use_global_device_ids=true | all-gather | bytes 8448 | tf_op jit(solution)/shard_map/all_gather | solution.py:29
  569.7 314.1 %all-gather.6.cloned.1.call-done = f32[2048,128,64]{1,2,0:T(8,128)} async-done(((f32[64,128,64]{1,2,0:T(8,128)}), f32[2048,128,64]{1,2,0:T(8,128)}) %all-gather.6.cloned.1.call-update) | async-done | bytes 67108880 | tf_op jit(solution)/shard_map/all_gather | solution.py:29
  883.9 417.4 %while.64 = (s32[]{:T(128)}, f32[64,128,64]{2,1,0:T(8,128)}, s32[]{:T(128)}, f32[32,64]{1,0:T(8,128)S(1)}, f32[32,64,128,64]{2,3,1,0:T(8,128)}, /*index=5*/s32[]{:T(128)}, s32[]{:T(128)}) while((s32[]{:T(128)}, f32[64,128,64]{2,1,0:T(8,128)}, s32[]{:T(128)}, f32[32,64]{1,0:T(8,128)S(1)}, f32[32,64,128,64]{2,3,1,0:T(8,128)}, ...), condition=%wide.region_9.10_spmd.clone, body=%wide.region_8.9_spmd.clone.sunk | while | flops 2097156 | bytes 14680937 | solution.py:39
  902.7 6.1 fusion.103
  915.8 6.1 fusion.103
  928.9 6.1 fusion.103
  955.0 6.1 fusion.103
  968.1 6.1 fusion.103
  981.2 6.1 fusion.103
  994.3 6.1 fusion.103
  1020.4 6.1 fusion.103
  1301.3 10.0 fusion.52
  1325.1 347.1 %all-gather.8.cloned.1.call-done = f32[2048,128,64]{1,2,0:T(8,128)} async-done(((f32[64,128,64]{1,2,0:T(8,128)}), f32[2048,128,64]{1,2,0:T(8,128)}) %all-gather.8.cloned.1.call-update) | async-done | bytes 67108880 | tf_op jit(solution)/shard_map/all_gather | solution.py:29
  1672.3 416.4 %while.65 = (s32[]{:T(128)}, f32[64,128,64]{2,1,0:T(8,128)}, s32[]{:T(128)}, f32[32,64]{1,0:T(8,128)S(1)}, f32[32,64,128,64]{2,3,1,0:T(8,128)}, /*index=5*/s32[]{:T(128)}, s32[]{:T(128)}) while((s32[]{:T(128)}, f32[64,128,64]{2,1,0:T(8,128)}, s32[]{:T(128)}, f32[32,64]{1,0:T(8,128)S(1)}, f32[32,64,128,64]{2,3,1,0:T(8,128)}, ...), condition=%wide.region_13.14_spmd.clone, body=%wide.region_12.13_spmd.clone.sunk | while | flops 2097156 | bytes 14680937 | solution.py:39
  2088.7 10.0 fusion.55
  (795 shorter events, 1163.3 us)
Async XLA Ops:
  7.2 491.9 %copy-start = (bf16[4096,256]{1,0:T(8,128)(2,1)S(1)}, bf16[4096,256]{1,0:T(8,128)(2,1)}, u32[]{:S(2)}) copy-start(bf16[4096,256]{1,0:T(8,128)(2,1)} %param.23) | copy-start | bytes 6291460
  7.2 164.3 %copy-start.39 = (s32[128,64]{0,1:T(8,128)S(1)}, s32[128,64]{0,1:T(8,128)}, u32[]{:S(2)}) copy-start(s32[128,64]{0,1:T(8,128)} %param.20) | copy-start | bytes 98308
  7.2 164.4 %copy-start.45 = (f32[64]{0:T(128)S(1)}, f32[64]{0:T(128)}, u32[]{:S(2)}) copy-start(f32[64]{0:T(128)} %param.19) | copy-start | bytes 772
  7.2 876.7 %all-gather.6.cloned.1.call-start = ((), (), s32[]{:S(2)}) async-start(), calls=%async_computation | async-start | bytes 69206016 | tf_op jit(solution)/shard_map/all_gather | solution.py:29
  9.6 176.5 %copy-start.6 = (bf16[128,1024]{0,1:T(8,128)(2,1)}, bf16[128,1024]{0,1:T(8,128)(2,1)S(1)}, u32[]{:S(2)}) copy-start(bf16[128,1024]{0,1:T(8,128)(2,1)S(1)} %copy.65) | copy-start | bytes 786436
  9.7 3.9 collective-permute-start
  13.6 172.5 %copy-start.9 = (bf16[2,128,1024]{1,2,0:T(8,128)(2,1)}, bf16[2,128,1024]{1,2,0:T(8,128)(2,1)S(1)}, u32[]{:S(2)}) copy-start(bf16[2,128,1024]{1,2,0:T(8,128)(2,1)S(1)} %collective-permute-done) | copy-start | bytes 1572868
  13.6 10.6 collective-permute-start.1
  25.0 10.5 collective-permute-start.2
  36.3 10.5 collective-permute-start.3
  47.6 10.5 collective-permute-start.4
  58.9 10.5 collective-permute-start.5
  70.2 10.5 collective-permute-start.6
  81.5 10.5 collective-permute-start.7
  92.8 10.5 collective-permute-start.8
  104.1 10.5 collective-permute-start.9
  115.3 10.5 collective-permute-start.10
  126.6 10.5 collective-permute-start.11
  137.9 10.6 collective-permute-start.12
  149.4 11.5 collective-permute-start.13
  160.9 11.6 collective-permute-start.14
  171.6 16.2 copy-start.40
  172.4 13.7 copy-start.36
  172.5 19.6 collective-permute-start.15
  190.8 5.0 copy-start.34
  344.2 4.4 copy-start.3
  375.9 4.4 copy-start.3
  407.5 4.4 copy-start.3
  428.6 4.4 copy-start.3
  439.2 4.4 copy-start.3
  470.8 4.4 copy-start.3
  502.5 1169.8 %all-gather.8.cloned.1.call-start = ((), (), s32[]{:S(2)}) async-start(), calls=%async_computation.1 | async-start | bytes 69206016 | tf_op jit(solution)/shard_map/all_gather | solution.py:29
  (64 other events, 110.4 us)
Sparse Core Ops, SparseCore 0:
  502.6 381.2 all-gather.5
  1318.4 353.8 all-gather.7
where the time goes:
time: 2120 us; the launch traced here: 2110 us
  waiting for transfers between devices  682 us (32%)
  local copies, waits for them, and re-layouts  633 us (30%)
  other arithmetic  436 us (21%)
  starting transfers between devices  143 us (7%)
  matrix products  140 us (7%)
  blocking collectives  60.6 us (3%)
    all_gather x2, waiting for transfers between devices, prefix(): everything = jax.tree.map(lambda part: lax.all_gather(part, axis), x)  661 us
    dynamic_slice x128, local copies, waits for them, and re-layouts, step(): new = combine(before, jax.tree.map(lambda part: part[k], everything))  446 us
    select_n x64, other arithmetic, step(): return jax.tree.map(lambda a, b: jnp.where(reached, a, b), new, before)  387 us
    ppermute x16, starting transfers between devices, shifted(): return lax.ppermute(block, axis, route)  143 us
    slice x34, local copies, waits for them, and re-layouts, block_scores(): window_kv[0]  116 us
    dot_general x17, matrix products, weighted(): jnp.einsum('kgts,skd->kgtd', probs, value_row_block, preferred_element_ty...  74.6 us
    all_gather x1, blocking collectives, prefix(): everything = jax.tree.map(lambda part: lax.all_gather(part, axis), x)  60.6 us
  transfers between devices with their start and end apart: 18, of which 17 were waited for; matrix products, arithmetic and copies ran while one was open for 1% of the time, Pallas kernels for 0%

commit v1 on v0

--- a/solution.py
+++ b/solution.py
@@ -1,8 +1,12 @@
+import functools
 import math
 
 import jax
 import jax.numpy as jnp
 from jax import lax
+from jax.experimental import pallas as pl
+from jax.experimental.pallas import tpu as pltpu
+from jax.sharding import Mesh
 from jax.sharding import PartitionSpec as P
 
 QUERY_HEADS = 32
@@ -186,20 +190,543 @@
     return (first_pass, second_pass)
 
 
+F32 = jnp.float32
+BF16 = jnp.bfloat16
+LANES = 128
+INNER = (((1,), (1,)), ((), ()))
+VMEM_BYTES = 60 * 1024 * 1024
+
+
+def dot(a, b, dims=(((1,), (0,)), ((), ()))):
+    return lax.dot_general(a, b, dims, preferred_element_type=F32)
+
+
+def lane_select(low, high):
+    lane = lax.broadcasted_iota(jnp.int32, (1, LANES), 1)
+    return jnp.where(lane < SP, low, high)
+
+
+def split_rows(*rows):
+    which = lax.broadcasted_iota(jnp.int32, (16, LANES), 0)
+    tile = jnp.zeros((16, LANES), F32)
+    for i, row in enumerate(rows):
+        for n in range(3):
+            piece = row.astype(BF16).astype(F32)
+            tile = jnp.where(which == 3 * i + n, piece, tile)
+            row = row - piece
+    return jnp.concatenate([tile, jnp.zeros_like(tile)], 1).astype(BF16)
+
+
+def joined_row(proj_ref, i):
+    pieces = proj_ref[0, LANES:, :LANES].astype(F32)
+    return pieces[3 * i : 3 * i + 1] + pieces[3 * i + 1 : 3 * i + 2] + pieces[3 * i + 2 : 3 * i + 3]
+
+
+def column(row):
+    return jnp.broadcast_to(row, (LANES, LANES)).T
+
+
+def pack_kv_kernel(k_ref, v_ref, out_ref):
+    out_ref[0, :LANES, :] = k_ref[...]
+    out_ref[0, LANES:, :] = v_ref[...]
+
+
+def pack_kernel(q_ref, gate_ref, codes_ref, out_ref):
+    heads = q_ref.shape[1] // LANES
+    for h in range(heads):
+        cols = pl.ds(h * LANES, LANES)
+        out_ref[0, pl.ds(h * LANES, LANES), :] = q_ref[:, cols]
+        out_ref[0, pl.ds((heads + h) * LANES, LANES), :] = gate_ref[:, cols]
+    out_ref[0, pl.ds(2 * heads * LANES, 16), :] = codes_ref[0]
+
+
+def attend_kernel(
+    place_ref, q_ref, ko_ref, vo_ref, k1_ref, v1_ref, k2_ref, v2_ref, bc_ref, x_ref, part_ref, s_ref
+):
+    j = pl.program_id(0)
+    plane = place_ref[0]
+    blocks = ko_ref.shape[0]
+    rows = q_ref.shape[1]
+    q = q_ref[0]
+    bias1 = jnp.where(plane >= 1, 0.0, -jnp.inf).astype(F32)
+    bias2 = jnp.where(plane >= 2, 0.0, -jnp.inf).astype(F32)
+    lane = lax.broadcasted_iota(jnp.int32, (1, 2 * LANES), 1)
+    t_pos = lax.broadcasted_iota(jnp.int32, (rows, LANES), 0) % LANES
+    s_pos = lax.broadcasted_iota(jnp.int32, (rows, LANES), 1)
+    causal = s_pos <= t_pos
+    half = blocks // 2
+
+    def mixed(i, own_ref, far_ref):
+        return jnp.where(i < j, own_ref[i], far_ref[i + 1])
+
+    top = None
+    for i in range(2 * half):
+        if i < half:
+            keys = k1_ref[2 * i : 2 * i + 2].reshape(2 * LANES, HEAD_SIZE)
+            s = dot(q, keys, INNER) + bias1
+        else:
+            a = 2 * (i - half)
+            first = mixed(a, ko_ref, k2_ref)
+            bias_a = jnp.where(a < j, 0.0, bias2)
+            if i < 2 * half - 1:
+                keys = jnp.concatenate([first, mixed(a + 1, ko_ref, k2_ref)], 0)
+                bias_b = jnp.where(a + 1 < j, 0.0, bias2)
+                s = dot(q, keys, INNER) + jnp.where(lane < LANES, bias_a, bias_b)
+            else:
+                keys = jnp.concatenate([first, ko_ref[j]], 0)
+                s = dot(q, keys, INNER)
+                edge = dot(q, k2_ref[j], INNER) + bias2
+                s = jnp.concatenate(
+                    [s[:, :LANES] + bias_a, jnp.where(causal, s[:, LANES:], edge)], 1
+                )
+        s_ref[i] = s
+        high = jnp.maximum(s[:, :LANES], s[:, LANES:])
+        top = high if top is None else jnp.maximum(top, high)
+    factor = math.log2(math.e) / math.sqrt(HEAD_SIZE)
+    top = jnp.max(top, axis=1, keepdims=True) * factor
+    weight = jnp.zeros((rows, LANES), F32)
+    for i in range(2 * half):
+        p = jnp.exp2(s_ref[i] * factor - top)
+        s_ref[i] = p
+        weight += p[:, :LANES] + p[:, LANES:]
+    weight = 1.0 / jnp.sum(weight, axis=1, keepdims=True)
+    total = jnp.zeros((rows, HEAD_SIZE), F32)
+    for i in range(2 * half):
+        p = (s_ref[i] * weight).astype(BF16)
+        if i < half:
+            vals = v1_ref[2 * i : 2 * i + 2].reshape(2 * LANES, HEAD_SIZE)
+        else:
+            a = 2 * (i - half)
+            first = mixed(a, vo_ref, v2_ref)
+            if i < 2 * half - 1:
+                vals = jnp.concatenate([first, mixed(a + 1, vo_ref, v2_ref)], 0)
+            else:
+                last = p[:, LANES:]
+                zero = jnp.zeros_like(last)
+                far = jnp.where(causal, zero, last)
+                p = jnp.concatenate([p[:, :LANES], jnp.where(causal, last, zero)], 1)
+                vals = jnp.concatenate([first, vo_ref[j]], 0)
+                total += dot(far, v2_ref[j])
+        total += dot(p, vals)
+    x = total.astype(BF16)
+    x_ref[0] = x
+    heads = rows // LANES
+    part = jnp.zeros((LANES, 2 * NS), F32)
+    squares = jnp.zeros((LANES, LANES), F32)
+    for h in range(heads):
+        piece = x[h * LANES : (h + 1) * LANES]
+        part += dot(piece, bc_ref[pl.ds(h * LANES, LANES), :])
+        wide = piece.astype(F32)
+        squares += wide * wide
+    high = squares.astype(BF16)
+    low = (squares - high.astype(F32)).astype(BF16)
+    row_ones = jnp.ones((16, LANES), BF16)
+    row = dot(row_ones, high, INNER) + dot(row_ones, low, INNER)
+    part_ref[0, :LANES, :] = part
+    part_ref[0, LANES:, :LANES] = row[:8]
+    part_ref[0, LANES:, LANES:] = jnp.zeros_like(row[:8])
+
+
+def project_kernel(channels, part_ref, out_ref):
+    total = part_ref[0]
+    for i in range(1, part_ref.shape[0]):
+        total += part_ref[i]
+    inverse = 1.0 / jnp.sqrt(total[LANES : LANES + 1, :LANES] / channels + EPSILON)
+    scale = column(inverse)
+    out_ref[:LANES, :NS] = (total[:LANES, :NS] * scale).astype(BF16)
+    out_ref[:LANES, NS:] = (total[:LANES, NS:] * scale).astype(BF16)
+    out_ref[LANES:, :] = split_rows(inverse)
+
+
+def code_sums(codes_ref):
+    u = lax.broadcasted_iota(jnp.int32, (LANES, LANES), 0)
+    t = lax.broadcasted_iota(jnp.int32, (LANES, LANES), 1)
+    upper = jnp.where(u <= t, 1.0, 0.0).astype(BF16)
+    sums = dot(codes_ref[0], upper)
+    return sums[:8] * 128.0 + sums[8:]
+
+
+def columns_of(by_row):
+    pad = jnp.zeros((LANES - by_row.shape[0], LANES), F32)
+    return jnp.concatenate([by_row, pad], 0).T
+
+
+def states_kernel(with_gain, place_ref, x_ref, proj_ref, codes_ref, rates_ref, *rest):
+    if with_gain:
+        gain_ref, *rest = rest
+    normed_ref, enter_ref, end_ref, decay_ref, state_ref, count_ref = rest
+    k = pl.program_id(0)
+
+    @pl.when(k == 0)
+    def _():
+        state_ref[...] = jnp.zeros_like(state_ref)
+        count_ref[...] = jnp.zeros_like(count_ref)
+
+    sums = code_sums(codes_ref)
+    last = sums[:, LANES - 1 :]
+    weights = jnp.exp(-rates_ref[0] * (last - sums))
+    block_decay = jnp.exp(-rates_ref[0] * last)
+    count_ref[...] += jnp.broadcast_to(last, count_ref.shape)
+    b_across = proj_ref[0, :LANES, :NS].astype(F32).T
+    inverse = column(joined_row(proj_ref, 0))
+    if with_gain:
+        out_inverse = column(joined_row(proj_ref, 1))
+    for pair in range(x_ref.shape[1] // LANES):
+        rows = pl.ds(pair * LANES, LANES)
+        x = x_ref[0, rows, :].astype(F32)
+        if with_gain:
+            x = x * out_inverse * gain_ref[0, pair : pair + 1, :]
+            x = x.astype(BF16).astype(F32)
+        x = (x * inverse).astype(BF16)
+        normed_ref[0, rows, :] = x
+        h = 2 * pair
+        b = jnp.concatenate(
+            [b_across * weights[h : h + 1], b_across * weights[h + 1 : h + 2]], 0
+        ).astype(BF16)
+        both = dot(b, x)
+        contrib = lane_select(both[:NS], both[NS:])
+        state = state_ref[rows, :]
+        enter_ref[0, rows, :] = state
+        decay = lane_select(block_decay[h : h + 1], block_decay[h + 1 : h + 2])
+        state_ref[rows, :] = decay * state + contrib
+
+    @pl.when(k == pl.num_programs(0) - 1)
+    def _():
+        end_ref[...] = state_ref[...].astype(BF16)
+        whole = jnp.exp(-rates_ref[0] * count_ref[...])
+        for pair in range(x_ref.shape[1] // LANES):
+            decay_ref[pair : pair + 1, :] = lane_select(
+                whole[2 * pair : 2 * pair + 1], whole[2 * pair + 1 : 2 * pair + 2]
+            )
+        decay_ref[4:, :] = jnp.zeros((4, LANES), F32)
+
+
+def local_kernel(place_ref, x_ref, proj_ref, codes_ref, rates_ref, enter_ref, y_ref):
+    ell = -rates_ref[0] * code_sums(codes_ref)
+    ell_col = columns_of(ell)
+    grown = jnp.exp(ell_col)
+    b = proj_ref[0, :LANES, :NS]
+    c = proj_ref[0, :LANES, NS:]
+    gram = dot(c, b, INNER)
+    c = c.astype(F32)
+    t = lax.broadcasted_iota(jnp.int32, (LANES, LANES), 0)
+    s = lax.broadcasted_iota(jnp.int32, (LANES, LANES), 1)
+    lower = t >= s
+    lane = lax.broadcasted_iota(jnp.int32, (LANES, LANES), 1)
+    for pair in range(x_ref.shape[1] // LANES):
+        mixes, highs, lows = [], [], []
+        for h in (2 * pair, 2 * pair + 1):
+            gap = jnp.where(lower, ell_col[:, h : h + 1] - ell[h : h + 1], -jnp.inf)
+            mixes.append((gram * jnp.exp(gap)).astype(BF16))
+            carry = c * grown[:, h : h + 1]
+            high = carry.astype(BF16)
+            highs.append(high)
+            lows.append((carry - high.astype(F32)).astype(BF16))
+        x = x_ref[0, pl.ds(pair * LANES, LANES), :]
+        state = enter_ref[0, pl.ds(pair * NS, NS), :]
+        high = state.astype(BF16)
+        low = (state - high.astype(F32)).astype(BF16)
+        zero = jnp.zeros_like(x)
+
+        def halves(v):
+            return [jnp.where(lane < SP, v, zero), jnp.where(lane < SP, zero, v)]
+
+        right = jnp.concatenate(halves(x) + halves(high) + halves(low) + halves(high), 0)
+        left = jnp.concatenate(mixes + highs + highs + lows, 1)
+        y_ref[0, pl.ds(pair * LANES, LANES), :] = dot(left, right)
+
+
+def gated_kernel(planes, place_ref, y_ref, gate_ref, proj_ref, codes_ref, rates_ref, *rest):
+    states, decays = rest[: planes - 1], rest[planes - 1 : 2 * planes - 3]
+    out_ref, full_ref, count_ref = rest[2 * planes - 3 :]
+    k = pl.program_id(0)
+
+    @pl.when(k == 0)
+    def _():
+        count_ref[...] = jnp.zeros_like(count_ref)
+
+    sums = code_sums(codes_ref)
+    ell = -rates_ref[0] * (sums + count_ref[...])
+    count_ref[...] += jnp.broadcast_to(sums[:, LANES - 1 :], count_ref.shape)
+    grown = columns_of(jnp.exp(ell))
+    c = proj_ref[0, :LANES, NS:].astype(F32)
+    lane = lax.broadcasted_iota(jnp.int32, (LANES, LANES), 1)
+    for pair in range(y_ref.shape[1] // LANES):
+        rows = pl.ds(pair * LANES, LANES)
+        state = states[-1][rows, :].astype(F32)
+        for i in range(planes - 3, -1, -1):
+            state = states[i][rows, :].astype(F32) + decays[i][pair : pair + 1, :] * state
+        state = state.astype(BF16)
+        zero = jnp.zeros_like(state)
+        right = jnp.concatenate(
+            [jnp.where(lane < SP, state, zero), jnp.where(lane < SP, zero, state)], 0
+        )
+        h = 2 * pair
+        left = jnp.concatenate([c * grown[:, h : h + 1], c * grown[:, h + 1 : h + 2]], 1)
+        y = y_ref[0, rows, :] + dot(left.astype(BF16), right)
+        gate = gate_ref[0, rows, :].astype(F32)
+        y = y * (gate / (1.0 + jnp.exp(-gate)))
+        out_ref[0, rows, :] = y.astype(BF16)
+        full_ref[0, rows, :] = y
+
+
+def finish_kernel(channels, with_proj, g_ref, gain_ref, *rest):
+    if with_proj:
+        bc_ref, out_ref, proj_ref = rest
+    else:
+        (out_ref,) = rest
+    parts, wide = g_ref.shape[0], g_ref.shape[1] // LANES
+    squares = jnp.zeros((LANES, LANES), F32)
+    for p in range(parts):
+        for i in range(wide):
+            g = g_ref[p, i * LANES : (i + 1) * LANES, :].astype(F32)
+            squares += g * g
+    inverse = 1.0 / jnp.sqrt(jnp.sum(squares, 1, keepdims=True) / channels + EPSILON)
+    scaled = jnp.zeros((LANES, LANES), F32)
+    proj = jnp.zeros((LANES, 2 * NS), F32)
+    for p in range(parts):
+        for i in range(wide):
+            n = p * wide + i
+            g = g_ref[p, i * LANES : (i + 1) * LANES, :].astype(F32)
+            out = g * inverse * gain_ref[n : n + 1, :]
+            out_ref[:, n * LANES : (n + 1) * LANES] = out
+            if with_proj:
+                x = out.astype(BF16)
+                proj += dot(x, bc_ref[n * LANES : (n + 1) * LANES, :])
+                x = x.astype(F32)
+                scaled += x * x
+    if with_proj:
+        mean = jnp.sum(scaled, 1, keepdims=True) / channels
+        both = 1.0 / jnp.sqrt(mean + EPSILON)
+        proj_ref[:LANES, :] = (proj * both).astype(BF16)
+        wide = jnp.broadcast_to(both, (LANES, LANES)).T
+        proj_ref[LANES:, :] = split_rows(wide[:1], jnp.broadcast_to(inverse, wide.shape).T[:1])
+
+
+def params(**kw):
+    return pltpu.CompilerParams(vmem_limit_bytes=VMEM_BYTES, **kw)
+
+
+def cost(flops, nbytes, exps=0):
+    return pl.CostEstimate(flops=flops, bytes_accessed=nbytes, transcendentals=exps)
+
+
+def whole_block(shape):
+    return pl.BlockSpec(shape, lambda *_: (0,) * len(shape))
+
+
+def head_sharded(
+    planes, queries, rotated_keys, values, decay_rates, decay_codes, gate_input, norm_gain, bc_weight
+):
+    tokens, channels = queries.shape
+    peers = lax.axis_size("peer")
+    wide = channels // peers
+    pairs = wide // LANES
+    place = jnp.stack([lax.axis_index("plane"), lax.axis_index("peer")]).astype(jnp.int32)
+
+    def moved(x, distance):
+        return lax.ppermute(x, "plane", [(i, i + distance) for i in range(planes - distance)])
+
+    kv = pl.pallas_call(
+        pack_kv_kernel,
+        grid=(peers,),
+        in_specs=[pl.BlockSpec((tokens, HEAD_SIZE), lambda p: (0, p))] * 2,
+        out_specs=pl.BlockSpec((1, 2 * tokens, HEAD_SIZE), lambda p: (p, 0, 0)),
+        out_shape=jax.ShapeDtypeStruct((peers, 2 * tokens, HEAD_SIZE), BF16),
+        name="pack_kv",
+    )(rotated_keys, values)
+    kv_own = lax.all_to_all(kv, "peer", 0, 0)
+    kv_one = moved(kv_own, 1)
+    kv_two = moved(kv_one, 1)
+
+    coded = jnp.stack([decay_codes >> 7, decay_codes & 127], 0).astype(BF16)
+    heads = decay_codes.shape[1] // peers
+    coded = jnp.transpose(coded.reshape(2, tokens, peers, heads), (2, 0, 3, 1))
+    coded = coded.reshape(peers, 2 * heads, tokens)
+    q_rows = 2 * wide + 2 * heads
+    packed = pl.pallas_call(
+        pack_kernel,
+        grid=(peers,),
+        in_specs=[
+            pl.BlockSpec((tokens, wide), lambda p: (0, p)),
+            pl.BlockSpec((tokens, wide), lambda p: (0, p)),
+            pl.BlockSpec((1, 2 * heads, tokens), lambda p: (p, 0, 0)),
+        ],
+        out_specs=pl.BlockSpec((1, q_rows, LANES), lambda p: (p, 0, 0)),
+        out_shape=jax.ShapeDtypeStruct((peers, q_rows, LANES), BF16),
+        name="pack_queries",
+    )(queries, gate_input, coded)
+    arrived = lax.all_to_all(packed, "peer", 0, 0)
+
+    def keys_spec(which):
+        return pl.BlockSpec((peers, tokens, HEAD_SIZE), lambda j, s: (0, which, 0))
+
+    def block(rows, which=0, lanes=LANES):
+        return pl.BlockSpec((1, rows, lanes), lambda j, s: (j, which, 0))
+
+    proj_rows = tokens + 16
+    attended, partial = pl.pallas_call(
+        attend_kernel,
+        grid_spec=pltpu.PrefetchScalarGridSpec(
+            num_scalar_prefetch=1,
+            grid=(peers,),
+            in_specs=[block(wide)]
+            + [keys_spec(0), keys_spec(1)] * 3
+            + [pl.BlockSpec((wide, 2 * NS), lambda j, s: (s[1], 0))],
+            out_specs=[block(wide), block(tokens + 8, 0, 2 * NS)],
+            scratch_shapes=[pltpu.VMEM((peers, wide, 2 * tokens), F32)],
+        ),
+        out_shape=[
+            jax.ShapeDtypeStruct((peers, wide, LANES), BF16),
+            jax.ShapeDtypeStruct((peers, tokens + 8, 2 * NS), F32),
+        ],
+        compiler_params=params(),
+        cost_estimate=cost(5 * 10**9, 4 * 10**6, 9 * 10**6),
+        name="attend",
+    )(place, arrived, kv_own, kv_own, kv_one, kv_one, kv_two, kv_two, bc_weight)
+
+    shares = lax.all_to_all(partial, "peer", 0, 0)
+    proj = pl.pallas_call(
+        functools.partial(project_kernel, channels),
+        in_specs=[whole_block((peers, tokens + 8, 2 * NS))],
+        out_specs=whole_block((proj_rows, 2 * NS)),
+        out_shape=jax.ShapeDtypeStruct((proj_rows, 2 * NS), BF16),
+        name="project",
+    )(shares)
+
+    rates = jnp.broadcast_to(decay_rates.reshape(peers, heads, 1), (peers, heads, LANES))
+    gains = norm_gain.reshape(peers, pairs, LANES)
+    rates_spec = pl.BlockSpec((1, heads, LANES), lambda j, s: (s[1], 0, 0))
+    gains_spec = pl.BlockSpec((1, pairs, LANES), lambda j, s: (s[1], 0, 0))
+    codes_spec = block(2 * heads, 2 * wide // (2 * heads))
+    proj_spec = block(proj_rows, 0, 2 * NS)
+
+    def ssd(x, projected, with_gain, decays):
+        common = [block(wide), proj_spec, codes_spec, rates_spec]
+        operands = [x, projected, arrived, rates]
+        if with_gain:
+            common = common + [gains_spec]
+            operands = operands + [gains]
+        normed, entering, end, decay = pl.pallas_call(
+            functools.partial(states_kernel, with_gain),
+            grid_spec=pltpu.PrefetchScalarGridSpec(
+                num_scalar_prefetch=1,
+                grid=(peers,),
+                in_specs=common,
+                out_specs=[
+                    block(wide),
+                    block(wide),
+                    pl.BlockSpec((wide, LANES), lambda j, s: (0, 0)),
+                    pl.BlockSpec((8, LANES), lambda j, s: (0, 0)),
+                ],
+                scratch_shapes=[pltpu.VMEM((wide, LANES), F32), pltpu.VMEM((heads, LANES), F32)],
+            ),
+            out_shape=[
+                jax.ShapeDtypeStruct((peers, wide, LANES), BF16),
+                jax.ShapeDtypeStruct((peers, wide, LANES), F32),
+                jax.ShapeDtypeStruct((wide, LANES), BF16),
+                jax.ShapeDtypeStruct((8, LANES), F32),
+            ],
+            compiler_params=params(),
+            cost_estimate=cost(10**9, 4 * 10**6),
+            name="states",
+        )(place, *operands)
+        earlier = [moved(end, i) for i in range(1, planes)]
+        if decays is None:
+            decays = [moved(decay, i) for i in range(1, planes - 1)]
+        y = pl.pallas_call(
+            local_kernel,
+            grid_spec=pltpu.PrefetchScalarGridSpec(
+                num_scalar_prefetch=1,
+                grid=(peers,),
+                in_specs=[block(wide), proj_spec, codes_spec, rates_spec, block(wide)],
+                out_specs=block(wide),
+            ),
+            out_shape=jax.ShapeDtypeStruct((peers, wide, LANES), F32),
+            compiler_params=params(),
+            cost_estimate=cost(2 * 10**9, 5 * 10**6, 10**6),
+            name="local",
+        )(place, normed, projected, arrived, rates, entering)
+        gated, full = pl.pallas_call(
+            functools.partial(gated_kernel, planes),
+            grid_spec=pltpu.PrefetchScalarGridSpec(
+                num_scalar_prefetch=1,
+                grid=(peers,),
+                in_specs=[block(wide), block(wide, 1), proj_spec, codes_spec, rates_spec]
+                + [pl.BlockSpec((wide, LANES), lambda j, s: (0, 0))] * (planes - 1)
+                + [pl.BlockSpec((8, LANES), lambda j, s: (0, 0))] * (planes - 2),
+                out_specs=[block(wide), block(wide)],
+                scratch_shapes=[pltpu.VMEM((heads, LANES), F32)],
+            ),
+            out_shape=[
+                jax.ShapeDtypeStruct((peers, wide, LANES), BF16),
+                jax.ShapeDtypeStruct((peers, wide, LANES), F32),
+            ],
+            compiler_params=params(),
+            cost_estimate=cost(10**9, 5 * 10**6, 10**6),
+            name="gated",
+        )(place, y, arrived, projected, arrived, rates, *earlier, *decays)
+        return gated, full, decays
+
+    gain_rows = norm_gain.reshape(channels // LANES, LANES)
+    gathered = (peers, wide, LANES)
+
+    projected = lax.all_gather(proj, "peer")
+    gated, full, decays = ssd(attended, projected, False, None)
+    first, proj = pl.pallas_call(
+        functools.partial(finish_kernel, channels, True),
+        in_specs=[
+            whole_block(gathered),
+            whole_block(gain_rows.shape),
+            whole_block((channels, 2 * NS)),
+        ],
+        out_specs=[whole_block((tokens, channels)), whole_block((proj_rows, 2 * NS))],
+        out_shape=[
+            jax.ShapeDtypeStruct((tokens, channels), F32),
+            jax.ShapeDtypeStruct((proj_rows, 2 * NS), BF16),
+        ],
+        compiler_params=params(),
+        name="finish_first",
+    )(lax.all_to_all(gated, "peer", 0, 0), gain_rows, bc_weight)
+    projected = lax.all_gather(proj, "peer")
+    gated, _, _ = ssd(full, projected, True, decays)
+    second = pl.pallas_call(
+        functools.partial(finish_kernel, channels, False),
+        in_specs=[whole_block(gathered), whole_block(gain_rows.shape)],
+        out_specs=whole_block((tokens, channels)),
+        out_shape=jax.ShapeDtypeStruct((tokens, channels), F32),
+        compiler_params=params(),
+        name="finish_second",
+    )(lax.all_to_all(gated, "peer", 0, 0), gain_rows)
+    return first, second
+
+
 def solution(mesh):
-    return jax.shard_map(
-        on_device,
-        mesh=mesh,
-        in_specs=(
-            P("seq", "tp"),
-            P("seq", "tp"),
-            P("seq", "tp"),
-            P("tp"),
-            P("seq", "tp"),
-            P("seq", "tp"),
-            P("tp"),
-            P("tp", None),
-        ),
-        out_specs=(P("seq", "tp"), P("seq", "tp")),
-        check_vma=False,
-    )
+    seq, tp = mesh.shape["seq"], mesh.shape["tp"]
+    peers = KEY_VALUE_HEADS // tp
+    planes = seq // peers
+    grouped = (
+        tp == 1
+        and seq % peers == 0
+        and planes >= 3
+        and 2 * peers * STRETCH == WINDOW_LENGTH
+    )
+
+    def call(*args):
+        tokens = args[0].shape[0] // seq
+        if grouped and tokens == STRETCH:
+            devices = mesh.devices.reshape(planes, peers, tp)
+            inner = Mesh(devices, ("plane", "peer", "tp"))
+            line, body = ("plane", "peer"), functools.partial(head_sharded, planes)
+        else:
+            inner, line, body = mesh, "seq", on_device
+        split = P(line, "tp")
+        return jax.shard_map(
+            body,
+            mesh=inner,
+            in_specs=(split, split, split, P("tp"), split, split, P("tp"), P("tp", None)),
+            out_specs=(split, split),
+            check_vma=False,
+        )(*args)
+
+    return call

time: 2120 us -> 254 us (0.12)
  waiting for transfers between devices: 682 us -> 41.1 us
  local copies, waits for them, and re-layouts: 633 us -> 6.53 us
  other arithmetic: 436 us -> 1.23 us
  matrix products: 140 us -> 0 us
  starting transfers between devices: 143 us -> 39.2 us
  Pallas kernels: 0 us -> 101 us
    all_gather x2 -> x0, waiting for transfers between devices: 661 us -> none  [prefix(): everything = jax.tree.map(lambda part: lax.all_gather(part, axis), x)]
    dynamic_slice x162 -> x0, local copies, waits for them, and re-layouts: 459 us -> none  [the longest x128 446 us: step(): new = combine(before, jax.tree.map(lambda part: part[k], everything))]
    select_n x64 -> x0, other arithmetic: 387 us -> none  [step(): return jax.tree.map(lambda a, b: jnp.where(reached, a, b), new, before)]
    dot_general x44 -> x0, matrix products: 140 us -> none  [the longest x17 74.6 us: weighted(): jnp.einsum('kgts,skd->kgtd', probs, value_row_block, preferred_element_ty...]
    slice x34 -> x0, local copies, waits for them, and re-layouts: 116 us -> none  [block_scores(): window_kv[0]]
    ppermute x16 -> x10, starting transfers between devices: 143 us -> 26.7 us  [moved(): lax.ppermute(x, 'plane', [(i, i + distance) for i in range(planes - dista...]
    pallas_call x0 -> x12, Pallas kernels: none -> 101 us  [the longest x1 25.8 us: head_sharded(): pl.pallas_call(attend_kernel, grid_spec=pltpu.PrefetchScalarGridSpec(num_...]
    all_to_all x0 -> x2, blocking collectives: none -> 39.1 us  [head_sharded(): lax.all_to_all(gated, 'peer', 0, 0)]
  transfers between devices with their start and end apart: 18 -> 13, of which waited for: 17 -> 4; matrix products, arithmetic and copies ran while one was open for 1% -> 1% of each run, Pallas kernels for 0% -> 10%
where the time goes in v1:
time: 254 us; the launch traced here: 251 us
  Pallas kernels  101 us (40%)
  blocking collectives  61 us (24%)
  waiting for transfers between devices  41.1 us (16%)
  starting transfers between devices  39.2 us (15%)
  local copies, waits for them, and re-layouts  6.53 us (3%)
    all_to_all x2, blocking collectives, head_sharded(): lax.all_to_all(gated, 'peer', 0, 0)  39.1 us
    ppermute x10, starting transfers between devices, moved(): lax.ppermute(x, 'plane', [(i, i + distance) for i in range(planes - dista...  26.7 us
    pallas_call x1, Pallas kernels, head_sharded(): pl.pallas_call(attend_kernel, grid_spec=pltpu.PrefetchScalarGridSpec(num_...  25.8 us
    ppermute x10, waiting for transfers between devices, moved(): lax.ppermute(x, 'plane', [(i, i + distance) for i in range(planes - dista...  21.9 us
    all_gather x2, blocking collectives, head_sharded(): projected = lax.all_gather(proj, 'peer')  21.9 us
    pallas_call x2, Pallas kernels, ssd(): pl.pallas_call(local_kernel, grid_spec=pltpu.PrefetchScalarGridSpec(num_s...  20.3 us
    pallas_call x2, Pallas kernels, ssd(): pl.pallas_call(functools.partial(gated_kernel, planes), grid_spec=pltpu.P...  19.5 us
    pallas_call x2, Pallas kernels, ssd(): pl.pallas_call(functools.partial(states_kernel, with_gain), grid_spec=plt...  16.7 us
  transfers between devices with their start and end apart: 13, of which 4 were waited for; matrix products, arithmetic and copies ran while one was open for 1% of the time, Pallas kernels for 10%

profile of v1, /device:TPU:0, one launch (start us, length us, event | category | flops | bytes accessed | tf_op | source)
XLA Modules:
  0.0 251.4 jit_solution(13349060593774921792)
XLA Ops:
  0.6 4.5 %pack_kv.1 = bf16[8,256,128]{2,1,0:T(8,128)(2,1)} custom-call(bf16[128,1024]{1,0:T(8,128)(2,1)} %k_ref.1, bf16[128,1024]{1,0:T(8,128)(2,1)} %v_ref.1), custom_call_target="tpu_custom_call" | custom-call | tf_op jit(solution)/shard_map/pack_kv/pallas_call | solution.py:530
  5.1 5.2 %all-to-all-start.1 = ((bf16[8,256,128]{2,1,0:T(8,128)(2,1)}), bf16[8,256,128]{2,1,0:T(8,128)(2,1)S(1)}, u32[]{:S(2)}, u32[]{:S(2)}) async-start(bf16[8,256,128]{2,1,0:T(8,128)(2,1)} %pack_kv.1), calls=%async_computation.1 | async-start | bytes 1048576 | tf_op jit(solution)/shard_map/all_to_all | solution.py:538
  11.0 5.9 %pack_queries.1 = bf16[8,1040,128]{2,1,0:T(8,128)(2,1)} custom-call(bf16[128,4096]{1,0:T(8,128)(2,1)} %q_ref.1, bf16[128,4096]{1,0:T(8,128)(2,1)} %gate_ref.1, bf16[8,16,128]{2,1,0:T(8,128)(2,1)} %maximum_bitcast_fusion.codes_ref), custom_call_target="tpu_custom_call" | custom-call | tf_op jit(solution)/shard_map/pack_queries/pallas_call | solution.py:547
  16.8 3.2 %all-to-all-done.1.ko_ref.vo_ref = bf16[8,256,128]{2,1,0:T(8,128)(2,1)S(1)} async-done(((bf16[8,256,128]{2,1,0:T(8,128)(2,1)}), bf16[8,256,128]{2,1,0:T(8,128)(2,1)S(1)}, u32[]{:S(2)}, u32[]{:S(2)}) %all-to-all-start.1) | async-done | bytes 524320 | tf_op jit(solution)/shard_map/all_to_all | solution.py:538
  20.0 3.6 %all-to-all-start = ((bf16[8,1040,128]{2,1,0:T(8,128)(2,1)}), bf16[8,1040,128]{2,1,0:T(8,128)(2,1)S(1)}, u32[]{:S(2)}, u32[]{:S(2)}) async-start(bf16[8,1040,128]{2,1,0:T(8,128)(2,1)} %pack_queries.1), calls=%async_computation | async-start | bytes 4259840 | tf_op jit(solution)/shard_map/all_to_all | solution.py:559
  23.7 3.5 %collective-permute-start = (bf16[8,256,128]{2,1,0:T(8,128)(2,1)S(1)}, bf16[8,256,128]{2,1,0:T(8,128)(2,1)S(1)}, u32[]{:S(2)}, u32[]{:S(2)}) collective-permute-start(bf16[8,256,128]{2,1,0:T(8,128)(2,1)S(1)} %all-to-all-done.1.ko_ref.vo_ref), channel_id=1, source_target_pairs={{0,8},{8,16},{16,24},{1,9},{9,17},{17,25},{2,10},{10,18},{18,26},{... | collective-permute-start | bytes 1572872 | tf_op jit(solution)/shard_map/ppermute | solution.py:528
  27.2 11.7 %collective-permute-done.k1_ref.v1_ref = bf16[8,256,128]{2,1,0:T(8,128)(2,1)S(1)} collective-permute-done((bf16[8,256,128]{2,1,0:T(8,128)(2,1)S(1)}, bf16[8,256,128]{2,1,0:T(8,128)(2,1)S(1)}, u32[]{:S(2)}, u32[]{:S(2)}) %collective-permute-start) | collective-permute-done | bytes 524320 | tf_op jit(solution)/shard_map/ppermute | solution.py:528
  38.9 4.4 %collective-permute-start.1 = (bf16[8,256,128]{2,1,0:T(8,128)(2,1)S(1)}, bf16[8,256,128]{2,1,0:T(8,128)(2,1)S(1)}, u32[]{:S(2)}, u32[]{:S(2)}) collective-permute-start(bf16[8,256,128]{2,1,0:T(8,128)(2,1)S(1)} %collective-permute-done.k1_ref.v1_ref), channel_id=1, source_target_pairs={{0,8},{8,16},{16,24},{1,9},{9,17},{17,25},{2,10},{10,18},{18,26},{... | collective-permute-start | bytes 1572872 | tf_op jit(solution)/shard_map/ppermute | solution.py:528
  43.9 10.2 %collective-permute-done.1.k2_ref.v2_ref = bf16[8,256,128]{2,1,0:T(8,128)(2,1)S(1)} collective-permute-done((bf16[8,256,128]{2,1,0:T(8,128)(2,1)S(1)}, bf16[8,256,128]{2,1,0:T(8,128)(2,1)S(1)}, u32[]{:S(2)}, u32[]{:S(2)}) %collective-permute-start.1) | collective-permute-done | bytes 524320 | tf_op jit(solution)/shard_map/ppermute | solution.py:528
  54.9 1.4 copy-done
  56.3 25.8 %attend.1 = (bf16[8,512,128]{2,1,0:T(8,128)(2,1)}, f32[8,136,256]{2,1,0:T(8,128)}) custom-call(s32[2]{0:T(128)} %pad_add_fusion.place_ref, bf16[8,1040,128]{2,1,0:T(8,128)(2,1)} %copy-done, bf16[8,256,128]{2,1,0:T(8,128)(2,1)} %copy-done.2, bf16[8,256,128]{2,1,0:T(8,128)(2,1)} %copy-done.2, bf16[8,256,128]{2,1,0:T(8,128)(2,1)} %copy-done.13, ...), custom_call_target="tpu_custom_call" | custom-call | flops 5000000000 | bytes 4000000 | tf_op jit(solution)/shard_map/attend/pallas_call | solution.py:568
  82.0 3.7 %all-to-all-start.2 = ((f32[8,136,256]{2,1,0:T(8,128)}), f32[8,136,256]{2,1,0:T(8,128)S(1)}, u32[]{:S(2)}, u32[]{:S(2)}) async-start(f32[8,136,256]{2,1,0:T(8,128)} %get-tuple-element.17), calls=%async_computation.2 | async-start | bytes 2228224 | tf_op jit(solution)/shard_map/all_to_all | solution.py:588
  85.8 16.0 %all-to-all-done.2.part_ref = f32[8,136,256]{2,1,0:T(8,128)S(1)} async-done(((f32[8,136,256]{2,1,0:T(8,128)}), f32[8,136,256]{2,1,0:T(8,128)S(1)}, u32[]{:S(2)}, u32[]{:S(2)}) %all-to-all-start.2) | async-done | bytes 1114144 | tf_op jit(solution)/shard_map/all_to_all | solution.py:588
  102.8 2.0 project.1
  104.8 10.9 %all-gather = bf16[1152,256]{1,0:T(8,128)(2,1)} all-gather(bf16[144,256]{1,0:T(8,128)(2,1)} %project.1), channel_id=2, replica_groups=mesh['plane'=4,'peer'=8,'tp'=1] {'peer'}, dimensions={0}, use_global_device_ids=true | all-gather | bytes 663552 | tf_op jit(solution)/shard_map/all_gather | solution.py:674
  116.4 8.2 %states.2 = (bf16[8,512,128]{2,1,0:T(8,128)(2,1)}, f32[8,512,128]{2,1,0:T(8,128)}, bf16[512,128]{1,0:T(8,128)(2,1)}, f32[8,128]{1,0:T(8,128)}) custom-call(s32[2]{0:T(128)} %pad_add_fusion.place_ref, bf16[8,512,128]{2,1,0:T(8,128)(2,1)} %get-tuple-element.16.x_ref, bf16[8,144,256]{2,1,0:T(8,128)(2,1)} %bitcast.21, bf16[8,1040,128]{2,1,0:T(8,128)(2,1)} %copy-done, ...), custom_call_target="tpu_custom_call" | custom-call | flops 1000000000 | bytes 4000000 | tf_op jit(solution)/shard_map/states/pallas_call | solution.py:610
  124.7 5.4 %collective-permute-start.6 = (f32[8,128]{1,0:T(8,128)}, f32[8,128]{1,0:T(8,128)S(1)}, u32[]{:S(2)}, u32[]{:S(2)}) collective-permute-start(f32[8,128]{1,0:T(8,128)} %get-tuple-element.21), channel_id=1, source_target_pairs={{0,16},{8,24},{1,17},{9,25},{2,18},{10,26},{3,19},{11,27},{4,20},{... | collective-permute-start | bytes 12296 | tf_op jit(solution)/shard_map/ppermute | solution.py:528
  130.1 3.5 %collective-permute-start.5 = (f32[8,128]{1,0:T(8,128)}, f32[8,128]{1,0:T(8,128)S(1)}, u32[]{:S(2)}, u32[]{:S(2)}) collective-permute-start(f32[8,128]{1,0:T(8,128)} %get-tuple-element.21), channel_id=1, source_target_pairs={{0,8},{8,16},{16,24},{1,9},{9,17},{17,25},{2,10},{10,18},{18,26},{... | collective-permute-start | bytes 12296 | tf_op jit(solution)/shard_map/ppermute | solution.py:528
  136.2 1.3 collective-permute-start.2
  137.5 10.2 %local.2.y_ref = f32[8,512,128]{2,1,0:T(8,128)} custom-call(s32[2]{0:T(128)} %pad_add_fusion.place_ref, bf16[8,512,128]{2,1,0:T(8,128)(2,1)} %get-tuple-element.18.x_ref, bf16[8,144,256]{2,1,0:T(8,128)(2,1)} %bitcast.22, bf16[8,1040,128]{2,1,0:T(8,128)(2,1)} %copy-done, f32[8,8,128]{2,1,0:T(8,128)} %broadcast_in_dim.8.rates_ref, ...), custom_call_target="tpu_custom_call" | custom-call | flops 2000000000 | bytes 5000000 | tf_op jit(solution)/shard_map/local/pallas_call | solution.py:637
  149.1 9.7 %gated.2 = (bf16[8,512,128]{2,1,0:T(8,128)(2,1)}, f32[8,512,128]{2,1,0:T(8,128)}) custom-call(s32[2]{0:T(128)} %pad_add_fusion.place_ref, f32[8,512,128]{2,1,0:T(8,128)} %local.2.y_ref, bf16[8,1040,128]{2,1,0:T(8,128)(2,1)} %copy-done, bf16[8,144,256]{2,1,0:T(8,128)(2,1)} %bitcast.23, bf16[8,1040,128]{2,1,0:T(8,128)(2,1)} %copy-done, ...), custom_call_target="tpu_custom_call" | custom-call | flops 1000000000 | bytes 5000000 | tf_op jit(solution)/shard_map/gated/pallas_call | solution.py:650
  158.8 19.6 %all_to_all.25.g_ref = bf16[8,512,128]{2,1,0:T(8,128)(2,1)} all-to-all(bf16[8,512,128]{2,1,0:T(8,128)(2,1)} %get-tuple-element.22), channel_id=1, replica_groups=mesh['plane'=4,'peer'=8,'tp'=1] {'peer'}, dimensions={0} | all-to-all | bytes 2097152 | tf_op jit(solution)/shard_map/all_to_all | solution.py:690
  178.4 3.8 %finish_first.1 = (f32[128,4096]{1,0:T(8,128)}, bf16[144,256]{1,0:T(8,128)(2,1)}) custom-call(bf16[8,512,128]{2,1,0:T(8,128)(2,1)} %all_to_all.25.g_ref, f32[32,128]{1,0:T(8,128)} %bitcast.24, bf16[4096,256]{1,0:T(8,128)(2,1)} %rest_0_.1), custom_call_target="tpu_custom_call" | custom-call | tf_op jit(solution)/shard_map/finish_first/pallas_call | solution.py:676
  182.2 10.9 %all-gather.1 = bf16[1152,256]{1,0:T(8,128)(2,1)} all-gather(bf16[144,256]{1,0:T(8,128)(2,1)} %get-tuple-element.25), channel_id=3, replica_groups=mesh['plane'=4,'peer'=8,'tp'=1] {'peer'}, dimensions={0}, use_global_device_ids=true | all-gather | bytes 663552 | tf_op jit(solution)/shard_map/all_gather | solution.py:691
  193.1 8.5 %states.3 = (bf16[8,512,128]{2,1,0:T(8,128)(2,1)}, f32[8,512,128]{2,1,0:T(8,128)}, bf16[512,128]{1,0:T(8,128)(2,1)}, f32[8,128]{1,0:T(8,128)}) custom-call(s32[2]{0:T(128)} %pad_add_fusion.place_ref, f32[8,512,128]{2,1,0:T(8,128)} %get-tuple-element.24.x_ref, bf16[8,144,256]{2,1,0:T(8,128)(2,1)} %bitcast.18, bf16[8,1040,128]{2,1,0:T(8,128)(2,1)} %copy-done, ...), custom_call_target="tpu_custom_call" | custom-call | flops 1000000000 | bytes 4000000 | tf_op jit(solution)/shard_map/states/pallas_call | solution.py:610
  201.6 2.2 collective-permute-start.9
  203.9 1.4 collective-permute-start.8
  205.2 2.4 collective-permute-start.7
  207.6 10.2 %local.3.y_ref = f32[8,512,128]{2,1,0:T(8,128)} custom-call(s32[2]{0:T(128)} %pad_add_fusion.place_ref, bf16[8,512,128]{2,1,0:T(8,128)(2,1)} %get-tuple-element.26.x_ref, bf16[8,144,256]{2,1,0:T(8,128)(2,1)} %bitcast.19, bf16[8,1040,128]{2,1,0:T(8,128)(2,1)} %copy-done, f32[8,8,128]{2,1,0:T(8,128)} %broadcast_in_dim.8.rates_ref, ...), custom_call_target="tpu_custom_call" | custom-call | flops 2000000000 | bytes 5000000 | tf_op jit(solution)/shard_map/local/pallas_call | solution.py:637
  219.2 9.8 %gated.3 = (bf16[8,512,128]{2,1,0:T(8,128)(2,1)}, f32[8,512,128]{2,1,0:T(8,128)}) custom-call(s32[2]{0:T(128)} %pad_add_fusion.place_ref, f32[8,512,128]{2,1,0:T(8,128)} %local.3.y_ref, bf16[8,1040,128]{2,1,0:T(8,128)(2,1)} %copy-done, bf16[8,144,256]{2,1,0:T(8,128)(2,1)} %bitcast.20, bf16[8,1040,128]{2,1,0:T(8,128)(2,1)} %copy-done, ...), custom_call_target="tpu_custom_call" | custom-call | flops 1000000000 | bytes 5000000 | tf_op jit(solution)/shard_map/gated/pallas_call | solution.py:650
  228.9 19.6 %all_to_all.26.g_ref = bf16[8,512,128]{2,1,0:T(8,128)(2,1)} all-to-all(bf16[8,512,128]{2,1,0:T(8,128)(2,1)} %get-tuple-element.29), channel_id=1, replica_groups=mesh['plane'=4,'peer'=8,'tp'=1] {'peer'}, dimensions={0} | all-to-all | bytes 2097152 | tf_op jit(solution)/shard_map/all_to_all | solution.py:700
  248.5 3.0 %finish_second.1 = f32[128,4096]{1,0:T(8,128)} custom-call(bf16[8,512,128]{2,1,0:T(8,128)(2,1)} %all_to_all.26.g_ref, f32[32,128]{1,0:T(8,128)} %bitcast.26), custom_call_target="tpu_custom_call" | custom-call | tf_op jit(solution)/shard_map/finish_second/pallas_call | solution.py:693
  (45 shorter events, 9.0 us)
Async XLA Ops:
  0.6 9.7 %copy-start.9 = (s32[128,64]{0,1:T(8,128)S(1)}, s32[128,64]{0,1:T(8,128)}, u32[]{:S(2)}) copy-start(s32[128,64]{0,1:T(8,128)} %param.12) | copy-start | bytes 98308
  5.1 14.9 %all-to-all-start.1 = ((bf16[8,256,128]{2,1,0:T(8,128)(2,1)}), bf16[8,256,128]{2,1,0:T(8,128)(2,1)S(1)}, u32[]{:S(2)}, u32[]{:S(2)}) async-start(bf16[8,256,128]{2,1,0:T(8,128)(2,1)} %pack_kv.1), calls=%async_computation.1 | async-start | bytes 1048576 | tf_op jit(solution)/shard_map/all_to_all | solution.py:538
  20.0 3.6 %copy-start.2 = (bf16[8,256,128]{2,1,0:T(8,128)(2,1)}, bf16[8,256,128]{2,1,0:T(8,128)(2,1)S(1)}, u32[]{:S(2)}) copy-start(bf16[8,256,128]{2,1,0:T(8,128)(2,1)S(1)} %all-to-all-done.1.ko_ref.vo_ref) | copy-start | bytes 1572868
  20.0 34.1 %all-to-all-start = ((bf16[8,1040,128]{2,1,0:T(8,128)(2,1)}), bf16[8,1040,128]{2,1,0:T(8,128)(2,1)S(1)}, u32[]{:S(2)}, u32[]{:S(2)}) async-start(bf16[8,1040,128]{2,1,0:T(8,128)(2,1)} %pack_queries.1), calls=%async_computation | async-start | bytes 4259840 | tf_op jit(solution)/shard_map/all_to_all | solution.py:559
  23.7 15.2 %collective-permute-start = (bf16[8,256,128]{2,1,0:T(8,128)(2,1)S(1)}, bf16[8,256,128]{2,1,0:T(8,128)(2,1)S(1)}, u32[]{:S(2)}, u32[]{:S(2)}) collective-permute-start(bf16[8,256,128]{2,1,0:T(8,128)(2,1)S(1)} %all-to-all-done.1.ko_ref.vo_ref), channel_id=1, source_target_pairs={{0,8},{8,16},{16,24},{1,9},{9,17},{17,25},{2,10},{10,18},{18,26},{... | collective-permute-start | bytes 1572872 | tf_op jit(solution)/shard_map/ppermute | solution.py:528
  38.9 15.2 %copy-start.13 = (bf16[8,256,128]{2,1,0:T(8,128)(2,1)}, bf16[8,256,128]{2,1,0:T(8,128)(2,1)S(1)}, u32[]{:S(2)}) copy-start(bf16[8,256,128]{2,1,0:T(8,128)(2,1)S(1)} %collective-permute-done.k1_ref.v1_ref) | copy-start | bytes 1572868
  38.9 15.2 %collective-permute-start.1 = (bf16[8,256,128]{2,1,0:T(8,128)(2,1)S(1)}, bf16[8,256,128]{2,1,0:T(8,128)(2,1)S(1)}, u32[]{:S(2)}, u32[]{:S(2)}) collective-permute-start(bf16[8,256,128]{2,1,0:T(8,128)(2,1)S(1)} %collective-permute-done.k1_ref.v1_ref), channel_id=1, source_target_pairs={{0,8},{8,16},{16,24},{1,9},{9,17},{17,25},{2,10},{10,18},{18,26},{... | collective-permute-start | bytes 1572872 | tf_op jit(solution)/shard_map/ppermute | solution.py:528
  54.1 0.8 copy-start.14
  54.9 1.4 copy-start
  82.0 3.7 %copy-start.12 = (f32[64]{0:T(128)S(1)}, f32[64]{0:T(128)}, u32[]{:S(2)}) copy-start(f32[64]{0:T(128)} %param.11) | copy-start | bytes 772
  82.0 19.8 %all-to-all-start.2 = ((f32[8,136,256]{2,1,0:T(8,128)}), f32[8,136,256]{2,1,0:T(8,128)S(1)}, u32[]{:S(2)}, u32[]{:S(2)}) async-start(f32[8,136,256]{2,1,0:T(8,128)} %get-tuple-element.17), calls=%async_computation.2 | async-start | bytes 2228224 | tf_op jit(solution)/shard_map/all_to_all | solution.py:588
  101.8 1.0 copy-start.1
  124.7 23.0 %collective-permute-start.6 = (f32[8,128]{1,0:T(8,128)}, f32[8,128]{1,0:T(8,128)S(1)}, u32[]{:S(2)}, u32[]{:S(2)}) collective-permute-start(f32[8,128]{1,0:T(8,128)} %get-tuple-element.21), channel_id=1, source_target_pairs={{0,16},{8,24},{1,17},{9,25},{2,18},{10,26},{3,19},{11,27},{4,20},{... | collective-permute-start | bytes 12296 | tf_op jit(solution)/shard_map/ppermute | solution.py:528
  130.1 17.6 %collective-permute-start.5 = (f32[8,128]{1,0:T(8,128)}, f32[8,128]{1,0:T(8,128)S(1)}, u32[]{:S(2)}, u32[]{:S(2)}) collective-permute-start(f32[8,128]{1,0:T(8,128)} %get-tuple-element.21), channel_id=1, source_target_pairs={{0,8},{8,16},{16,24},{1,9},{9,17},{17,25},{2,10},{10,18},{18,26},{... | collective-permute-start | bytes 12296 | tf_op jit(solution)/shard_map/ppermute | solution.py:528
  133.6 14.1 %collective-permute-start.4 = (bf16[512,128]{1,0:T(8,128)(2,1)}, bf16[512,128]{1,0:T(8,128)(2,1)S(1)}, u32[]{:S(2)}, u32[]{:S(2)}) collective-permute-start(bf16[512,128]{1,0:T(8,128)(2,1)} %get-tuple-element.20), channel_id=1, source_target_pairs={{0,24},{1,25},{2,26},{3,27},{4,28},{5,29},{6,30},{7,31}} | collective-permute-start | bytes 393224 | tf_op jit(solution)/shard_map/ppermute | solution.py:528
  134.9 12.8 %collective-permute-start.3 = (bf16[512,128]{1,0:T(8,128)(2,1)}, bf16[512,128]{1,0:T(8,128)(2,1)S(1)}, u32[]{:S(2)}, u32[]{:S(2)}) collective-permute-start(bf16[512,128]{1,0:T(8,128)(2,1)} %get-tuple-element.20), channel_id=1, source_target_pairs={{0,16},{8,24},{1,17},{9,25},{2,18},{10,26},{3,19},{11,27},{4,20},{... | collective-permute-start | bytes 393224 | tf_op jit(solution)/shard_map/ppermute | solution.py:528
  136.2 11.6 %collective-permute-start.2 = (bf16[512,128]{1,0:T(8,128)(2,1)}, bf16[512,128]{1,0:T(8,128)(2,1)S(1)}, u32[]{:S(2)}, u32[]{:S(2)}) collective-permute-start(bf16[512,128]{1,0:T(8,128)(2,1)} %get-tuple-element.20), channel_id=1, source_target_pairs={{0,8},{8,16},{16,24},{1,9},{9,17},{17,25},{2,10},{10,18},{18,26},{... | collective-permute-start | bytes 393224 | tf_op jit(solution)/shard_map/ppermute | solution.py:528
  147.7 0.6 copy-start.10
  147.7 0.6 copy-start.11
  147.7 0.7 copy-start.3
  147.7 0.7 copy-start.5
  148.4 0.7 copy-start.7
  201.6 16.2 %collective-permute-start.9 = (bf16[512,128]{1,0:T(8,128)(2,1)}, bf16[512,128]{1,0:T(8,128)(2,1)S(1)}, u32[]{:S(2)}, u32[]{:S(2)}) collective-permute-start(bf16[512,128]{1,0:T(8,128)(2,1)} %get-tuple-element.28), channel_id=1, source_target_pairs={{0,24},{1,25},{2,26},{3,27},{4,28},{5,29},{6,30},{7,31}} | collective-permute-start | bytes 393224 | tf_op jit(solution)/shard_map/ppermute | solution.py:528
  203.9 14.0 %collective-permute-start.8 = (bf16[512,128]{1,0:T(8,128)(2,1)}, bf16[512,128]{1,0:T(8,128)(2,1)S(1)}, u32[]{:S(2)}, u32[]{:S(2)}) collective-permute-start(bf16[512,128]{1,0:T(8,128)(2,1)} %get-tuple-element.28), channel_id=1, source_target_pairs={{0,16},{8,24},{1,17},{9,25},{2,18},{10,26},{3,19},{11,27},{4,20},{... | collective-permute-start | bytes 393224 | tf_op jit(solution)/shard_map/ppermute | solution.py:528
  205.2 12.6 %collective-permute-start.7 = (bf16[512,128]{1,0:T(8,128)(2,1)}, bf16[512,128]{1,0:T(8,128)(2,1)S(1)}, u32[]{:S(2)}, u32[]{:S(2)}) collective-permute-start(bf16[512,128]{1,0:T(8,128)(2,1)} %get-tuple-element.28), channel_id=1, source_target_pairs={{0,8},{8,16},{16,24},{1,9},{9,17},{17,25},{2,10},{10,18},{18,26},{... | collective-permute-start | bytes 393224 | tf_op jit(solution)/shard_map/ppermute | solution.py:528
  217.8 0.7 copy-start.4
  217.8 0.7 copy-start.6
  218.5 0.6 copy-start.8

commit v2 on v1

--- a/solution.py
+++ b/solution.py
@@ -194,7 +194,7 @@
 BF16 = jnp.bfloat16
 LANES = 128
 INNER = (((1,), (1,)), ((), ()))
-VMEM_BYTES = 60 * 1024 * 1024
+VMEM_BYTES = 24 * 1024 * 1024
 
 
 def dot(a, b, dims=(((1,), (0,)), ((), ()))):
@@ -217,8 +217,7 @@
     return jnp.concatenate([tile, jnp.zeros_like(tile)], 1).astype(BF16)
 
 
-def joined_row(proj_ref, i):
-    pieces = proj_ref[0, LANES:, :LANES].astype(F32)
+def joined_row(pieces, i):
     return pieces[3 * i : 3 * i + 1] + pieces[3 * i + 1 : 3 * i + 2] + pieces[3 * i + 2 : 3 * i + 3]
 
 
@@ -227,17 +226,22 @@
 
 
 def pack_kv_kernel(k_ref, v_ref, out_ref):
-    out_ref[0, :LANES, :] = k_ref[...]
-    out_ref[0, LANES:, :] = v_ref[...]
-
-
-def pack_kernel(q_ref, gate_ref, codes_ref, out_ref):
-    heads = q_ref.shape[1] // LANES
-    for h in range(heads):
-        cols = pl.ds(h * LANES, LANES)
-        out_ref[0, pl.ds(h * LANES, LANES), :] = q_ref[:, cols]
-        out_ref[0, pl.ds((heads + h) * LANES, LANES), :] = gate_ref[:, cols]
-    out_ref[0, pl.ds(2 * heads * LANES, 16), :] = codes_ref[0]
+    for p in range(out_ref.shape[0]):
+        cols = pl.ds(p * LANES, LANES)
+        out_ref[p, :LANES, :] = k_ref[:, cols]
+        out_ref[p, LANES:, :] = v_ref[:, cols]
+
+
+def pack_heads_kernel(x_ref, *rest):
+    out_ref = rest[-1]
+    peers = out_ref.shape[0]
+    heads = x_ref.shape[1] // LANES // peers
+    for p in range(peers):
+        for h in range(heads):
+            cols = pl.ds((p * heads + h) * LANES, LANES)
+            out_ref[p, pl.ds(h * LANES, LANES), :] = x_ref[:, cols]
+        if len(rest) == 2:
+            out_ref[p, pl.ds(heads * LANES, 16), :] = rest[0][p]
 
 
 def attend_kernel(
@@ -338,11 +342,11 @@
     out_ref[LANES:, :] = split_rows(inverse)
 
 
-def code_sums(codes_ref):
+def code_sums(codes):
     u = lax.broadcasted_iota(jnp.int32, (LANES, LANES), 0)
     t = lax.broadcasted_iota(jnp.int32, (LANES, LANES), 1)
     upper = jnp.where(u <= t, 1.0, 0.0).astype(BF16)
-    sums = dot(codes_ref[0], upper)
+    sums = dot(codes, upper)
     return sums[:8] * 128.0 + sums[8:]
 
 
@@ -351,123 +355,134 @@
     return jnp.concatenate([by_row, pad], 0).T
 
 
-def states_kernel(with_gain, place_ref, x_ref, proj_ref, codes_ref, rates_ref, *rest):
+def states_kernel(with_gain, x_ref, proj_ref, side_ref, rates_ref, *rest):
     if with_gain:
         gain_ref, *rest = rest
-    normed_ref, enter_ref, end_ref, decay_ref, state_ref, count_ref = rest
-    k = pl.program_id(0)
-
-    @pl.when(k == 0)
-    def _():
-        state_ref[...] = jnp.zeros_like(state_ref)
-        count_ref[...] = jnp.zeros_like(count_ref)
-
-    sums = code_sums(codes_ref)
-    last = sums[:, LANES - 1 :]
-    weights = jnp.exp(-rates_ref[0] * (last - sums))
-    block_decay = jnp.exp(-rates_ref[0] * last)
-    count_ref[...] += jnp.broadcast_to(last, count_ref.shape)
-    b_across = proj_ref[0, :LANES, :NS].astype(F32).T
-    inverse = column(joined_row(proj_ref, 0))
-    if with_gain:
-        out_inverse = column(joined_row(proj_ref, 1))
-    for pair in range(x_ref.shape[1] // LANES):
-        rows = pl.ds(pair * LANES, LANES)
-        x = x_ref[0, rows, :].astype(F32)
+    normed_ref, enter_ref, end_ref, state_ref, count_ref = rest
+    peers, wide = x_ref.shape[:2]
+    pairs = wide // LANES
+    rates = rates_ref[...]
+    state_ref[...] = jnp.zeros_like(state_ref)
+    count_ref[...] = jnp.zeros_like(count_ref)
+
+    @pl.loop(0, peers)
+    def _(k):
+        sums = code_sums(side_ref[k, pl.ds(wide, 16), :])
+        last = sums[:, LANES - 1 :]
+        weights = jnp.exp(-rates * (last - sums))
+        block_decay = jnp.exp(-rates * last)
+        count_ref[...] += jnp.broadcast_to(last, count_ref.shape)
+        b_across = proj_ref[k, :LANES, :NS].astype(F32).T
+        pieces = proj_ref[k, LANES:, :LANES].astype(F32)
+        inverse = column(joined_row(pieces, 0))
         if with_gain:
-            x = x * out_inverse * gain_ref[0, pair : pair + 1, :]
-            x = x.astype(BF16).astype(F32)
-        x = (x * inverse).astype(BF16)
-        normed_ref[0, rows, :] = x
-        h = 2 * pair
-        b = jnp.concatenate(
-            [b_across * weights[h : h + 1], b_across * weights[h + 1 : h + 2]], 0
-        ).astype(BF16)
-        both = dot(b, x)
-        contrib = lane_select(both[:NS], both[NS:])
-        state = state_ref[rows, :]
-        enter_ref[0, rows, :] = state
-        decay = lane_select(block_decay[h : h + 1], block_decay[h + 1 : h + 2])
-        state_ref[rows, :] = decay * state + contrib
-
-    @pl.when(k == pl.num_programs(0) - 1)
-    def _():
-        end_ref[...] = state_ref[...].astype(BF16)
-        whole = jnp.exp(-rates_ref[0] * count_ref[...])
-        for pair in range(x_ref.shape[1] // LANES):
-            decay_ref[pair : pair + 1, :] = lane_select(
-                whole[2 * pair : 2 * pair + 1], whole[2 * pair + 1 : 2 * pair + 2]
-            )
-        decay_ref[4:, :] = jnp.zeros((4, LANES), F32)
-
-
-def local_kernel(place_ref, x_ref, proj_ref, codes_ref, rates_ref, enter_ref, y_ref):
-    ell = -rates_ref[0] * code_sums(codes_ref)
-    ell_col = columns_of(ell)
-    grown = jnp.exp(ell_col)
-    b = proj_ref[0, :LANES, :NS]
-    c = proj_ref[0, :LANES, NS:]
-    gram = dot(c, b, INNER)
-    c = c.astype(F32)
+            out_inverse = column(joined_row(pieces, 1))
+        for pair in range(pairs):
+            rows = pl.ds(pair * LANES, LANES)
+            x = x_ref[k, rows, :].astype(F32)
+            if with_gain:
+                x = x * out_inverse * gain_ref[pair : pair + 1, :]
+                x = x.astype(BF16).astype(F32)
+            x = (x * inverse).astype(BF16)
+            normed_ref[k, rows, :] = x
+            h = 2 * pair
+            b = jnp.concatenate(
+                [b_across * weights[h : h + 1], b_across * weights[h + 1 : h + 2]], 0
+            ).astype(BF16)
+            both = dot(b, x)
+            contrib = lane_select(both[:NS], both[NS:])
+            state = state_ref[rows, :]
+            enter_ref[k, rows, :] = state
+            decay = lane_select(block_decay[h : h + 1], block_decay[h + 1 : h + 2])
+            state_ref[rows, :] = decay * state + contrib
+
+    end_ref[:wide, :] = state_ref[...].astype(BF16)
+    whole = jnp.exp(-rates * count_ref[...])
+    which = lax.broadcasted_iota(jnp.int32, (16, LANES), 0)
+    tile = jnp.zeros((16, LANES), F32)
+    for pair in range(pairs):
+        row = lane_select(whole[2 * pair : 2 * pair + 1], whole[2 * pair + 1 : 2 * pair + 2])
+        for n in range(3):
+            piece = row.astype(BF16).astype(F32)
+            tile = jnp.where(which == 3 * pair + n, piece, tile)
+            row = row - piece
+    end_ref[wide:, :] = tile.astype(BF16)
+
+
+def carried(c_twice, grown, states):
+    parts = []
+    for state in states:
+        high = state.astype(BF16)
+        low = (state - high.astype(F32)).astype(BF16)
+        parts.append(jnp.concatenate([high, low], 0))
+    out = dot(c_twice, jnp.concatenate(parts, 1))
+    scaled = []
+    for pair in range(len(states)):
+        scale = lane_select(grown[:, 2 * pair : 2 * pair + 1], grown[:, 2 * pair + 1 : 2 * pair + 2])
+        scaled.append(scale * out[:, pair * LANES : (pair + 1) * LANES])
+    return scaled
+
+
+def local_kernel(x_ref, proj_ref, side_ref, rates_ref, enter_ref, y_ref, silu_ref):
+    peers, wide = x_ref.shape[:2]
+    pairs = wide // LANES
     t = lax.broadcasted_iota(jnp.int32, (LANES, LANES), 0)
     s = lax.broadcasted_iota(jnp.int32, (LANES, LANES), 1)
     lower = t >= s
-    lane = lax.broadcasted_iota(jnp.int32, (LANES, LANES), 1)
-    for pair in range(x_ref.shape[1] // LANES):
-        mixes, highs, lows = [], [], []
-        for h in (2 * pair, 2 * pair + 1):
-            gap = jnp.where(lower, ell_col[:, h : h + 1] - ell[h : h + 1], -jnp.inf)
-            mixes.append((gram * jnp.exp(gap)).astype(BF16))
-            carry = c * grown[:, h : h + 1]
-            high = carry.astype(BF16)
-            highs.append(high)
-            lows.append((carry - high.astype(F32)).astype(BF16))
-        x = x_ref[0, pl.ds(pair * LANES, LANES), :]
-        state = enter_ref[0, pl.ds(pair * NS, NS), :]
-        high = state.astype(BF16)
-        low = (state - high.astype(F32)).astype(BF16)
-        zero = jnp.zeros_like(x)
-
-        def halves(v):
-            return [jnp.where(lane < SP, v, zero), jnp.where(lane < SP, zero, v)]
-
-        right = jnp.concatenate(halves(x) + halves(high) + halves(low) + halves(high), 0)
-        left = jnp.concatenate(mixes + highs + highs + lows, 1)
-        y_ref[0, pl.ds(pair * LANES, LANES), :] = dot(left, right)
-
-
-def gated_kernel(planes, place_ref, y_ref, gate_ref, proj_ref, codes_ref, rates_ref, *rest):
-    states, decays = rest[: planes - 1], rest[planes - 1 : 2 * planes - 3]
-    out_ref, full_ref, count_ref = rest[2 * planes - 3 :]
-    k = pl.program_id(0)
-
-    @pl.when(k == 0)
-    def _():
-        count_ref[...] = jnp.zeros_like(count_ref)
-
-    sums = code_sums(codes_ref)
-    ell = -rates_ref[0] * (sums + count_ref[...])
-    count_ref[...] += jnp.broadcast_to(sums[:, LANES - 1 :], count_ref.shape)
-    grown = columns_of(jnp.exp(ell))
-    c = proj_ref[0, :LANES, NS:].astype(F32)
-    lane = lax.broadcasted_iota(jnp.int32, (LANES, LANES), 1)
-    for pair in range(y_ref.shape[1] // LANES):
+
+    @pl.loop(0, peers)
+    def _(k):
+        ell = -rates_ref[...] * code_sums(side_ref[k, pl.ds(wide, 16), :])
+        ell_col = columns_of(ell)
+        b = proj_ref[k, :LANES, :NS]
+        c = proj_ref[k, :LANES, NS:]
+        gram = dot(c, b, INNER)
+        states = [enter_ref[k, pl.ds(pair * NS, NS), :] for pair in range(pairs)]
+        carry = carried(jnp.concatenate([c, c], 1), jnp.exp(ell_col), states)
+        for pair in range(pairs):
+            rows = pl.ds(pair * LANES, LANES)
+            mixes = []
+            for h in (2 * pair, 2 * pair + 1):
+                gap = jnp.where(lower, ell_col[:, h : h + 1] - ell[h : h + 1], -jnp.inf)
+                mixes.append((gram * jnp.exp(gap)).astype(BF16))
+            x = x_ref[k, rows, :]
+            zero = jnp.zeros_like(x)
+            right = jnp.concatenate([lane_select(x, zero), lane_select(zero, x)], 0)
+            y_ref[k, rows, :] = dot(jnp.concatenate(mixes, 1), right) + carry[pair]
+            gate = side_ref[k, rows, :].astype(F32)
+            silu_ref[k, rows, :] = gate / (1.0 + jnp.exp(-gate))
+
+
+def gated_kernel(planes, with_full, y_ref, silu_ref, proj_ref, side_ref, rates_ref, *rest):
+    ends, rest = rest[: planes - 1], rest[planes - 1 :]
+    out_ref = rest[0]
+    count_ref, enter_ref = rest[-2:]
+    peers, wide = y_ref.shape[:2]
+    pairs = wide // LANES
+    rates = rates_ref[...]
+    count_ref[...] = jnp.zeros_like(count_ref)
+    for pair in range(pairs):
         rows = pl.ds(pair * LANES, LANES)
-        state = states[-1][rows, :].astype(F32)
+        state = ends[-1][rows, :].astype(F32)
         for i in range(planes - 3, -1, -1):
-            state = states[i][rows, :].astype(F32) + decays[i][pair : pair + 1, :] * state
-        state = state.astype(BF16)
-        zero = jnp.zeros_like(state)
-        right = jnp.concatenate(
-            [jnp.where(lane < SP, state, zero), jnp.where(lane < SP, zero, state)], 0
-        )
-        h = 2 * pair
-        left = jnp.concatenate([c * grown[:, h : h + 1], c * grown[:, h + 1 : h + 2]], 1)
-        y = y_ref[0, rows, :] + dot(left.astype(BF16), right)
-        gate = gate_ref[0, rows, :].astype(F32)
-        y = y * (gate / (1.0 + jnp.exp(-gate)))
-        out_ref[0, rows, :] = y.astype(BF16)
-        full_ref[0, rows, :] = y
+            decay = joined_row(ends[i][wide:, :].astype(F32), pair)
+            state = ends[i][rows, :].astype(F32) + decay * state
+        enter_ref[rows, :] = state
+
+    @pl.loop(0, peers)
+    def _(k):
+        sums = code_sums(side_ref[k, pl.ds(wide, 16), :])
+        grown = columns_of(jnp.exp(-rates * (sums + count_ref[...])))
+        count_ref[...] += jnp.broadcast_to(sums[:, LANES - 1 :], count_ref.shape)
+        c = proj_ref[k, :LANES, NS:]
+        states = [enter_ref[pl.ds(pair * NS, NS), :] for pair in range(pairs)]
+        carry = carried(jnp.concatenate([c, c], 1), grown, states)
+        for pair in range(pairs):
+            rows = pl.ds(pair * LANES, LANES)
+            y = (y_ref[k, rows, :] + carry[pair]) * silu_ref[k, rows, :]
+            out_ref[k, rows, :] = y.astype(BF16)
+            if with_full:
+                rest[1][k, rows, :] = y
 
 
 def finish_kernel(channels, with_proj, g_ref, gain_ref, *rest):
@@ -522,41 +537,41 @@
     peers = lax.axis_size("peer")
     wide = channels // peers
     pairs = wide // LANES
-    place = jnp.stack([lax.axis_index("plane"), lax.axis_index("peer")]).astype(jnp.int32)
+    heads = decay_codes.shape[1] // peers
+    peer = lax.axis_index("peer")
+    place = jnp.stack([lax.axis_index("plane"), peer]).astype(jnp.int32)
 
     def moved(x, distance):
         return lax.ppermute(x, "plane", [(i, i + distance) for i in range(planes - distance)])
 
     kv = pl.pallas_call(
         pack_kv_kernel,
-        grid=(peers,),
-        in_specs=[pl.BlockSpec((tokens, HEAD_SIZE), lambda p: (0, p))] * 2,
-        out_specs=pl.BlockSpec((1, 2 * tokens, HEAD_SIZE), lambda p: (p, 0, 0)),
         out_shape=jax.ShapeDtypeStruct((peers, 2 * tokens, HEAD_SIZE), BF16),
+        compiler_params=params(),
         name="pack_kv",
     )(rotated_keys, values)
     kv_own = lax.all_to_all(kv, "peer", 0, 0)
     kv_one = moved(kv_own, 1)
     kv_two = moved(kv_one, 1)
 
+    packed = pl.pallas_call(
+        pack_heads_kernel,
+        out_shape=jax.ShapeDtypeStruct((peers, wide, LANES), BF16),
+        compiler_params=params(),
+        name="pack_queries",
+    )(queries)
+    arrived = lax.all_to_all(packed, "peer", 0, 0)
+
     coded = jnp.stack([decay_codes >> 7, decay_codes & 127], 0).astype(BF16)
-    heads = decay_codes.shape[1] // peers
     coded = jnp.transpose(coded.reshape(2, tokens, peers, heads), (2, 0, 3, 1))
     coded = coded.reshape(peers, 2 * heads, tokens)
-    q_rows = 2 * wide + 2 * heads
     packed = pl.pallas_call(
-        pack_kernel,
-        grid=(peers,),
-        in_specs=[
-            pl.BlockSpec((tokens, wide), lambda p: (0, p)),
-            pl.BlockSpec((tokens, wide), lambda p: (0, p)),
-            pl.BlockSpec((1, 2 * heads, tokens), lambda p: (p, 0, 0)),
-        ],
-        out_specs=pl.BlockSpec((1, q_rows, LANES), lambda p: (p, 0, 0)),
-        out_shape=jax.ShapeDtypeStruct((peers, q_rows, LANES), BF16),
-        name="pack_queries",
-    )(queries, gate_input, coded)
-    arrived = lax.all_to_all(packed, "peer", 0, 0)
+        pack_heads_kernel,
+        out_shape=jax.ShapeDtypeStruct((peers, wide + 16, LANES), BF16),
+        compiler_params=params(),
+        name="pack_gates",
+    )(gate_input, coded)
+    side = lax.all_to_all(packed, "peer", 0, 0)
 
     def keys_spec(which):
         return pl.BlockSpec((peers, tokens, HEAD_SIZE), lambda j, s: (0, which, 0))
@@ -594,85 +609,44 @@
         name="project",
     )(shares)
 
-    rates = jnp.broadcast_to(decay_rates.reshape(peers, heads, 1), (peers, heads, LANES))
-    gains = norm_gain.reshape(peers, pairs, LANES)
-    rates_spec = pl.BlockSpec((1, heads, LANES), lambda j, s: (s[1], 0, 0))
-    gains_spec = pl.BlockSpec((1, pairs, LANES), lambda j, s: (s[1], 0, 0))
-    codes_spec = block(2 * heads, 2 * wide // (2 * heads))
-    proj_spec = block(proj_rows, 0, 2 * NS)
-
-    def ssd(x, projected, with_gain, decays):
-        common = [block(wide), proj_spec, codes_spec, rates_spec]
-        operands = [x, projected, arrived, rates]
-        if with_gain:
-            common = common + [gains_spec]
-            operands = operands + [gains]
-        normed, entering, end, decay = pl.pallas_call(
+    rates = lax.dynamic_slice_in_dim(decay_rates, peer * heads, heads, 0)
+    rates = jnp.broadcast_to(rates[:, None], (heads, LANES))
+    gains = lax.dynamic_slice_in_dim(norm_gain.reshape(peers, pairs, LANES), peer, 1, 0)[0]
+    full_shape = jax.ShapeDtypeStruct((peers, wide, LANES), F32)
+    half_shape = jax.ShapeDtypeStruct((peers, wide, LANES), BF16)
+
+    def ssd(x, projected, with_gain):
+        operands = [x, projected, side, rates] + ([gains] if with_gain else [])
+        normed, entering, end = pl.pallas_call(
             functools.partial(states_kernel, with_gain),
-            grid_spec=pltpu.PrefetchScalarGridSpec(
-                num_scalar_prefetch=1,
-                grid=(peers,),
-                in_specs=common,
-                out_specs=[
-                    block(wide),
-                    block(wide),
-                    pl.BlockSpec((wide, LANES), lambda j, s: (0, 0)),
-                    pl.BlockSpec((8, LANES), lambda j, s: (0, 0)),
-                ],
-                scratch_shapes=[pltpu.VMEM((wide, LANES), F32), pltpu.VMEM((heads, LANES), F32)],
-            ),
-            out_shape=[
-                jax.ShapeDtypeStruct((peers, wide, LANES), BF16),
-                jax.ShapeDtypeStruct((peers, wide, LANES), F32),
-                jax.ShapeDtypeStruct((wide, LANES), BF16),
-                jax.ShapeDtypeStruct((8, LANES), F32),
-            ],
+            out_shape=[half_shape, full_shape, jax.ShapeDtypeStruct((wide + 16, LANES), BF16)],
+            scratch_shapes=[pltpu.VMEM((wide, LANES), F32), pltpu.VMEM((heads, LANES), F32)],
             compiler_params=params(),
             cost_estimate=cost(10**9, 4 * 10**6),
             name="states",
-        )(place, *operands)
+        )(*operands)
         earlier = [moved(end, i) for i in range(1, planes)]
-        if decays is None:
-            decays = [moved(decay, i) for i in range(1, planes - 1)]
-        y = pl.pallas_call(
+        y, silu = pl.pallas_call(
             local_kernel,
-            grid_spec=pltpu.PrefetchScalarGridSpec(
-                num_scalar_prefetch=1,
-                grid=(peers,),
-                in_specs=[block(wide), proj_spec, codes_spec, rates_spec, block(wide)],
-                out_specs=block(wide),
-            ),
-            out_shape=jax.ShapeDtypeStruct((peers, wide, LANES), F32),
+            out_shape=[full_shape, full_shape],
             compiler_params=params(),
             cost_estimate=cost(2 * 10**9, 5 * 10**6, 10**6),
             name="local",
-        )(place, normed, projected, arrived, rates, entering)
-        gated, full = pl.pallas_call(
-            functools.partial(gated_kernel, planes),
-            grid_spec=pltpu.PrefetchScalarGridSpec(
-                num_scalar_prefetch=1,
-                grid=(peers,),
-                in_specs=[block(wide), block(wide, 1), proj_spec, codes_spec, rates_spec]
-                + [pl.BlockSpec((wide, LANES), lambda j, s: (0, 0))] * (planes - 1)
-                + [pl.BlockSpec((8, LANES), lambda j, s: (0, 0))] * (planes - 2),
-                out_specs=[block(wide), block(wide)],
-                scratch_shapes=[pltpu.VMEM((heads, LANES), F32)],
-            ),
-            out_shape=[
-                jax.ShapeDtypeStruct((peers, wide, LANES), BF16),
-                jax.ShapeDtypeStruct((peers, wide, LANES), F32),
-            ],
+        )(normed, projected, side, rates, entering)
+        return pl.pallas_call(
+            functools.partial(gated_kernel, planes, not with_gain),
+            out_shape=[half_shape] if with_gain else [half_shape, full_shape],
+            scratch_shapes=[pltpu.VMEM((heads, LANES), F32), pltpu.VMEM((wide, LANES), F32)],
             compiler_params=params(),
             cost_estimate=cost(10**9, 5 * 10**6, 10**6),
             name="gated",
-        )(place, y, arrived, projected, arrived, rates, *earlier, *decays)
-        return gated, full, decays
+        )(y, silu, projected, side, rates, *earlier)
 
     gain_rows = norm_gain.reshape(channels // LANES, LANES)
     gathered = (peers, wide, LANES)
 
     projected = lax.all_gather(proj, "peer")
-    gated, full, decays = ssd(attended, projected, False, None)
+    gated, full = ssd(attended, projected, False)
     first, proj = pl.pallas_call(
         functools.partial(finish_kernel, channels, True),
         in_specs=[
@@ -689,7 +663,7 @@
         name="finish_first",
     )(lax.all_to_all(gated, "peer", 0, 0), gain_rows, bc_weight)
     projected = lax.all_gather(proj, "peer")
-    gated, _, _ = ssd(full, projected, True, decays)
+    (gated,) = ssd(full, projected, True)
     second = pl.pallas_call(
         functools.partial(finish_kernel, channels, False),
         in_specs=[whole_block(gathered), whole_block(gain_rows.shape)],

time: 254 us -> 221 us (0.87)
  Pallas kernels: 101 us -> 63.5 us
  starting transfers between devices: 39.2 us -> 44.5 us
  waiting for transfers between devices: 41.1 us -> 44.8 us
    pallas_call x8 -> x9, Pallas kernels: 66.9 us -> 32.5 us  [the longest x2 13.3 us: ssd(): pl.pallas_call(local_kernel, out_shape=[full_shape, full_shape], compiler...]
    all_to_all x2 -> x1, blocking collectives: 39.1 us -> 17.9 us  [head_sharded(): lax.all_to_all(gated, 'peer', 0, 0)]
    all_to_all x0 -> x1, blocking collectives: none -> 14.8 us  [head_sharded(): kv_own = lax.all_to_all(kv, 'peer', 0, 0)]
    all_to_all x1 -> x2, waiting for transfers between devices: 3.18 us -> 15.3 us  [the longest x1 15.3 us: head_sharded(): lax.all_to_all(gated, 'peer', 0, 0)]
    ppermute x10 -> x8, waiting for transfers between devices: 21.9 us -> 9.95 us  [moved(): lax.ppermute(x, 'plane', [(i, i + distance) for i in range(planes - dista...]
    all_gather x2, blocking collectives: 21.9 us -> 27.2 us  [head_sharded(): projected = lax.all_gather(proj, 'peer')]
    all_to_all x1, waiting for transfers between devices: 0.01 us -> 4.67 us  [head_sharded(): arrived = lax.all_to_all(packed, 'peer', 0, 0)]
    ppermute x10 -> x8, starting transfers between devices: 26.7 us -> 29.4 us  [moved(): lax.ppermute(x, 'plane', [(i, i + distance) for i in range(planes - dista...]
  transfers between devices with their start and end apart: 13 -> 12, of which waited for: 4 -> 5; matrix products, arithmetic and copies ran while one was open for 1% -> 0% of each run, Pallas kernels for 10% -> 8%
where the time goes in v2:
time: 221 us; the launch traced here: 220 us
  Pallas kernels  63.5 us (29%)
  blocking collectives  59.9 us (27%)
  waiting for transfers between devices  44.8 us (20%)
  starting transfers between devices  44.5 us (20%)
  local copies, waits for them, and re-layouts  6.05 us (3%)
    ppermute x8, starting transfers between devices, moved(): lax.ppermute(x, 'plane', [(i, i + distance) for i in range(planes - dista...  29.4 us
    all_gather x2, blocking collectives, head_sharded(): projected = lax.all_gather(proj, 'peer')  27.2 us
    pallas_call x1, Pallas kernels, head_sharded(): pl.pallas_call(attend_kernel, grid_spec=pltpu.PrefetchScalarGridSpec(num_...  25.4 us
    all_to_all x1, blocking collectives, head_sharded(): lax.all_to_all(gated, 'peer', 0, 0)  17.9 us
    all_to_all x1, waiting for transfers between devices, head_sharded(): lax.all_to_all(gated, 'peer', 0, 0)  15.3 us
    all_to_all x1, waiting for transfers between devices, head_sharded(): shares = lax.all_to_all(partial, 'peer', 0, 0)  14.9 us
    all_to_all x1, blocking collectives, head_sharded(): kv_own = lax.all_to_all(kv, 'peer', 0, 0)  14.8 us
    pallas_call x2, Pallas kernels, ssd(): pl.pallas_call(local_kernel, out_shape=[full_shape, full_shape], compiler...  13.3 us
  transfers between devices with their start and end apart: 12, of which 5 were waited for; matrix products, arithmetic and copies ran while one was open for 0% of the time, Pallas kernels for 8%

profile of v2, /device:TPU:0, one launch (start us, length us, event | category | flops | bytes accessed | tf_op | source)
XLA Modules:
  0.0 219.8 jit_solution(12927124368804487913)
XLA Ops:
  2.7 14.8 %all_to_all.30.ko_ref.vo_ref = bf16[8,256,128]{2,1,0:T(8,128)(2,1)} all-to-all(bf16[8,256,128]{2,1,0:T(8,128)(2,1)S(1)} %pack_kv.1), channel_id=1, replica_groups=mesh['plane'=4,'peer'=8,'tp'=1] {'peer'}, dimensions={0} | all-to-all | bytes 1048576 | tf_op jit(solution)/shard_map/all_to_all | solution.py:553
  17.5 4.4 %collective-permute-start = (bf16[8,256,128]{2,1,0:T(8,128)(2,1)}, bf16[8,256,128]{2,1,0:T(8,128)(2,1)}, u32[]{:S(2)}, u32[]{:S(2)}) collective-permute-start(bf16[8,256,128]{2,1,0:T(8,128)(2,1)} %all_to_all.30.ko_ref.vo_ref), channel_id=1, source_target_pairs={{0,8},{8,16},{16,24},{1,9},{9,17},{17,25},{2,10},{10,18},{18,26},{... | collective-permute-start | bytes 1572872 | tf_op jit(solution)/shard_map/ppermute | solution.py:545
  23.1 3.6 %all-to-all-start = ((bf16[8,512,128]{2,1,0:T(8,128)(2,1)}), bf16[8,512,128]{2,1,0:T(8,128)(2,1)S(1)}, u32[]{:S(2)}, u32[]{:S(2)}) async-start(bf16[8,512,128]{2,1,0:T(8,128)(2,1)} %pack_queries.1), calls=%async_computation | async-start | bytes 2097152 | tf_op jit(solution)/shard_map/all_to_all | solution.py:563
  26.7 5.4 %collective-permute-done.k1_ref.v1_ref = bf16[8,256,128]{2,1,0:T(8,128)(2,1)} collective-permute-done((bf16[8,256,128]{2,1,0:T(8,128)(2,1)}, bf16[8,256,128]{2,1,0:T(8,128)(2,1)}, u32[]{:S(2)}, u32[]{:S(2)}) %collective-permute-start) | collective-permute-done | bytes 524320 | tf_op jit(solution)/shard_map/ppermute | solution.py:545
  32.1 5.2 %collective-permute-start.1 = (bf16[8,256,128]{2,1,0:T(8,128)(2,1)}, bf16[8,256,128]{2,1,0:T(8,128)(2,1)}, u32[]{:S(2)}, u32[]{:S(2)}) collective-permute-start(bf16[8,256,128]{2,1,0:T(8,128)(2,1)} %collective-permute-done.k1_ref.v1_ref), channel_id=1, source_target_pairs={{0,8},{8,16},{16,24},{1,9},{9,17},{17,25},{2,10},{10,18},{18,26},{... | collective-permute-start | bytes 1572872 | tf_op jit(solution)/shard_map/ppermute | solution.py:545
  37.3 4.7 %all-to-all-done.q_ref = bf16[8,512,128]{2,1,0:T(8,128)(2,1)S(1)} async-done(((bf16[8,512,128]{2,1,0:T(8,128)(2,1)}), bf16[8,512,128]{2,1,0:T(8,128)(2,1)S(1)}, u32[]{:S(2)}, u32[]{:S(2)}) %all-to-all-start) | async-done | bytes 1048608 | tf_op jit(solution)/shard_map/all_to_all | solution.py:563
  42.0 4.5 %collective-permute-done.1.k2_ref.v2_ref = bf16[8,256,128]{2,1,0:T(8,128)(2,1)} collective-permute-done((bf16[8,256,128]{2,1,0:T(8,128)(2,1)}, bf16[8,256,128]{2,1,0:T(8,128)(2,1)}, u32[]{:S(2)}, u32[]{:S(2)}) %collective-permute-start.1) | collective-permute-done | bytes 524320 | tf_op jit(solution)/shard_map/ppermute | solution.py:545
  46.5 25.4 %attend.1 = (bf16[8,512,128]{2,1,0:T(8,128)(2,1)S(1)}, f32[8,136,256]{2,1,0:T(8,128)}) custom-call(s32[2]{0:T(128)S(1)} %pad_add_fusion.place_ref, bf16[8,512,128]{2,1,0:T(8,128)(2,1)S(1)} %all-to-all-done.q_ref, bf16[8,256,128]{2,1,0:T(8,128)(2,1)} %all_to_all.30.ko_ref.vo_ref, bf16[8,256,128]{2,1,0:T(8,128)(2,1)} %all_to_all.30.ko_ref.vo_ref, ...), custom_call_target="tpu_custom_call" | custom-call | flops 5000000000 | bytes 4000000 | tf_op jit(solution)/shard_map/attend/pallas_call | solution.py:583
  72.9 4.4 %all-to-all-start.2 = ((f32[8,136,256]{2,1,0:T(8,128)}), f32[8,136,256]{2,1,0:T(8,128)}, u32[]{:S(2)}, u32[]{:S(2)}) async-start(f32[8,136,256]{2,1,0:T(8,128)} %get-tuple-element.19), calls=%async_computation.2 | async-start | bytes 2228224 | tf_op jit(solution)/shard_map/all_to_all | solution.py:603
  78.5 14.9 %all-to-all-done.2.part_ref = f32[8,136,256]{2,1,0:T(8,128)} async-done(((f32[8,136,256]{2,1,0:T(8,128)}), f32[8,136,256]{2,1,0:T(8,128)}, u32[]{:S(2)}, u32[]{:S(2)}) %all-to-all-start.2) | async-done | bytes 1114144 | tf_op jit(solution)/shard_map/all_to_all | solution.py:603
  93.4 3.6 %all-to-all-start.3 = ((bf16[8,528,128]{2,1,0:T(8,128)(2,1)}), bf16[8,528,128]{2,1,0:T(8,128)(2,1)S(1)}, u32[]{:S(2)}, u32[]{:S(2)}) async-start(bf16[8,528,128]{2,1,0:T(8,128)(2,1)} %pack_gates.1), calls=%async_computation.3 | async-start | bytes 2162688 | tf_op jit(solution)/shard_map/all_to_all | solution.py:574
  97.0 2.0 project.1
  99.1 18.2 %all-gather = bf16[1152,256]{1,0:T(8,128)(2,1)S(1)} all-gather(bf16[144,256]{1,0:T(8,128)(2,1)} %project.1), channel_id=2, replica_groups=mesh['plane'=4,'peer'=8,'tp'=1] {'peer'}, dimensions={0}, use_global_device_ids=true | all-gather | bytes 663552 | tf_op jit(solution)/shard_map/all_gather | solution.py:648
  117.4 3.8 %states.2 = (bf16[8,512,128]{2,1,0:T(8,128)(2,1)S(1)}, f32[8,512,128]{2,1,0:T(8,128)S(1)}, bf16[528,128]{1,0:T(8,128)(2,1)S(1)}) custom-call(bf16[8,512,128]{2,1,0:T(8,128)(2,1)S(1)} %copy-done.10, bf16[8,144,256]{2,1,0:T(8,128)(2,1)S(1)} %bitcast.23, bf16[8,528,128]{2,1,0:T(8,128)(2,1)S(1)} %all-to-all-done.3.side_ref, f32[8,128]{1,0:T(8,128)S(1)} %broadcast_in_dim.2.rates_ref), custom_call_target="tpu_custom_call" | custom-call | flops 1000000000 | bytes 4000000 | tf_op jit(solution)/shard_map/states/pallas_call | solution.py:620
  121.1 4.4 %collective-permute-start.2 = (bf16[528,128]{1,0:T(8,128)(2,1)S(1)}, bf16[528,128]{1,0:T(8,128)(2,1)S(1)}, u32[]{:S(2)}, u32[]{:S(2)}) collective-permute-start(bf16[528,128]{1,0:T(8,128)(2,1)S(1)} %get-tuple-element.24), channel_id=1, source_target_pairs={{0,8},{8,16},{16,24},{1,9},{9,17},{17,25},{2,10},{10,18},{18,26},{... | collective-permute-start | bytes 405512 | tf_op jit(solution)/shard_map/ppermute | solution.py:545
  125.5 4.5 %collective-permute-start.3 = (bf16[528,128]{1,0:T(8,128)(2,1)S(1)}, bf16[528,128]{1,0:T(8,128)(2,1)S(1)}, u32[]{:S(2)}, u32[]{:S(2)}) collective-permute-start(bf16[528,128]{1,0:T(8,128)(2,1)S(1)} %get-tuple-element.24), channel_id=1, source_target_pairs={{0,16},{8,24},{1,17},{9,25},{2,18},{10,26},{3,19},{11,27},{4,20},{... | collective-permute-start | bytes 405512 | tf_op jit(solution)/shard_map/ppermute | solution.py:545
  130.0 1.3 collective-permute-start.4
  131.4 6.7 %local.2 = (f32[8,512,128]{2,1,0:T(8,128)S(1)}, f32[8,512,128]{2,1,0:T(8,128)S(1)}) custom-call(bf16[8,512,128]{2,1,0:T(8,128)(2,1)S(1)} %get-tuple-element.20.x_ref, bf16[8,144,256]{2,1,0:T(8,128)(2,1)S(1)} %bitcast.24, bf16[8,528,128]{2,1,0:T(8,128)(2,1)S(1)} %all-to-all-done.3.side_ref, f32[8,128]{1,0:T(8,128)S(1)} %broadcast_in_dim.2.rates_ref, ...), custom_call_target="tpu_custom_call" | custom-call | flops 2000000000 | bytes 5000000 | tf_op jit(solution)/shard_map/local/pallas_call | solution.py:629
  138.1 5.1 %gated.2 = (bf16[8,512,128]{2,1,0:T(8,128)(2,1)}, f32[8,512,128]{2,1,0:T(8,128)S(1)}) custom-call(f32[8,512,128]{2,1,0:T(8,128)S(1)} %get-tuple-element.22.y_ref, f32[8,512,128]{2,1,0:T(8,128)S(1)} %get-tuple-element.23.silu_ref, bf16[8,144,256]{2,1,0:T(8,128)(2,1)S(1)} %bitcast.25, bf16[8,528,128]{2,1,0:T(8,128)(2,1)S(1)} %all-to-all-done.3.side_ref, ...), custom_call_target="tpu_custom_call" | custom-call | flops 1000000000 | bytes 5000000 | tf_op jit(solution)/shard_map/gated/pallas_call | solution.py:636
  143.1 1.3 copy-done.2
  144.4 3.7 %all-to-all-start.4 = ((bf16[8,512,128]{2,1,0:T(8,128)(2,1)}), bf16[8,512,128]{2,1,0:T(8,128)(2,1)S(1)}, u32[]{:S(2)}, u32[]{:S(2)}) async-start(bf16[8,512,128]{2,1,0:T(8,128)(2,1)} %get-tuple-element.25), calls=%async_computation.4 | async-start | bytes 2097152 | tf_op jit(solution)/shard_map/all_to_all | solution.py:664
  148.2 15.3 %all-to-all-done.4.g_ref = bf16[8,512,128]{2,1,0:T(8,128)(2,1)S(1)} async-done(((bf16[8,512,128]{2,1,0:T(8,128)(2,1)}), bf16[8,512,128]{2,1,0:T(8,128)(2,1)S(1)}, u32[]{:S(2)}, u32[]{:S(2)}) %all-to-all-start.4) | async-done | bytes 1048608 | tf_op jit(solution)/shard_map/all_to_all | solution.py:664
  163.5 1.6 copy-done.1
  165.1 1.9 finish_first.1
  166.9 9.0 %all-gather.1 = bf16[1152,256]{1,0:T(8,128)(2,1)S(1)} all-gather(bf16[144,256]{1,0:T(8,128)(2,1)S(1)} %get-tuple-element.28), channel_id=3, replica_groups=mesh['plane'=4,'peer'=8,'tp'=1] {'peer'}, dimensions={0}, use_global_device_ids=true | all-gather | bytes 663552 | tf_op jit(solution)/shard_map/all_gather | solution.py:665
  175.9 3.8 %states.3 = (bf16[8,512,128]{2,1,0:T(8,128)(2,1)S(1)}, f32[8,512,128]{2,1,0:T(8,128)S(1)}, bf16[528,128]{1,0:T(8,128)(2,1)S(1)}) custom-call(f32[8,512,128]{2,1,0:T(8,128)S(1)} %copy-done.3, bf16[8,144,256]{2,1,0:T(8,128)(2,1)S(1)} %bitcast.20, bf16[8,528,128]{2,1,0:T(8,128)(2,1)S(1)} %all-to-all-done.3.side_ref, f32[8,128]{1,0:T(8,128)S(1)} %broadcast_in_dim.2.rates_ref, ...), custom_call_target="tpu_custom_call" | custom-call | flops 1000000000 | bytes 4000000 | tf_op jit(solution)/shard_map/states/pallas_call | solution.py:620
  179.8 3.0 %collective-permute-start.5 = (bf16[528,128]{1,0:T(8,128)(2,1)S(1)}, bf16[528,128]{1,0:T(8,128)(2,1)S(1)}, u32[]{:S(2)}, u32[]{:S(2)}) collective-permute-start(bf16[528,128]{1,0:T(8,128)(2,1)S(1)} %get-tuple-element.33), channel_id=1, source_target_pairs={{0,8},{8,16},{16,24},{1,9},{9,17},{17,25},{2,10},{10,18},{18,26},{... | collective-permute-start | bytes 405512 | tf_op jit(solution)/shard_map/ppermute | solution.py:545
  182.8 5.3 %collective-permute-start.6 = (bf16[528,128]{1,0:T(8,128)(2,1)S(1)}, bf16[528,128]{1,0:T(8,128)(2,1)S(1)}, u32[]{:S(2)}, u32[]{:S(2)}) collective-permute-start(bf16[528,128]{1,0:T(8,128)(2,1)S(1)} %get-tuple-element.33), channel_id=1, source_target_pairs={{0,16},{8,24},{1,17},{9,25},{2,18},{10,26},{3,19},{11,27},{4,20},{... | collective-permute-start | bytes 405512 | tf_op jit(solution)/shard_map/ppermute | solution.py:545
  189.4 6.7 %local.3 = (f32[8,512,128]{2,1,0:T(8,128)S(1)}, f32[8,512,128]{2,1,0:T(8,128)S(1)}) custom-call(bf16[8,512,128]{2,1,0:T(8,128)(2,1)S(1)} %get-tuple-element.29.x_ref, bf16[8,144,256]{2,1,0:T(8,128)(2,1)S(1)} %bitcast.21, bf16[8,528,128]{2,1,0:T(8,128)(2,1)S(1)} %all-to-all-done.3.side_ref, f32[8,128]{1,0:T(8,128)S(1)} %broadcast_in_dim.2.rates_ref, ...), custom_call_target="tpu_custom_call" | custom-call | flops 2000000000 | bytes 5000000 | tf_op jit(solution)/shard_map/local/pallas_call | solution.py:629
  196.1 4.1 %gated.3 = bf16[8,512,128]{2,1,0:T(8,128)(2,1)S(1)} custom-call(f32[8,512,128]{2,1,0:T(8,128)S(1)} %get-tuple-element.31.y_ref, f32[8,512,128]{2,1,0:T(8,128)S(1)} %get-tuple-element.32.silu_ref, bf16[8,144,256]{2,1,0:T(8,128)(2,1)S(1)} %bitcast.22, bf16[8,528,128]{2,1,0:T(8,128)(2,1)S(1)} %all-to-all-done.3.side_ref, ...), custom_call_target="tpu_custom_call" | custom-call | flops 1000000000 | bytes 5000000 | tf_op jit(solution)/shard_map/gated/pallas_call | solution.py:636
  200.2 17.9 %all_to_all.31.g_ref = bf16[8,512,128]{2,1,0:T(8,128)(2,1)S(1)} all-to-all(bf16[8,512,128]{2,1,0:T(8,128)(2,1)S(1)} %gated.3), channel_id=1, replica_groups=mesh['plane'=4,'peer'=8,'tp'=1] {'peer'}, dimensions={0} | all-to-all | bytes 2097152 | tf_op jit(solution)/shard_map/all_to_all | solution.py:674
  218.1 1.7 finish_second.1
  (41 shorter events, 7.0 us)
Async XLA Ops:
  0.6 21.3 %copy-start.4 = (bf16[128,4096]{1,0:T(8,128)(2,1)S(1)}, bf16[128,4096]{1,0:T(8,128)(2,1)}, u32[]{:S(2)}) copy-start(bf16[128,4096]{1,0:T(8,128)(2,1)} %x_ref.2) | copy-start | bytes 3145732
  0.6 1.0 copy-start.6
  1.7 0.9 copy-start.7
  17.5 29.0 %copy-start = (bf16[4096,256]{1,0:T(8,128)(2,1)S(1)}, bf16[4096,256]{1,0:T(8,128)(2,1)}, u32[]{:S(2)}) copy-start(bf16[4096,256]{1,0:T(8,128)(2,1)} %rest_0_.1) | copy-start | bytes 6291460
  17.5 14.5 %collective-permute-start = (bf16[8,256,128]{2,1,0:T(8,128)(2,1)}, bf16[8,256,128]{2,1,0:T(8,128)(2,1)}, u32[]{:S(2)}, u32[]{:S(2)}) collective-permute-start(bf16[8,256,128]{2,1,0:T(8,128)(2,1)} %all_to_all.30.ko_ref.vo_ref), channel_id=1, source_target_pairs={{0,8},{8,16},{16,24},{1,9},{9,17},{17,25},{2,10},{10,18},{18,26},{... | collective-permute-start | bytes 1572872 | tf_op jit(solution)/shard_map/ppermute | solution.py:545
  23.1 18.9 %all-to-all-start = ((bf16[8,512,128]{2,1,0:T(8,128)(2,1)}), bf16[8,512,128]{2,1,0:T(8,128)(2,1)S(1)}, u32[]{:S(2)}, u32[]{:S(2)}) async-start(bf16[8,512,128]{2,1,0:T(8,128)(2,1)} %pack_queries.1), calls=%async_computation | async-start | bytes 2097152 | tf_op jit(solution)/shard_map/all_to_all | solution.py:563
  32.1 14.5 %collective-permute-start.1 = (bf16[8,256,128]{2,1,0:T(8,128)(2,1)}, bf16[8,256,128]{2,1,0:T(8,128)(2,1)}, u32[]{:S(2)}, u32[]{:S(2)}) collective-permute-start(bf16[8,256,128]{2,1,0:T(8,128)(2,1)} %collective-permute-done.k1_ref.v1_ref), channel_id=1, source_target_pairs={{0,8},{8,16},{16,24},{1,9},{9,17},{17,25},{2,10},{10,18},{18,26},{... | collective-permute-start | bytes 1572872 | tf_op jit(solution)/shard_map/ppermute | solution.py:545
  71.9 1.0 copy-start.9
  72.9 4.4 %copy-start.11 = (s32[128,64]{0,1:T(8,128)S(1)}, s32[128,64]{0,1:T(8,128)}, u32[]{:S(2)}) copy-start(s32[128,64]{0,1:T(8,128)} %param.12) | copy-start | bytes 98308
  72.9 4.4 %copy-start.5 = (bf16[128,4096]{1,0:T(8,128)(2,1)S(1)}, bf16[128,4096]{1,0:T(8,128)(2,1)}, u32[]{:S(2)}) copy-start(bf16[128,4096]{1,0:T(8,128)(2,1)} %x_ref.3) | copy-start | bytes 3145732
  72.9 20.5 %all-to-all-start.2 = ((f32[8,136,256]{2,1,0:T(8,128)}), f32[8,136,256]{2,1,0:T(8,128)}, u32[]{:S(2)}, u32[]{:S(2)}) async-start(f32[8,136,256]{2,1,0:T(8,128)} %get-tuple-element.19), calls=%async_computation.2 | async-start | bytes 2228224 | tf_op jit(solution)/shard_map/all_to_all | solution.py:603
  77.3 19.6 %copy-start.12 = (f32[64]{0:T(128)S(1)}, f32[64]{0:T(128)}, u32[]{:S(2)}) copy-start(f32[64]{0:T(128)} %param.11) | copy-start | bytes 772
  78.5 38.8 %copy-start.10 = (bf16[8,512,128]{2,1,0:T(8,128)(2,1)S(1)}, bf16[8,512,128]{2,1,0:T(8,128)(2,1)}, u32[]{:S(2)}) copy-start(bf16[8,512,128]{2,1,0:T(8,128)(2,1)} %copy-done.9) | copy-start | bytes 3145732
  93.4 23.9 %all-to-all-start.3 = ((bf16[8,528,128]{2,1,0:T(8,128)(2,1)}), bf16[8,528,128]{2,1,0:T(8,128)(2,1)S(1)}, u32[]{:S(2)}, u32[]{:S(2)}) async-start(bf16[8,528,128]{2,1,0:T(8,128)(2,1)} %pack_gates.1), calls=%async_computation.3 | async-start | bytes 2162688 | tf_op jit(solution)/shard_map/all_to_all | solution.py:574
  121.1 16.9 %collective-permute-start.2 = (bf16[528,128]{1,0:T(8,128)(2,1)S(1)}, bf16[528,128]{1,0:T(8,128)(2,1)S(1)}, u32[]{:S(2)}, u32[]{:S(2)}) collective-permute-start(bf16[528,128]{1,0:T(8,128)(2,1)S(1)} %get-tuple-element.24), channel_id=1, source_target_pairs={{0,8},{8,16},{16,24},{1,9},{9,17},{17,25},{2,10},{10,18},{18,26},{... | collective-permute-start | bytes 405512 | tf_op jit(solution)/shard_map/ppermute | solution.py:545
  125.5 12.5 %collective-permute-start.3 = (bf16[528,128]{1,0:T(8,128)(2,1)S(1)}, bf16[528,128]{1,0:T(8,128)(2,1)S(1)}, u32[]{:S(2)}, u32[]{:S(2)}) collective-permute-start(bf16[528,128]{1,0:T(8,128)(2,1)S(1)} %get-tuple-element.24), channel_id=1, source_target_pairs={{0,16},{8,24},{1,17},{9,25},{2,18},{10,26},{3,19},{11,27},{4,20},{... | collective-permute-start | bytes 405512 | tf_op jit(solution)/shard_map/ppermute | solution.py:545
  130.0 8.0 %collective-permute-start.4 = (bf16[528,128]{1,0:T(8,128)(2,1)S(1)}, bf16[528,128]{1,0:T(8,128)(2,1)S(1)}, u32[]{:S(2)}, u32[]{:S(2)}) collective-permute-start(bf16[528,128]{1,0:T(8,128)(2,1)S(1)} %get-tuple-element.24), channel_id=1, source_target_pairs={{0,24},{1,25},{2,26},{3,27},{4,28},{5,29},{6,30},{7,31}} | collective-permute-start | bytes 405512 | tf_op jit(solution)/shard_map/ppermute | solution.py:545
  143.1 1.3 copy-start.2
  144.4 3.7 %copy-start.8 = (f32[4096]{0:T(1024)S(1)}, f32[4096]{0:T(1024)}, u32[]{:S(2)}) copy-start(f32[4096]{0:T(1024)} %param.14) | copy-start | bytes 49156
  144.4 19.0 %all-to-all-start.4 = ((bf16[8,512,128]{2,1,0:T(8,128)(2,1)}), bf16[8,512,128]{2,1,0:T(8,128)(2,1)S(1)}, u32[]{:S(2)}, u32[]{:S(2)}) async-start(bf16[8,512,128]{2,1,0:T(8,128)(2,1)} %get-tuple-element.25), calls=%async_computation.4 | async-start | bytes 2097152 | tf_op jit(solution)/shard_map/all_to_all | solution.py:664
  163.5 1.6 copy-start.1
  165.0 10.9 %copy-start.3 = (f32[8,512,128]{2,1,0:T(8,128)S(1)}, f32[8,512,128]{2,1,0:T(8,128)}, u32[]{:S(2)}) copy-start(f32[8,512,128]{2,1,0:T(8,128)} %copy-done.2) | copy-start | bytes 6291460
  179.8 16.3 %collective-permute-start.5 = (bf16[528,128]{1,0:T(8,128)(2,1)S(1)}, bf16[528,128]{1,0:T(8,128)(2,1)S(1)}, u32[]{:S(2)}, u32[]{:S(2)}) collective-permute-start(bf16[528,128]{1,0:T(8,128)(2,1)S(1)} %get-tuple-element.33), channel_id=1, source_target_pairs={{0,8},{8,16},{16,24},{1,9},{9,17},{17,25},{2,10},{10,18},{18,26},{... | collective-permute-start | bytes 405512 | tf_op jit(solution)/shard_map/ppermute | solution.py:545
  182.8 13.3 %collective-permute-start.6 = (bf16[528,128]{1,0:T(8,128)(2,1)S(1)}, bf16[528,128]{1,0:T(8,128)(2,1)S(1)}, u32[]{:S(2)}, u32[]{:S(2)}) collective-permute-start(bf16[528,128]{1,0:T(8,128)(2,1)S(1)} %get-tuple-element.33), channel_id=1, source_target_pairs={{0,16},{8,24},{1,17},{9,25},{2,18},{10,26},{3,19},{11,27},{4,20},{... | collective-permute-start | bytes 405512 | tf_op jit(solution)/shard_map/ppermute | solution.py:545
  188.1 8.0 %collective-permute-start.7 = (bf16[528,128]{1,0:T(8,128)(2,1)S(1)}, bf16[528,128]{1,0:T(8,128)(2,1)S(1)}, u32[]{:S(2)}, u32[]{:S(2)}) collective-permute-start(bf16[528,128]{1,0:T(8,128)(2,1)S(1)} %get-tuple-element.33), channel_id=1, source_target_pairs={{0,24},{1,25},{2,26},{3,27},{4,28},{5,29},{6,30},{7,31}} | collective-permute-start | bytes 405512 | tf_op jit(solution)/shard_map/ppermute | solution.py:545

commit v3 on v2

--- a/solution.py
+++ b/solution.py
@@ -194,7 +194,7 @@
 BF16 = jnp.bfloat16
 LANES = 128
 INNER = (((1,), (1,)), ((), ()))
-VMEM_BYTES = 24 * 1024 * 1024
+MIB = 1024 * 1024
 
 
 def dot(a, b, dims=(((1,), (0,)), ((), ()))):
@@ -245,90 +245,114 @@
 
 
 def attend_kernel(
-    place_ref, q_ref, ko_ref, vo_ref, k1_ref, v1_ref, k2_ref, v2_ref, bc_ref, x_ref, part_ref, s_ref
+    place_ref, q_ref, ko_ref, vo_ref, k1_ref, v1_ref, k2_ref, v2_ref, bc_ref, x_ref, part_ref, *scores
 ):
-    j = pl.program_id(0)
     plane = place_ref[0]
     blocks = ko_ref.shape[0]
-    rows = q_ref.shape[1]
-    q = q_ref[0]
-    bias1 = jnp.where(plane >= 1, 0.0, -jnp.inf).astype(F32)
+    steps, rows = q_ref.shape[:2]
+    half = blocks // 2
+    count = 2 * half
+    unit_rows = 2 * LANES
+    splits = rows // unit_rows
+    factor = math.log2(math.e) / math.sqrt(HEAD_SIZE)
     bias2 = jnp.where(plane >= 2, 0.0, -jnp.inf).astype(F32)
     lane = lax.broadcasted_iota(jnp.int32, (1, 2 * LANES), 1)
-    t_pos = lax.broadcasted_iota(jnp.int32, (rows, LANES), 0) % LANES
-    s_pos = lax.broadcasted_iota(jnp.int32, (rows, LANES), 1)
+    t_pos = lax.broadcasted_iota(jnp.int32, (unit_rows, LANES), 0) % LANES
+    s_pos = lax.broadcasted_iota(jnp.int32, (unit_rows, LANES), 1)
     causal = s_pos <= t_pos
-    half = blocks // 2
-
-    def mixed(i, own_ref, far_ref):
-        return jnp.where(i < j, own_ref[i], far_ref[i + 1])
-
-    top = None
-    for i in range(2 * half):
-        if i < half:
-            keys = k1_ref[2 * i : 2 * i + 2].reshape(2 * LANES, HEAD_SIZE)
-            s = dot(q, keys, INNER) + bias1
-        else:
-            a = 2 * (i - half)
-            first = mixed(a, ko_ref, k2_ref)
-            bias_a = jnp.where(a < j, 0.0, bias2)
-            if i < 2 * half - 1:
-                keys = jnp.concatenate([first, mixed(a + 1, ko_ref, k2_ref)], 0)
-                bias_b = jnp.where(a + 1 < j, 0.0, bias2)
-                s = dot(q, keys, INNER) + jnp.where(lane < LANES, bias_a, bias_b)
+
+    def unit(n):
+        here, part = n // splits, n % splits
+        j = pl.program_id(0) * steps + here
+        s_ref = scores[n % len(scores)]
+        span = pl.ds(part * unit_rows, unit_rows)
+        held = {}
+
+        def mixed(i, own_ref, far_ref):
+            return jnp.where(i < j, own_ref[i], far_ref[i + 1])
+
+        def score(i):
+            q = q_ref[here, span, :]
+            if i < half:
+                s = dot(q, k1_ref[2 * i : 2 * i + 2].reshape(2 * LANES, HEAD_SIZE), INNER)
+                key = "near"
             else:
-                keys = jnp.concatenate([first, ko_ref[j]], 0)
-                s = dot(q, keys, INNER)
-                edge = dot(q, k2_ref[j], INNER) + bias2
-                s = jnp.concatenate(
-                    [s[:, :LANES] + bias_a, jnp.where(causal, s[:, LANES:], edge)], 1
-                )
-        s_ref[i] = s
-        high = jnp.maximum(s[:, :LANES], s[:, LANES:])
-        top = high if top is None else jnp.maximum(top, high)
-    factor = math.log2(math.e) / math.sqrt(HEAD_SIZE)
-    top = jnp.max(top, axis=1, keepdims=True) * factor
-    weight = jnp.zeros((rows, LANES), F32)
-    for i in range(2 * half):
-        p = jnp.exp2(s_ref[i] * factor - top)
-        s_ref[i] = p
-        weight += p[:, :LANES] + p[:, LANES:]
-    weight = 1.0 / jnp.sum(weight, axis=1, keepdims=True)
-    total = jnp.zeros((rows, HEAD_SIZE), F32)
-    for i in range(2 * half):
-        p = (s_ref[i] * weight).astype(BF16)
-        if i < half:
-            vals = v1_ref[2 * i : 2 * i + 2].reshape(2 * LANES, HEAD_SIZE)
-        else:
-            a = 2 * (i - half)
-            first = mixed(a, vo_ref, v2_ref)
-            if i < 2 * half - 1:
-                vals = jnp.concatenate([first, mixed(a + 1, vo_ref, v2_ref)], 0)
+                a = 2 * (i - half)
+                first = mixed(a, ko_ref, k2_ref)
+                bias_a = jnp.where(a < j, 0.0, bias2)
+                if i < count - 1:
+                    bias_b = jnp.where(a + 1 < j, 0.0, bias2)
+                    s = dot(q, jnp.concatenate([first, mixed(a + 1, ko_ref, k2_ref)], 0), INNER)
+                    s = s + jnp.where(lane < LANES, bias_a, bias_b)
+                else:
+                    s = dot(q, jnp.concatenate([first, ko_ref[j]], 0), INNER)
+                    edge = dot(q, k2_ref[j], INNER) + bias2
+                    s = jnp.concatenate(
+                        [s[:, :LANES] + bias_a, jnp.where(causal, s[:, LANES:], edge)], 1
+                    )
+                key = "rest"
+            s_ref[i] = s
+            high = jnp.maximum(s[:, :LANES], s[:, LANES:])
+            held[key] = jnp.maximum(held[key], high) if key in held else high
+            if i == count - 1:
+                near = jnp.where(plane >= 1, held.pop("near"), -jnp.inf)
+                top = jnp.max(jnp.maximum(near, held.pop("rest")), axis=1, keepdims=True) * factor
+                held["top"] = top
+                held["top_near"] = jnp.where(plane >= 1, top, jnp.inf)
+
+        def weigh(i):
+            p = jnp.exp2(s_ref[i] * factor - held["top_near" if i < half else "top"])
+            s_ref[i] = p
+            both = p[:, :LANES] + p[:, LANES:]
+            held["sum"] = held["sum"] + both if "sum" in held else both
+            if i == count - 1:
+                held["inverse"] = 1.0 / jnp.sum(held.pop("sum"), axis=1, keepdims=True)
+
+        def mix(i):
+            p = (s_ref[i] * held["inverse"]).astype(BF16)
+            if i < half:
+                vals = v1_ref[2 * i : 2 * i + 2].reshape(2 * LANES, HEAD_SIZE)
             else:
-                last = p[:, LANES:]
-                zero = jnp.zeros_like(last)
-                far = jnp.where(causal, zero, last)
-                p = jnp.concatenate([p[:, :LANES], jnp.where(causal, last, zero)], 1)
-                vals = jnp.concatenate([first, vo_ref[j]], 0)
-                total += dot(far, v2_ref[j])
-        total += dot(p, vals)
-    x = total.astype(BF16)
-    x_ref[0] = x
-    heads = rows // LANES
-    part = jnp.zeros((LANES, 2 * NS), F32)
-    squares = jnp.zeros((LANES, LANES), F32)
-    for h in range(heads):
-        piece = x[h * LANES : (h + 1) * LANES]
-        part += dot(piece, bc_ref[pl.ds(h * LANES, LANES), :])
-        wide = piece.astype(F32)
-        squares += wide * wide
-    high = squares.astype(BF16)
-    low = (squares - high.astype(F32)).astype(BF16)
-    row_ones = jnp.ones((16, LANES), BF16)
-    row = dot(row_ones, high, INNER) + dot(row_ones, low, INNER)
-    part_ref[0, :LANES, :] = part
-    part_ref[0, LANES:, :LANES] = row[:8]
-    part_ref[0, LANES:, LANES:] = jnp.zeros_like(row[:8])
+                a = 2 * (i - half)
+                first = mixed(a, vo_ref, v2_ref)
+                if i < count - 1:
+                    vals = jnp.concatenate([first, mixed(a + 1, vo_ref, v2_ref)], 0)
+                else:
+                    last = p[:, LANES:]
+                    zero = jnp.zeros_like(last)
+                    far = jnp.where(causal, zero, last)
+                    p = jnp.concatenate([p[:, :LANES], jnp.where(causal, last, zero)], 1)
+                    vals = jnp.concatenate([first, vo_ref[j]], 0)
+                    held["total"] += dot(far, v2_ref[j])
+            new = dot(p, vals)
+            held["total"] = held["total"] + new if "total" in held else new
+            if i == count - 1:
+                x_ref[here, span, :] = held.pop("total").astype(BF16)
+
+        return score, weigh, mix
+
+    units = [unit(n) for n in range(steps * splits)]
+    for phase in range(len(units) + 2):
+        for i in range(count):
+            for stage in (2, 1, 0):
+                n = phase - stage
+                if 0 <= n < len(units):
+                    units[n][stage](i)
+    for here in range(steps):
+        part = jnp.zeros((LANES, 2 * NS), F32)
+        squares = jnp.zeros((LANES, LANES), F32)
+        for h in range(rows // LANES):
+            piece = x_ref[here, pl.ds(h * LANES, LANES), :]
+            part += dot(piece, bc_ref[pl.ds(h * LANES, LANES), :])
+            wide = piece.astype(F32)
+            squares += wide * wide
+        high = squares.astype(BF16)
+        low = (squares - high.astype(F32)).astype(BF16)
+        row_ones = jnp.ones((16, LANES), BF16)
+        row = dot(row_ones, high, INNER) + dot(row_ones, low, INNER)
+        part_ref[here, :LANES, :] = part
+        part_ref[here, LANES:, :LANES] = row[:8]
+        part_ref[here, LANES:, LANES:] = jnp.zeros_like(row[:8])
 
 
 def project_kernel(channels, part_ref, out_ref):
@@ -518,8 +542,8 @@
         proj_ref[LANES:, :] = split_rows(wide[:1], jnp.broadcast_to(inverse, wide.shape).T[:1])
 
 
-def params(**kw):
-    return pltpu.CompilerParams(vmem_limit_bytes=VMEM_BYTES, **kw)
+def params(mib=12):
+    return pltpu.CompilerParams(vmem_limit_bytes=mib * MIB)
 
 
 def cost(flops, nbytes, exps=0):
@@ -551,7 +575,8 @@
         name="pack_kv",
     )(rotated_keys, values)
     kv_own = lax.all_to_all(kv, "peer", 0, 0)
-    kv_one = moved(kv_own, 1)
+    with jax.named_scope("shift_near"):
+        kv_one = moved(kv_own, 1)
     kv_two = moved(kv_one, 1)
 
     packed = pl.pallas_call(
@@ -560,8 +585,10 @@
         compiler_params=params(),
         name="pack_queries",
     )(queries)
-    arrived = lax.all_to_all(packed, "peer", 0, 0)
-
+    with jax.named_scope("trade_queries"):
+        arrived = lax.all_to_all(packed, "peer", 0, 0)
+
+    arrived, gate_after = lax.optimization_barrier((arrived, gate_input))
     coded = jnp.stack([decay_codes >> 7, decay_codes & 127], 0).astype(BF16)
     coded = jnp.transpose(coded.reshape(2, tokens, peers, heads), (2, 0, 3, 1))
     coded = coded.reshape(peers, 2 * heads, tokens)
@@ -570,37 +597,43 @@
         out_shape=jax.ShapeDtypeStruct((peers, wide + 16, LANES), BF16),
         compiler_params=params(),
         name="pack_gates",
-    )(gate_input, coded)
-    side = lax.all_to_all(packed, "peer", 0, 0)
+    )(gate_after, coded)
+    with jax.named_scope("trade_gates"):
+        side = lax.all_to_all(packed, "peer", 0, 0)
 
     def keys_spec(which):
         return pl.BlockSpec((peers, tokens, HEAD_SIZE), lambda j, s: (0, which, 0))
 
-    def block(rows, which=0, lanes=LANES):
-        return pl.BlockSpec((1, rows, lanes), lambda j, s: (j, which, 0))
+    steps = 1
+
+    def block(rows, lanes=LANES):
+        return pl.BlockSpec((steps, rows, lanes), lambda j, s: (j, 0, 0))
 
     proj_rows = tokens + 16
-    attended, partial = pl.pallas_call(
-        attend_kernel,
-        grid_spec=pltpu.PrefetchScalarGridSpec(
-            num_scalar_prefetch=1,
-            grid=(peers,),
-            in_specs=[block(wide)]
-            + [keys_spec(0), keys_spec(1)] * 3
-            + [pl.BlockSpec((wide, 2 * NS), lambda j, s: (s[1], 0))],
-            out_specs=[block(wide), block(tokens + 8, 0, 2 * NS)],
-            scratch_shapes=[pltpu.VMEM((peers, wide, 2 * tokens), F32)],
-        ),
-        out_shape=[
-            jax.ShapeDtypeStruct((peers, wide, LANES), BF16),
-            jax.ShapeDtypeStruct((peers, tokens + 8, 2 * NS), F32),
-        ],
-        compiler_params=params(),
-        cost_estimate=cost(5 * 10**9, 4 * 10**6, 9 * 10**6),
-        name="attend",
-    )(place, arrived, kv_own, kv_own, kv_one, kv_one, kv_two, kv_two, bc_weight)
-
-    shares = lax.all_to_all(partial, "peer", 0, 0)
+    with jax.named_scope("attention"):
+        attended, partial = pl.pallas_call(
+            attend_kernel,
+            grid_spec=pltpu.PrefetchScalarGridSpec(
+                num_scalar_prefetch=1,
+                grid=(peers // steps,),
+                in_specs=[block(wide)]
+                + [keys_spec(0), keys_spec(1)] * 3
+                + [pl.BlockSpec((wide, 2 * NS), lambda j, s: (s[1], 0))],
+                out_specs=[block(wide), block(tokens + 8, 2 * NS)],
+                scratch_shapes=[pltpu.VMEM((peers, 2 * tokens, 2 * tokens), F32)] * 3,
+            ),
+            out_shape=[
+                jax.ShapeDtypeStruct((peers, wide, LANES), BF16),
+                jax.ShapeDtypeStruct((peers, tokens + 8, 2 * NS), F32),
+            ],
+            compiler_params=params(20),
+            cost_estimate=cost(5 * 10**9, 4 * 10**6, 9 * 10**6),
+            name="attend",
+        )(place, arrived, kv_own, kv_own, kv_one, kv_one, kv_two, kv_two, bc_weight)
+
+    partial, side = lax.optimization_barrier((partial, side))
+    with jax.named_scope("trade_partial"):
+        shares = lax.all_to_all(partial, "peer", 0, 0)
     proj = pl.pallas_call(
         functools.partial(project_kernel, channels),
         in_specs=[whole_block((peers, tokens + 8, 2 * NS))],

time: 221 us -> 214 us (0.968)
  blocking collectives: 59.9 us -> 36.2 us
  waiting for transfers between devices: 44.8 us -> 53.7 us
  local copies, waits for them, and re-layouts: 6.05 us -> 12.5 us
  starting transfers between devices: 44.5 us -> 49.4 us
  Pallas kernels: 63.5 us -> 59.7 us
    all_to_all x1 -> x0, blocking collectives: 14.8 us -> none  [head_sharded(): kv_own = lax.all_to_all(kv, 'peer', 0, 0)]
    all_gather x2, blocking collectives: 27.2 us -> 18.3 us  [head_sharded(): projected = lax.all_gather(proj, 'peer')]
    all_to_all x0 -> x1, waiting for transfers between devices: none -> 8.54 us  [head_sharded(): kv_own = lax.all_to_all(kv, 'peer', 0, 0)]
    unnamed x26 -> x38, local copies, waits for them, and re-layouts: 5.89 us -> 12.4 us
    all_to_all x0 -> x1, starting transfers between devices: none -> 5.2 us  [head_sharded(): kv_own = lax.all_to_all(kv, 'peer', 0, 0)]
    all_to_all x1, waiting for transfers between devices: 4.67 us -> 0.01 us  [head_sharded(): arrived = lax.all_to_all(packed, 'peer', 0, 0)]
    pallas_call x1, Pallas kernels: 25.4 us -> 20.8 us  [head_sharded(): pl.pallas_call(attend_kernel, grid_spec=pltpu.PrefetchScalarGridSpec(num_...]
    ppermute x8, waiting for transfers between devices: 9.95 us -> 13.9 us  [moved(): lax.ppermute(x, 'plane', [(i, i + distance) for i in range(planes - dista...]
  transfers between devices with their start and end apart: 12 -> 13, of which waited for: 5 -> 5; matrix products, arithmetic and copies ran while one was open for 0% -> 0% of each run, Pallas kernels for 8% -> 17%
where the time goes in v3:
time: 214 us; the launch traced here: 213 us
  Pallas kernels  59.7 us (28%)
  waiting for transfers between devices  53.7 us (25%)
  starting transfers between devices  49.4 us (23%)
  blocking collectives  36.2 us (17%)
  local copies, waits for them, and re-layouts  12.5 us (6%)
    ppermute x8, starting transfers between devices, moved(): lax.ppermute(x, 'plane', [(i, i + distance) for i in range(planes - dista...  29.4 us
    pallas_call x1, Pallas kernels, head_sharded(): pl.pallas_call(attend_kernel, grid_spec=pltpu.PrefetchScalarGridSpec(num_...  20.8 us
    all_gather x2, blocking collectives, head_sharded(): projected = lax.all_gather(proj, 'peer')  18.3 us
    all_to_all x1, blocking collectives, head_sharded(): lax.all_to_all(gated, 'peer', 0, 0)  17.9 us
    all_to_all x1, waiting for transfers between devices, head_sharded(): shares = lax.all_to_all(partial, 'peer', 0, 0)  16 us
    all_to_all x1, waiting for transfers between devices, head_sharded(): lax.all_to_all(gated, 'peer', 0, 0)  15.3 us
    ppermute x8, waiting for transfers between devices, moved(): lax.ppermute(x, 'plane', [(i, i + distance) for i in range(planes - dista...  13.9 us
    pallas_call x2, Pallas kernels, ssd(): pl.pallas_call(local_kernel, out_shape=[full_shape, full_shape], compiler...  13.3 us
  transfers between devices with their start and end apart: 13, of which 5 were waited for; matrix products, arithmetic and copies ran while one was open for 0% of the time, Pallas kernels for 17%

profile of v3, /device:TPU:0, one launch (start us, length us, event | category | flops | bytes accessed | tf_op | source)
XLA Modules:
  0.0 212.6 jit_solution(15050217055105445047)
XLA Ops:
  3.5 5.2 %all-to-all-start.1 = ((bf16[8,256,128]{2,1,0:T(8,128)(2,1)}), bf16[8,256,128]{2,1,0:T(8,128)(2,1)S(1)}, u32[]{:S(2)}, u32[]{:S(2)}) async-start(bf16[8,256,128]{2,1,0:T(8,128)(2,1)} %pack_kv.1), calls=%async_computation.1 | async-start | bytes 1048576 | tf_op jit(solution)/shard_map/all_to_all | solution.py:577
  9.9 8.5 %all-to-all-done.1.ko_ref.vo_ref = bf16[8,256,128]{2,1,0:T(8,128)(2,1)S(1)} async-done(((bf16[8,256,128]{2,1,0:T(8,128)(2,1)}), bf16[8,256,128]{2,1,0:T(8,128)(2,1)S(1)}, u32[]{:S(2)}, u32[]{:S(2)}) %all-to-all-start.1) | async-done | bytes 524320 | tf_op jit(solution)/shard_map/all_to_all | solution.py:577
  18.4 3.6 %all-to-all-start = ((bf16[8,512,128]{2,1,0:T(8,128)(2,1)}), bf16[8,512,128]{2,1,0:T(8,128)(2,1)S(1)}, u32[]{:S(2)}, u32[]{:S(2)}) async-start(bf16[8,512,128]{2,1,0:T(8,128)(2,1)} %pack_queries.1), calls=%async_computation | async-start | bytes 2097152 | tf_op jit(solution)/shard_map/trade_queries/all_to_all | solution.py:589
  22.0 4.3 %collective-permute-start = (bf16[8,256,128]{2,1,0:T(8,128)(2,1)S(1)}, bf16[8,256,128]{2,1,0:T(8,128)(2,1)}, u32[]{:S(2)}, u32[]{:S(2)}) collective-permute-start(bf16[8,256,128]{2,1,0:T(8,128)(2,1)S(1)} %all-to-all-done.1.ko_ref.vo_ref), channel_id=1, source_target_pairs={{0,8},{8,16},{16,24},{1,9},{9,17},{17,25},{2,10},{10,18},{18,26},{... | collective-permute-start | bytes 1572872 | tf_op jit(solution)/shard_map/shift_near/ppermute | solution.py:569
  26.3 10.9 %collective-permute-done.k1_ref.v1_ref = bf16[8,256,128]{2,1,0:T(8,128)(2,1)} collective-permute-done((bf16[8,256,128]{2,1,0:T(8,128)(2,1)S(1)}, bf16[8,256,128]{2,1,0:T(8,128)(2,1)}, u32[]{:S(2)}, u32[]{:S(2)}) %collective-permute-start) | collective-permute-done | bytes 524320 | tf_op jit(solution)/shard_map/shift_near/ppermute | solution.py:569
  37.2 5.3 %collective-permute-start.1 = (bf16[8,256,128]{2,1,0:T(8,128)(2,1)}, bf16[8,256,128]{2,1,0:T(8,128)(2,1)}, u32[]{:S(2)}, u32[]{:S(2)}) collective-permute-start(bf16[8,256,128]{2,1,0:T(8,128)(2,1)} %collective-permute-done.k1_ref.v1_ref), channel_id=1, source_target_pairs={{0,8},{8,16},{16,24},{1,9},{9,17},{17,25},{2,10},{10,18},{18,26},{... | collective-permute-start | bytes 1572872 | tf_op jit(solution)/shard_map/ppermute | solution.py:569
  45.9 3.8 %all-to-all-start.2 = ((bf16[8,528,128]{2,1,0:T(8,128)(2,1)}), bf16[8,528,128]{2,1,0:T(8,128)(2,1)S(1)}, u32[]{:S(2)}, u32[]{:S(2)}) async-start(bf16[8,528,128]{2,1,0:T(8,128)(2,1)} %pack_gates.1), calls=%async_computation.2 | async-start | bytes 2162688 | tf_op jit(solution)/shard_map/trade_gates/all_to_all | solution.py:602
  49.9 3.0 %collective-permute-done.1.k2_ref.v2_ref = bf16[8,256,128]{2,1,0:T(8,128)(2,1)} collective-permute-done((bf16[8,256,128]{2,1,0:T(8,128)(2,1)}, bf16[8,256,128]{2,1,0:T(8,128)(2,1)}, u32[]{:S(2)}, u32[]{:S(2)}) %collective-permute-start.1) | collective-permute-done | bytes 524320 | tf_op jit(solution)/shard_map/ppermute | solution.py:569
  55.1 20.8 %attend.1 = (bf16[8,512,128]{2,1,0:T(8,128)(2,1)S(1)}, f32[8,136,256]{2,1,0:T(8,128)S(1)}) custom-call(s32[2]{0:T(128)S(1)} %pad_add_fusion.place_ref, bf16[8,512,128]{2,1,0:T(8,128)(2,1)S(1)} %copy-done.8, bf16[8,256,128]{2,1,0:T(8,128)(2,1)S(1)} %copy-done.10, bf16[8,256,128]{2,1,0:T(8,128)(2,1)S(1)} %copy-done.10, ...), custom_call_target="tpu_custom_call" | custom-call | flops 5000000000 | bytes 4000000 | tf_op jit(solution)/shard_map/attention/attend/pallas_call | solution.py:614
  78.0 3.7 %all-to-all-start.3 = ((f32[8,136,256]{2,1,0:T(8,128)}), f32[8,136,256]{2,1,0:T(8,128)S(1)}, u32[]{:S(2)}, u32[]{:S(2)}) async-start(f32[8,136,256]{2,1,0:T(8,128)} %copy-done.4), calls=%async_computation.3 | async-start | bytes 2228224 | tf_op jit(solution)/shard_map/trade_partial/all_to_all | solution.py:636
  81.8 16.0 %all-to-all-done.3.part_ref = f32[8,136,256]{2,1,0:T(8,128)S(1)} async-done(((f32[8,136,256]{2,1,0:T(8,128)}), f32[8,136,256]{2,1,0:T(8,128)S(1)}, u32[]{:S(2)}, u32[]{:S(2)}) %all-to-all-start.3) | async-done | bytes 1114144 | tf_op jit(solution)/shard_map/trade_partial/all_to_all | solution.py:636
  98.7 2.0 project.1
  100.8 9.3 %all-gather = bf16[1152,256]{1,0:T(8,128)(2,1)S(1)} all-gather(bf16[144,256]{1,0:T(8,128)(2,1)} %project.1), channel_id=2, replica_groups=mesh['plane'=4,'peer'=8,'tp'=1] {'peer'}, dimensions={0}, use_global_device_ids=true | all-gather | bytes 663552 | tf_op jit(solution)/shard_map/all_gather | solution.py:681
  110.2 3.8 %states.2 = (bf16[8,512,128]{2,1,0:T(8,128)(2,1)S(1)}, f32[8,512,128]{2,1,0:T(8,128)S(1)}, bf16[528,128]{1,0:T(8,128)(2,1)S(1)}) custom-call(bf16[8,512,128]{2,1,0:T(8,128)(2,1)S(1)} %copy-done.15, bf16[8,144,256]{2,1,0:T(8,128)(2,1)S(1)} %bitcast.23, bf16[8,528,128]{2,1,0:T(8,128)(2,1)S(1)} %all-to-all-done.2.side_ref, f32[8,128]{1,0:T(8,128)S(1)} %broadcast_in_dim.2.rates_ref), custom_call_target="tpu_custom_call" | custom-call | flops 1000000000 | bytes 4000000 | tf_op jit(solution)/shard_map/states/pallas_call | solution.py:653
  113.9 4.4 %collective-permute-start.2 = (bf16[528,128]{1,0:T(8,128)(2,1)S(1)}, bf16[528,128]{1,0:T(8,128)(2,1)S(1)}, u32[]{:S(2)}, u32[]{:S(2)}) collective-permute-start(bf16[528,128]{1,0:T(8,128)(2,1)S(1)} %get-tuple-element.32), channel_id=1, source_target_pairs={{0,8},{8,16},{16,24},{1,9},{9,17},{17,25},{2,10},{10,18},{18,26},{... | collective-permute-start | bytes 405512 | tf_op jit(solution)/shard_map/ppermute | solution.py:569
  118.3 4.5 %collective-permute-start.3 = (bf16[528,128]{1,0:T(8,128)(2,1)S(1)}, bf16[528,128]{1,0:T(8,128)(2,1)S(1)}, u32[]{:S(2)}, u32[]{:S(2)}) collective-permute-start(bf16[528,128]{1,0:T(8,128)(2,1)S(1)} %get-tuple-element.32), channel_id=1, source_target_pairs={{0,16},{8,24},{1,17},{9,25},{2,18},{10,26},{3,19},{11,27},{4,20},{... | collective-permute-start | bytes 405512 | tf_op jit(solution)/shard_map/ppermute | solution.py:569
  122.8 1.3 collective-permute-start.4
  124.2 6.7 %local.2 = (f32[8,512,128]{2,1,0:T(8,128)S(1)}, f32[8,512,128]{2,1,0:T(8,128)S(1)}) custom-call(bf16[8,512,128]{2,1,0:T(8,128)(2,1)S(1)} %get-tuple-element.28.x_ref, bf16[8,144,256]{2,1,0:T(8,128)(2,1)S(1)} %bitcast.24, bf16[8,528,128]{2,1,0:T(8,128)(2,1)S(1)} %all-to-all-done.2.side_ref, f32[8,128]{1,0:T(8,128)S(1)} %broadcast_in_dim.2.rates_ref, ...), custom_call_target="tpu_custom_call" | custom-call | flops 2000000000 | bytes 5000000 | tf_op jit(solution)/shard_map/local/pallas_call | solution.py:662
  130.9 5.1 %gated.2 = (bf16[8,512,128]{2,1,0:T(8,128)(2,1)}, f32[8,512,128]{2,1,0:T(8,128)S(1)}) custom-call(f32[8,512,128]{2,1,0:T(8,128)S(1)} %get-tuple-element.30.y_ref, f32[8,512,128]{2,1,0:T(8,128)S(1)} %get-tuple-element.31.silu_ref, bf16[8,144,256]{2,1,0:T(8,128)(2,1)S(1)} %bitcast.25, bf16[8,528,128]{2,1,0:T(8,128)(2,1)S(1)} %all-to-all-done.2.side_ref, ...), custom_call_target="tpu_custom_call" | custom-call | flops 1000000000 | bytes 5000000 | tf_op jit(solution)/shard_map/gated/pallas_call | solution.py:669
  135.9 1.3 copy-done.2
  137.2 3.7 %all-to-all-start.4 = ((bf16[8,512,128]{2,1,0:T(8,128)(2,1)}), bf16[8,512,128]{2,1,0:T(8,128)(2,1)S(1)}, u32[]{:S(2)}, u32[]{:S(2)}) async-start(bf16[8,512,128]{2,1,0:T(8,128)(2,1)} %get-tuple-element.33), calls=%async_computation.4 | async-start | bytes 2097152 | tf_op jit(solution)/shard_map/all_to_all | solution.py:697
  141.0 15.3 %all-to-all-done.4.g_ref = bf16[8,512,128]{2,1,0:T(8,128)(2,1)S(1)} async-done(((bf16[8,512,128]{2,1,0:T(8,128)(2,1)}), bf16[8,512,128]{2,1,0:T(8,128)(2,1)S(1)}, u32[]{:S(2)}, u32[]{:S(2)}) %all-to-all-start.4) | async-done | bytes 1048608 | tf_op jit(solution)/shard_map/all_to_all | solution.py:697
  156.2 1.6 copy-done.1
  157.8 1.9 finish_first.1
  159.7 9.0 %all-gather.1 = bf16[1152,256]{1,0:T(8,128)(2,1)S(1)} all-gather(bf16[144,256]{1,0:T(8,128)(2,1)S(1)} %get-tuple-element.36), channel_id=3, replica_groups=mesh['plane'=4,'peer'=8,'tp'=1] {'peer'}, dimensions={0}, use_global_device_ids=true | all-gather | bytes 663552 | tf_op jit(solution)/shard_map/all_gather | solution.py:698
  168.7 3.8 %states.3 = (bf16[8,512,128]{2,1,0:T(8,128)(2,1)S(1)}, f32[8,512,128]{2,1,0:T(8,128)S(1)}, bf16[528,128]{1,0:T(8,128)(2,1)S(1)}) custom-call(f32[8,512,128]{2,1,0:T(8,128)S(1)} %copy-done.3, bf16[8,144,256]{2,1,0:T(8,128)(2,1)S(1)} %bitcast.20, bf16[8,528,128]{2,1,0:T(8,128)(2,1)S(1)} %all-to-all-done.2.side_ref, f32[8,128]{1,0:T(8,128)S(1)} %broadcast_in_dim.2.rates_ref, ...), custom_call_target="tpu_custom_call" | custom-call | flops 1000000000 | bytes 4000000 | tf_op jit(solution)/shard_map/states/pallas_call | solution.py:653
  172.5 3.0 %collective-permute-start.5 = (bf16[528,128]{1,0:T(8,128)(2,1)S(1)}, bf16[528,128]{1,0:T(8,128)(2,1)S(1)}, u32[]{:S(2)}, u32[]{:S(2)}) collective-permute-start(bf16[528,128]{1,0:T(8,128)(2,1)S(1)} %get-tuple-element.41), channel_id=1, source_target_pairs={{0,8},{8,16},{16,24},{1,9},{9,17},{17,25},{2,10},{10,18},{18,26},{... | collective-permute-start | bytes 405512 | tf_op jit(solution)/shard_map/ppermute | solution.py:569
  175.5 5.3 %collective-permute-start.6 = (bf16[528,128]{1,0:T(8,128)(2,1)S(1)}, bf16[528,128]{1,0:T(8,128)(2,1)S(1)}, u32[]{:S(2)}, u32[]{:S(2)}) collective-permute-start(bf16[528,128]{1,0:T(8,128)(2,1)S(1)} %get-tuple-element.41), channel_id=1, source_target_pairs={{0,16},{8,24},{1,17},{9,25},{2,18},{10,26},{3,19},{11,27},{4,20},{... | collective-permute-start | bytes 405512 | tf_op jit(solution)/shard_map/ppermute | solution.py:569
  182.2 6.7 %local.3 = (f32[8,512,128]{2,1,0:T(8,128)S(1)}, f32[8,512,128]{2,1,0:T(8,128)S(1)}) custom-call(bf16[8,512,128]{2,1,0:T(8,128)(2,1)S(1)} %get-tuple-element.37.x_ref, bf16[8,144,256]{2,1,0:T(8,128)(2,1)S(1)} %bitcast.21, bf16[8,528,128]{2,1,0:T(8,128)(2,1)S(1)} %all-to-all-done.2.side_ref, f32[8,128]{1,0:T(8,128)S(1)} %broadcast_in_dim.2.rates_ref, ...), custom_call_target="tpu_custom_call" | custom-call | flops 2000000000 | bytes 5000000 | tf_op jit(solution)/shard_map/local/pallas_call | solution.py:662
  188.9 4.1 %gated.3 = bf16[8,512,128]{2,1,0:T(8,128)(2,1)S(1)} custom-call(f32[8,512,128]{2,1,0:T(8,128)S(1)} %get-tuple-element.39.y_ref, f32[8,512,128]{2,1,0:T(8,128)S(1)} %get-tuple-element.40.silu_ref, bf16[8,144,256]{2,1,0:T(8,128)(2,1)S(1)} %bitcast.22, bf16[8,528,128]{2,1,0:T(8,128)(2,1)S(1)} %all-to-all-done.2.side_ref, ...), custom_call_target="tpu_custom_call" | custom-call | flops 1000000000 | bytes 5000000 | tf_op jit(solution)/shard_map/gated/pallas_call | solution.py:669
  193.0 17.9 %all_to_all.30.g_ref = bf16[8,512,128]{2,1,0:T(8,128)(2,1)S(1)} all-to-all(bf16[8,512,128]{2,1,0:T(8,128)(2,1)S(1)} %gated.3), channel_id=1, replica_groups=mesh['plane'=4,'peer'=8,'tp'=1] {'peer'}, dimensions={0} | all-to-all | bytes 2097152 | tf_op jit(solution)/shard_map/all_to_all | solution.py:707
  210.8 1.7 finish_second.1
  (54 shorter events, 14.3 us)
Async XLA Ops:
  0.6 8.1 %copy-start.5 = (bf16[128,4096]{1,0:T(8,128)(2,1)S(1)}, bf16[128,4096]{1,0:T(8,128)(2,1)}, u32[]{:S(2)}) copy-start(bf16[128,4096]{1,0:T(8,128)(2,1)} %x_ref.1) | copy-start | bytes 3145732
  0.6 1.0 copy-start.11
  1.7 0.9 copy-start.12
  3.5 14.9 %all-to-all-start.1 = ((bf16[8,256,128]{2,1,0:T(8,128)(2,1)}), bf16[8,256,128]{2,1,0:T(8,128)(2,1)S(1)}, u32[]{:S(2)}, u32[]{:S(2)}) async-start(bf16[8,256,128]{2,1,0:T(8,128)(2,1)} %pack_kv.1), calls=%async_computation.1 | async-start | bytes 1048576 | tf_op jit(solution)/shard_map/all_to_all | solution.py:577
  8.7 17.6 %copy-start.17 = (s32[128,64]{0,1:T(8,128)S(1)}, s32[128,64]{0,1:T(8,128)}, u32[]{:S(2)}) copy-start(s32[128,64]{0,1:T(8,128)} %param.12) | copy-start | bytes 98308
  18.4 24.1 %copy-start.9 = (bf16[8,256,128]{2,1,0:T(8,128)(2,1)}, bf16[8,256,128]{2,1,0:T(8,128)(2,1)S(1)}, u32[]{:S(2)}) copy-start(bf16[8,256,128]{2,1,0:T(8,128)(2,1)S(1)} %all-to-all-done.1.ko_ref.vo_ref) | copy-start | bytes 1572868
  18.4 24.1 %all-to-all-start = ((bf16[8,512,128]{2,1,0:T(8,128)(2,1)}), bf16[8,512,128]{2,1,0:T(8,128)(2,1)S(1)}, u32[]{:S(2)}, u32[]{:S(2)}) async-start(bf16[8,512,128]{2,1,0:T(8,128)(2,1)} %pack_queries.1), calls=%async_computation | async-start | bytes 2097152 | tf_op jit(solution)/shard_map/trade_queries/all_to_all | solution.py:589
  22.0 15.2 %collective-permute-start = (bf16[8,256,128]{2,1,0:T(8,128)(2,1)S(1)}, bf16[8,256,128]{2,1,0:T(8,128)(2,1)}, u32[]{:S(2)}, u32[]{:S(2)}) collective-permute-start(bf16[8,256,128]{2,1,0:T(8,128)(2,1)S(1)} %all-to-all-done.1.ko_ref.vo_ref), channel_id=1, source_target_pairs={{0,8},{8,16},{16,24},{1,9},{9,17},{17,25},{2,10},{10,18},{18,26},{... | collective-permute-start | bytes 1572872 | tf_op jit(solution)/shard_map/shift_near/ppermute | solution.py:569
  37.2 15.7 %collective-permute-start.1 = (bf16[8,256,128]{2,1,0:T(8,128)(2,1)}, bf16[8,256,128]{2,1,0:T(8,128)(2,1)}, u32[]{:S(2)}, u32[]{:S(2)}) collective-permute-start(bf16[8,256,128]{2,1,0:T(8,128)(2,1)} %collective-permute-done.k1_ref.v1_ref), channel_id=1, source_target_pairs={{0,8},{8,16},{16,24},{1,9},{9,17},{17,25},{2,10},{10,18},{18,26},{... | collective-permute-start | bytes 1572872 | tf_op jit(solution)/shard_map/ppermute | solution.py:569
  42.5 10.4 %copy-start = (bf16[4096,256]{1,0:T(8,128)(2,1)S(1)}, bf16[4096,256]{1,0:T(8,128)(2,1)}, u32[]{:S(2)}) copy-start(bf16[4096,256]{1,0:T(8,128)(2,1)} %rest_0_.1) | copy-start | bytes 6291460
  42.5 1.0 copy-start.7
  43.5 1.3 copy-start.6
  45.9 32.0 %all-to-all-start.2 = ((bf16[8,528,128]{2,1,0:T(8,128)(2,1)}), bf16[8,528,128]{2,1,0:T(8,128)(2,1)S(1)}, u32[]{:S(2)}, u32[]{:S(2)}) async-start(bf16[8,528,128]{2,1,0:T(8,128)(2,1)} %pack_gates.1), calls=%async_computation.2 | async-start | bytes 2162688 | tf_op jit(solution)/shard_map/trade_gates/all_to_all | solution.py:602
  52.9 1.2 copy-start.8
  54.1 1.0 copy-start.10
  76.0 1.0 copy-start.4
  77.0 1.0 copy-start.14
  78.0 3.7 %copy-start.18 = (f32[64]{0:T(128)S(1)}, f32[64]{0:T(128)}, u32[]{:S(2)}) copy-start(f32[64]{0:T(128)} %param.11) | copy-start | bytes 772
  78.0 32.2 %copy-start.15 = (bf16[8,512,128]{2,1,0:T(8,128)(2,1)S(1)}, bf16[8,512,128]{2,1,0:T(8,128)(2,1)}, u32[]{:S(2)}) copy-start(bf16[8,512,128]{2,1,0:T(8,128)(2,1)} %copy-done.14) | copy-start | bytes 3145732
  78.0 19.8 %all-to-all-start.3 = ((f32[8,136,256]{2,1,0:T(8,128)}), f32[8,136,256]{2,1,0:T(8,128)S(1)}, u32[]{:S(2)}, u32[]{:S(2)}) async-start(f32[8,136,256]{2,1,0:T(8,128)} %copy-done.4), calls=%async_computation.3 | async-start | bytes 2228224 | tf_op jit(solution)/shard_map/trade_partial/all_to_all | solution.py:636
  97.8 1.0 copy-start.16
  113.9 16.9 %collective-permute-start.2 = (bf16[528,128]{1,0:T(8,128)(2,1)S(1)}, bf16[528,128]{1,0:T(8,128)(2,1)S(1)}, u32[]{:S(2)}, u32[]{:S(2)}) collective-permute-start(bf16[528,128]{1,0:T(8,128)(2,1)S(1)} %get-tuple-element.32), channel_id=1, source_target_pairs={{0,8},{8,16},{16,24},{1,9},{9,17},{17,25},{2,10},{10,18},{18,26},{... | collective-permute-start | bytes 405512 | tf_op jit(solution)/shard_map/ppermute | solution.py:569
  118.3 12.5 %collective-permute-start.3 = (bf16[528,128]{1,0:T(8,128)(2,1)S(1)}, bf16[528,128]{1,0:T(8,128)(2,1)S(1)}, u32[]{:S(2)}, u32[]{:S(2)}) collective-permute-start(bf16[528,128]{1,0:T(8,128)(2,1)S(1)} %get-tuple-element.32), channel_id=1, source_target_pairs={{0,16},{8,24},{1,17},{9,25},{2,18},{10,26},{3,19},{11,27},{4,20},{... | collective-permute-start | bytes 405512 | tf_op jit(solution)/shard_map/ppermute | solution.py:569
  122.8 8.0 %collective-permute-start.4 = (bf16[528,128]{1,0:T(8,128)(2,1)S(1)}, bf16[528,128]{1,0:T(8,128)(2,1)S(1)}, u32[]{:S(2)}, u32[]{:S(2)}) collective-permute-start(bf16[528,128]{1,0:T(8,128)(2,1)S(1)} %get-tuple-element.32), channel_id=1, source_target_pairs={{0,24},{1,25},{2,26},{3,27},{4,28},{5,29},{6,30},{7,31}} | collective-permute-start | bytes 405512 | tf_op jit(solution)/shard_map/ppermute | solution.py:569
  135.9 1.3 copy-start.2
  137.2 3.7 %copy-start.13 = (f32[4096]{0:T(1024)S(1)}, f32[4096]{0:T(1024)}, u32[]{:S(2)}) copy-start(f32[4096]{0:T(1024)} %param.14) | copy-start | bytes 49156
  137.2 19.0 %all-to-all-start.4 = ((bf16[8,512,128]{2,1,0:T(8,128)(2,1)}), bf16[8,512,128]{2,1,0:T(8,128)(2,1)S(1)}, u32[]{:S(2)}, u32[]{:S(2)}) async-start(bf16[8,512,128]{2,1,0:T(8,128)(2,1)} %get-tuple-element.33), calls=%async_computation.4 | async-start | bytes 2097152 | tf_op jit(solution)/shard_map/all_to_all | solution.py:697
  156.2 1.6 copy-start.1
  157.8 10.9 %copy-start.3 = (f32[8,512,128]{2,1,0:T(8,128)S(1)}, f32[8,512,128]{2,1,0:T(8,128)}, u32[]{:S(2)}) copy-start(f32[8,512,128]{2,1,0:T(8,128)} %copy-done.2) | copy-start | bytes 6291460
  172.5 16.3 %collective-permute-start.5 = (bf16[528,128]{1,0:T(8,128)(2,1)S(1)}, bf16[528,128]{1,0:T(8,128)(2,1)S(1)}, u32[]{:S(2)}, u32[]{:S(2)}) collective-permute-start(bf16[528,128]{1,0:T(8,128)(2,1)S(1)} %get-tuple-element.41), channel_id=1, source_target_pairs={{0,8},{8,16},{16,24},{1,9},{9,17},{17,25},{2,10},{10,18},{18,26},{... | collective-permute-start | bytes 405512 | tf_op jit(solution)/shard_map/ppermute | solution.py:569
  175.5 13.3 %collective-permute-start.6 = (bf16[528,128]{1,0:T(8,128)(2,1)S(1)}, bf16[528,128]{1,0:T(8,128)(2,1)S(1)}, u32[]{:S(2)}, u32[]{:S(2)}) collective-permute-start(bf16[528,128]{1,0:T(8,128)(2,1)S(1)} %get-tuple-element.41), channel_id=1, source_target_pairs={{0,16},{8,24},{1,17},{9,25},{2,18},{10,26},{3,19},{11,27},{4,20},{... | collective-permute-start | bytes 405512 | tf_op jit(solution)/shard_map/ppermute | solution.py:569
  180.8 8.0 %collective-permute-start.7 = (bf16[528,128]{1,0:T(8,128)(2,1)S(1)}, bf16[528,128]{1,0:T(8,128)(2,1)S(1)}, u32[]{:S(2)}, u32[]{:S(2)}) collective-permute-start(bf16[528,128]{1,0:T(8,128)(2,1)S(1)} %get-tuple-element.41), channel_id=1, source_target_pairs={{0,24},{1,25},{2,26},{3,27},{4,28},{5,29},{6,30},{7,31}} | collective-permute-start | bytes 405512 | tf_op jit(solution)/shard_map/ppermute | solution.py:569

commit v4 on v3

--- a/solution.py
+++ b/solution.py
@@ -56,7 +56,7 @@
     paired = jnp.stack([rotated_keys, values], 0)
     moving = paired
     arrived = []
-    for counter in range(reach):
+    for _ in range(reach):
         moving = shifted(moving, "seq", 1)
         arrived.append(moving)
     kv_blocks = arrived[::-1]
@@ -157,7 +157,7 @@
     carried_state = jnp.zeros((head_count, NS, SP), jnp.float32)
     carried_state = stretch_decay[0][:, None, None] * carried_state + contrib[0]
     carried_decay = carried_decay * stretch_decay[0]
-    unused_decay, entering = prefix(
+    _, entering = prefix(
         (carried_decay, carried_state),
         "seq",
         combine_states,
@@ -240,8 +240,24 @@
         for h in range(heads):
             cols = pl.ds((p * heads + h) * LANES, LANES)
             out_ref[p, pl.ds(h * LANES, LANES), :] = x_ref[:, cols]
-        if len(rest) == 2:
+        if len(rest) == 3:
             out_ref[p, pl.ds(heads * LANES, 16), :] = rest[0][p]
+
+
+def same_kernel(x_ref, after_ref, out_ref):
+    pass
+
+
+def after(x, earlier):
+    anywhere = pl.BlockSpec(memory_space=pl.ANY)
+    return pl.pallas_call(
+        same_kernel,
+        in_specs=[anywhere, pl.BlockSpec(memory_space=pltpu.VMEM)],
+        out_specs=anywhere,
+        out_shape=jax.ShapeDtypeStruct(x.shape, x.dtype),
+        input_output_aliases={0: 0},
+        name="after",
+    )(x, earlier)
 
 
 def attend_kernel(
@@ -511,7 +527,9 @@
 
 def finish_kernel(channels, with_proj, g_ref, gain_ref, *rest):
     if with_proj:
-        bc_ref, out_ref, proj_ref = rest
+        bc_hbm, out_ref, proj_ref, bc_ref, bc_sem = rest
+        fetch = pltpu.make_async_copy(bc_hbm, bc_ref, bc_sem)
+        fetch.start()
     else:
         (out_ref,) = rest
     parts, wide = g_ref.shape[0], g_ref.shape[1] // LANES
@@ -521,6 +539,8 @@
             g = g_ref[p, i * LANES : (i + 1) * LANES, :].astype(F32)
             squares += g * g
     inverse = 1.0 / jnp.sqrt(jnp.sum(squares, 1, keepdims=True) / channels + EPSILON)
+    if with_proj:
+        fetch.wait()
     scaled = jnp.zeros((LANES, LANES), F32)
     proj = jnp.zeros((LANES, 2 * NS), F32)
     for p in range(parts):
@@ -558,6 +578,7 @@
     planes, queries, rotated_keys, values, decay_rates, decay_codes, gate_input, norm_gain, bc_weight
 ):
     tokens, channels = queries.shape
+    bc_weight = pltpu.with_memory_space_constraint(bc_weight, pltpu.HBM)
     peers = lax.axis_size("peer")
     wide = channels // peers
     pairs = wide // LANES
@@ -575,20 +596,19 @@
         name="pack_kv",
     )(rotated_keys, values)
     kv_own = lax.all_to_all(kv, "peer", 0, 0)
-    with jax.named_scope("shift_near"):
-        kv_one = moved(kv_own, 1)
+    kv_one = moved(kv_own, 1)
     kv_two = moved(kv_one, 1)
 
     packed = pl.pallas_call(
         pack_heads_kernel,
         out_shape=jax.ShapeDtypeStruct((peers, wide, LANES), BF16),
         compiler_params=params(),
+        in_specs=[pl.BlockSpec(memory_space=pltpu.VMEM), pl.BlockSpec(memory_space=pl.ANY)],
+        cost_estimate=cost(2 * 10**10, 2 * 10**6),
         name="pack_queries",
-    )(queries)
-    with jax.named_scope("trade_queries"):
-        arrived = lax.all_to_all(packed, "peer", 0, 0)
-
-    arrived, gate_after = lax.optimization_barrier((arrived, gate_input))
+    )(queries, kv_own)
+    arrived = lax.all_to_all(packed, "peer", 0, 0)
+
     coded = jnp.stack([decay_codes >> 7, decay_codes & 127], 0).astype(BF16)
     coded = jnp.transpose(coded.reshape(2, tokens, peers, heads), (2, 0, 3, 1))
     coded = coded.reshape(peers, 2 * heads, tokens)
@@ -596,10 +616,10 @@
         pack_heads_kernel,
         out_shape=jax.ShapeDtypeStruct((peers, wide + 16, LANES), BF16),
         compiler_params=params(),
+        in_specs=[pl.BlockSpec(memory_space=pltpu.VMEM)] * 2 + [pl.BlockSpec(memory_space=pl.ANY)],
         name="pack_gates",
-    )(gate_after, coded)
-    with jax.named_scope("trade_gates"):
-        side = lax.all_to_all(packed, "peer", 0, 0)
+    )(gate_input, coded, arrived)
+    side = lax.all_to_all(packed, "peer", 0, 0)
 
     def keys_spec(which):
         return pl.BlockSpec((peers, tokens, HEAD_SIZE), lambda j, s: (0, which, 0))
@@ -610,30 +630,28 @@
         return pl.BlockSpec((steps, rows, lanes), lambda j, s: (j, 0, 0))
 
     proj_rows = tokens + 16
-    with jax.named_scope("attention"):
-        attended, partial = pl.pallas_call(
-            attend_kernel,
-            grid_spec=pltpu.PrefetchScalarGridSpec(
-                num_scalar_prefetch=1,
-                grid=(peers // steps,),
-                in_specs=[block(wide)]
-                + [keys_spec(0), keys_spec(1)] * 3
-                + [pl.BlockSpec((wide, 2 * NS), lambda j, s: (s[1], 0))],
-                out_specs=[block(wide), block(tokens + 8, 2 * NS)],
-                scratch_shapes=[pltpu.VMEM((peers, 2 * tokens, 2 * tokens), F32)] * 3,
-            ),
-            out_shape=[
-                jax.ShapeDtypeStruct((peers, wide, LANES), BF16),
-                jax.ShapeDtypeStruct((peers, tokens + 8, 2 * NS), F32),
-            ],
-            compiler_params=params(20),
-            cost_estimate=cost(5 * 10**9, 4 * 10**6, 9 * 10**6),
-            name="attend",
-        )(place, arrived, kv_own, kv_own, kv_one, kv_one, kv_two, kv_two, bc_weight)
-
-    partial, side = lax.optimization_barrier((partial, side))
-    with jax.named_scope("trade_partial"):
-        shares = lax.all_to_all(partial, "peer", 0, 0)
+    attended, partial = pl.pallas_call(
+        attend_kernel,
+        grid_spec=pltpu.PrefetchScalarGridSpec(
+            num_scalar_prefetch=1,
+            grid=(peers // steps,),
+            in_specs=[block(wide)]
+            + [keys_spec(0), keys_spec(1)] * 3
+            + [pl.BlockSpec((wide, 2 * NS), lambda j, s: (s[1], 0))],
+            out_specs=[block(wide), block(tokens + 8, 2 * NS)],
+            scratch_shapes=[pltpu.VMEM((peers, 2 * tokens, 2 * tokens), F32)] * 3,
+        ),
+        out_shape=[
+            pltpu.HBM((peers, wide, LANES), BF16),
+            pltpu.HBM((peers, tokens + 8, 2 * NS), F32),
+        ],
+        compiler_params=params(20),
+        cost_estimate=cost(5 * 10**9, 4 * 10**6, 9 * 10**6),
+        name="attend",
+    )(place, arrived, kv_own, kv_own, kv_one, kv_one, kv_two, kv_two, bc_weight)
+
+    partial = after(partial, side[:1, :16])
+    shares = lax.all_to_all(partial, "peer", 0, 0)
     proj = pl.pallas_call(
         functools.partial(project_kernel, channels),
         in_specs=[whole_block((peers, tokens + 8, 2 * NS))],
@@ -668,7 +686,7 @@
         )(normed, projected, side, rates, entering)
         return pl.pallas_call(
             functools.partial(gated_kernel, planes, not with_gain),
-            out_shape=[half_shape] if with_gain else [half_shape, full_shape],
+            out_shape=[half_shape] if with_gain else [half_shape, pltpu.HBM(full_shape.shape, F32)],
             scratch_shapes=[pltpu.VMEM((heads, LANES), F32), pltpu.VMEM((wide, LANES), F32)],
             compiler_params=params(),
             cost_estimate=cost(10**9, 5 * 10**6, 10**6),
@@ -685,13 +703,14 @@
         in_specs=[
             whole_block(gathered),
             whole_block(gain_rows.shape),
-            whole_block((channels, 2 * NS)),
+            pl.BlockSpec(memory_space=pltpu.HBM),
         ],
         out_specs=[whole_block((tokens, channels)), whole_block((proj_rows, 2 * NS))],
         out_shape=[
             jax.ShapeDtypeStruct((tokens, channels), F32),
             jax.ShapeDtypeStruct((proj_rows, 2 * NS), BF16),
         ],
+        scratch_shapes=[pltpu.VMEM((channels, 2 * NS), BF16), pltpu.SemaphoreType.DMA],
         compiler_params=params(),
         name="finish_first",
     )(lax.all_to_all(gated, "peer", 0, 0), gain_rows, bc_weight)
@@ -728,12 +747,13 @@
         else:
             inner, line, body = mesh, "seq", on_device
         split = P(line, "tp")
-        return jax.shard_map(
+        run = jax.shard_map(
             body,
             mesh=inner,
             in_specs=(split, split, split, P("tp"), split, split, P("tp"), P("tp", None)),
             out_specs=(split, split),
             check_vma=False,
-        )(*args)
+        )
+        return run(*args)
 
     return call

time: 214 us -> 210 us (0.981)
  blocking collectives: 36.2 us -> 51.1 us
  local copies, waits for them, and re-layouts: 12.5 us -> 2.67 us
  waiting for transfers between devices: 53.7 us -> 47.9 us
  starting transfers between devices: 49.4 us -> 44.2 us
  Pallas kernels: 59.7 us -> 62.8 us
    all_to_all x0 -> x1, blocking collectives: none -> 14.8 us  [head_sharded(): kv_own = lax.all_to_all(kv, 'peer', 0, 0)]
    unnamed x38 -> x18, local copies, waits for them, and re-layouts: 12.4 us -> 1.92 us
    all_to_all x1 -> x0, waiting for transfers between devices: 8.54 us -> none  [head_sharded(): kv_own = lax.all_to_all(kv, 'peer', 0, 0)]
    all_to_all x1 -> x0, starting transfers between devices: 5.2 us -> none  [head_sharded(): kv_own = lax.all_to_all(kv, 'peer', 0, 0)]
    ppermute x8, waiting for transfers between devices: 13.9 us -> 16.6 us  [moved(): lax.ppermute(x, 'plane', [(i, i + distance) for i in range(planes - dista...]
  transfers between devices with their start and end apart: 13 -> 12, of which waited for: 5 -> 4; matrix products, arithmetic and copies ran while one was open for 0% -> 0% of each run, Pallas kernels for 17% -> 17%
where the time goes in v4:
time: 210 us
  Pallas kernels  62.8 us (30%)
  blocking collectives  51.1 us (24%)
  waiting for transfers between devices  47.9 us (23%)
  starting transfers between devices  44.2 us (21%)
  local copies, waits for them, and re-layouts  2.67 us (1%)
    ppermute x8, starting transfers between devices, moved(): lax.ppermute(x, 'plane', [(i, i + distance) for i in range(planes - dista...  28.6 us
    pallas_call x1, Pallas kernels, head_sharded(): pl.pallas_call(attend_kernel, grid_spec=pltpu.PrefetchScalarGridSpec(num_...  21.5 us
    all_gather x2, blocking collectives, head_sharded(): projected = lax.all_gather(proj, 'peer')  18.4 us
    all_to_all x1, blocking collectives, head_sharded(): lax.all_to_all(gated, 'peer', 0, 0)  17.9 us
    ppermute x8, waiting for transfers between devices, moved(): lax.ppermute(x, 'plane', [(i, i + distance) for i in range(planes - dista...  16.6 us
    all_to_all x1, waiting for transfers between devices, head_sharded(): shares = lax.all_to_all(partial, 'peer', 0, 0)  16 us
    all_to_all x1, waiting for transfers between devices, head_sharded(): lax.all_to_all(gated, 'peer', 0, 0)  15.3 us
    all_to_all x1, blocking collectives, head_sharded(): kv_own = lax.all_to_all(kv, 'peer', 0, 0)  14.8 us
  transfers between devices with their start and end apart: 12, of which 4 were waited for; matrix products, arithmetic and copies ran while one was open for 0% of the time, Pallas kernels for 17%

profile of v4, /device:TPU:0, one launch (start us, length us, event | category | flops | bytes accessed | tf_op | source)
XLA Modules:
  0.0 209.6 jit_solution(13895246882181528198)
XLA Ops:
  2.6 14.8 %all_to_all.30.rest_0_.ko_ref.vo_ref = bf16[8,256,128]{2,1,0:T(8,128)(2,1)S(1)} all-to-all(bf16[8,256,128]{2,1,0:T(8,128)(2,1)S(1)} %pack_kv.1), channel_id=1, replica_groups=mesh['plane'=4,'peer'=8,'tp'=1] {'peer'}, dimensions={0} | all-to-all | bytes 1048576 | tf_op jit(solution)/shard_map/all_to_all | solution.py:598
  17.5 1.2 pack_queries.1
  18.6 3.7 %all-to-all-start.1 = ((bf16[8,512,128]{2,1,0:T(8,128)(2,1)}), bf16[8,512,128]{2,1,0:T(8,128)(2,1)S(1)}, u32[]{:S(2)}, u32[]{:S(2)}) async-start(bf16[8,512,128]{2,1,0:T(8,128)(2,1)} %pack_queries.1), calls=%async_computation.1 | async-start | bytes 2097152 | tf_op jit(solution)/shard_map/all_to_all | solution.py:610
  22.3 3.5 %collective-permute-start = (bf16[8,256,128]{2,1,0:T(8,128)(2,1)S(1)}, bf16[8,256,128]{2,1,0:T(8,128)(2,1)S(1)}, u32[]{:S(2)}, u32[]{:S(2)}) collective-permute-start(bf16[8,256,128]{2,1,0:T(8,128)(2,1)S(1)} %all_to_all.30.rest_0_.ko_ref.vo_ref), channel_id=1, source_target_pairs={{0,8},{8,16},{16,24},{1,9},{9,17},{17,25},{2,10},{10,18},{18,26},{... | collective-permute-start | bytes 1572872 | tf_op jit(solution)/shard_map/ppermute | solution.py:590
  25.9 11.7 %collective-permute-done.k1_ref.v1_ref = bf16[8,256,128]{2,1,0:T(8,128)(2,1)S(1)} collective-permute-done((bf16[8,256,128]{2,1,0:T(8,128)(2,1)S(1)}, bf16[8,256,128]{2,1,0:T(8,128)(2,1)S(1)}, u32[]{:S(2)}, u32[]{:S(2)}) %collective-permute-start) | collective-permute-done | bytes 524320 | tf_op jit(solution)/shard_map/ppermute | solution.py:590
  37.5 5.2 %collective-permute-start.1 = (bf16[8,256,128]{2,1,0:T(8,128)(2,1)S(1)}, bf16[8,256,128]{2,1,0:T(8,128)(2,1)}, u32[]{:S(2)}, u32[]{:S(2)}) collective-permute-start(bf16[8,256,128]{2,1,0:T(8,128)(2,1)S(1)} %collective-permute-done.k1_ref.v1_ref), channel_id=1, source_target_pairs={{0,8},{8,16},{16,24},{1,9},{9,17},{17,25},{2,10},{10,18},{18,26},{... | collective-permute-start | bytes 1572872 | tf_op jit(solution)/shard_map/ppermute | solution.py:590
  42.8 1.2 pack_gates.1
  43.9 3.8 %all-to-all-start.2 = ((bf16[8,528,128]{2,1,0:T(8,128)(2,1)}), bf16[8,528,128]{2,1,0:T(8,128)(2,1)S(1)}, u32[]{:S(2)}, u32[]{:S(2)}) async-start(bf16[8,528,128]{2,1,0:T(8,128)(2,1)} %pack_gates.1), calls=%async_computation.2 | async-start | bytes 2162688 | tf_op jit(solution)/shard_map/all_to_all | solution.py:622
  47.9 4.9 %collective-permute-done.1.k2_ref.v2_ref = bf16[8,256,128]{2,1,0:T(8,128)(2,1)} collective-permute-done((bf16[8,256,128]{2,1,0:T(8,128)(2,1)S(1)}, bf16[8,256,128]{2,1,0:T(8,128)(2,1)}, u32[]{:S(2)}, u32[]{:S(2)}) %collective-permute-start.1) | collective-permute-done | bytes 524320 | tf_op jit(solution)/shard_map/ppermute | solution.py:590
  52.8 21.5 %attend.1 = (bf16[8,512,128]{2,1,0:T(8,128)(2,1)}, f32[8,136,256]{2,1,0:T(8,128)}) custom-call(s32[2]{0:T(128)S(1)} %pad_add_fusion.place_ref, bf16[8,512,128]{2,1,0:T(8,128)(2,1)S(1)} %all-to-all-done.1.q_ref.rest_1_, bf16[8,256,128]{2,1,0:T(8,128)(2,1)S(1)} %all_to_all.30.rest_0_.ko_ref.vo_ref, bf16[8,256,128]{2,1,0:T(8,128)(2,1)S(1)} %all_to_all.30.rest_0_.ko_ref.vo_ref, ...), custom_call_target="tpu_custom_call" | custom-call | flops 5000000000 | bytes 4000000 | tf_op jit(solution)/shard_map/attend/pallas_call | solution.py:633
  75.6 4.4 %all-to-all-start.3 = ((f32[8,136,256]{2,1,0:T(8,128)}), f32[8,136,256]{2,1,0:T(8,128)}, u32[]{:S(2)}, u32[]{:S(2)}) async-start(f32[8,136,256]{2,1,0:T(8,128)} %after.1), calls=%async_computation.3 | async-start | bytes 2228224 | tf_op jit(solution)/shard_map/all_to_all | solution.py:654
  80.1 16.0 %all-to-all-done.3.part_ref = f32[8,136,256]{2,1,0:T(8,128)} async-done(((f32[8,136,256]{2,1,0:T(8,128)}), f32[8,136,256]{2,1,0:T(8,128)}, u32[]{:S(2)}, u32[]{:S(2)}) %all-to-all-start.3) | async-done | bytes 1114144 | tf_op jit(solution)/shard_map/all_to_all | solution.py:654
  96.1 2.0 project.1
  98.1 9.3 %all-gather = bf16[1152,256]{1,0:T(8,128)(2,1)S(1)} all-gather(bf16[144,256]{1,0:T(8,128)(2,1)} %project.1), channel_id=2, replica_groups=mesh['plane'=4,'peer'=8,'tp'=1] {'peer'}, dimensions={0}, use_global_device_ids=true | all-gather | bytes 663552 | tf_op jit(solution)/shard_map/all_gather | solution.py:699
  107.5 3.8 %states.2 = (bf16[8,512,128]{2,1,0:T(8,128)(2,1)S(1)}, f32[8,512,128]{2,1,0:T(8,128)S(1)}, bf16[528,128]{1,0:T(8,128)(2,1)S(1)}) custom-call(bf16[8,512,128]{2,1,0:T(8,128)(2,1)S(1)} %copy-done.6, bf16[8,144,256]{2,1,0:T(8,128)(2,1)S(1)} %bitcast.23, bf16[8,528,128]{2,1,0:T(8,128)(2,1)S(1)} %all-to-all-done.2.side_ref, f32[8,128]{1,0:T(8,128)S(1)} %broadcast_in_dim.2.rates_ref), custom_call_target="tpu_custom_call" | custom-call | flops 1000000000 | bytes 4000000 | tf_op jit(solution)/shard_map/states/pallas_call | solution.py:671
  111.3 4.5 %collective-permute-start.2 = (bf16[528,128]{1,0:T(8,128)(2,1)S(1)}, bf16[528,128]{1,0:T(8,128)(2,1)S(1)}, u32[]{:S(2)}, u32[]{:S(2)}) collective-permute-start(bf16[528,128]{1,0:T(8,128)(2,1)S(1)} %get-tuple-element.24), channel_id=1, source_target_pairs={{0,8},{8,16},{16,24},{1,9},{9,17},{17,25},{2,10},{10,18},{18,26},{... | collective-permute-start | bytes 405512 | tf_op jit(solution)/shard_map/ppermute | solution.py:590
  115.8 4.5 %collective-permute-start.3 = (bf16[528,128]{1,0:T(8,128)(2,1)S(1)}, bf16[528,128]{1,0:T(8,128)(2,1)S(1)}, u32[]{:S(2)}, u32[]{:S(2)}) collective-permute-start(bf16[528,128]{1,0:T(8,128)(2,1)S(1)} %get-tuple-element.24), channel_id=1, source_target_pairs={{0,16},{8,24},{1,17},{9,25},{2,18},{10,26},{3,19},{11,27},{4,20},{... | collective-permute-start | bytes 405512 | tf_op jit(solution)/shard_map/ppermute | solution.py:590
  120.3 1.3 collective-permute-start.4
  121.6 6.7 %local.2 = (f32[8,512,128]{2,1,0:T(8,128)S(1)}, f32[8,512,128]{2,1,0:T(8,128)S(1)}) custom-call(bf16[8,512,128]{2,1,0:T(8,128)(2,1)S(1)} %get-tuple-element.20.x_ref, bf16[8,144,256]{2,1,0:T(8,128)(2,1)S(1)} %bitcast.24, bf16[8,528,128]{2,1,0:T(8,128)(2,1)S(1)} %all-to-all-done.2.side_ref, f32[8,128]{1,0:T(8,128)S(1)} %broadcast_in_dim.2.rates_ref, ...), custom_call_target="tpu_custom_call" | custom-call | flops 2000000000 | bytes 5000000 | tf_op jit(solution)/shard_map/local/pallas_call | solution.py:680
  128.3 5.8 %gated.2 = (bf16[8,512,128]{2,1,0:T(8,128)(2,1)}, f32[8,512,128]{2,1,0:T(8,128)}) custom-call(f32[8,512,128]{2,1,0:T(8,128)S(1)} %get-tuple-element.22.y_ref, f32[8,512,128]{2,1,0:T(8,128)S(1)} %get-tuple-element.23.silu_ref, bf16[8,144,256]{2,1,0:T(8,128)(2,1)S(1)} %bitcast.25, bf16[8,528,128]{2,1,0:T(8,128)(2,1)S(1)} %all-to-all-done.2.side_ref, ...), custom_call_target="tpu_custom_call" | custom-call | flops 1000000000 | bytes 5000000 | tf_op jit(solution)/shard_map/gated/pallas_call | solution.py:687
  134.1 3.7 %all-to-all-start.4 = ((bf16[8,512,128]{2,1,0:T(8,128)(2,1)}), bf16[8,512,128]{2,1,0:T(8,128)(2,1)S(1)}, u32[]{:S(2)}, u32[]{:S(2)}) async-start(bf16[8,512,128]{2,1,0:T(8,128)(2,1)} %get-tuple-element.25), calls=%async_computation.4 | async-start | bytes 2097152 | tf_op jit(solution)/shard_map/all_to_all | solution.py:716
  137.8 15.3 %all-to-all-done.4.g_ref = bf16[8,512,128]{2,1,0:T(8,128)(2,1)S(1)} async-done(((bf16[8,512,128]{2,1,0:T(8,128)(2,1)}), bf16[8,512,128]{2,1,0:T(8,128)(2,1)S(1)}, u32[]{:S(2)}, u32[]{:S(2)}) %all-to-all-start.4) | async-done | bytes 1048608 | tf_op jit(solution)/shard_map/all_to_all | solution.py:716
  153.1 3.6 %finish_first.1 = (f32[128,4096]{1,0:T(8,128)}, bf16[144,256]{1,0:T(8,128)(2,1)S(1)}) custom-call(bf16[8,512,128]{2,1,0:T(8,128)(2,1)S(1)} %all-to-all-done.4.g_ref, f32[32,128]{1,0:T(8,128)S(1)} %bitcast.27, bf16[4096,256]{1,0:T(8,128)(2,1)} %rest_0_.1), custom_call_target="tpu_custom_call" | custom-call | tf_op jit(solution)/shard_map/finish_first/pallas_call | solution.py:701
  156.7 9.0 %all-gather.1 = bf16[1152,256]{1,0:T(8,128)(2,1)S(1)} all-gather(bf16[144,256]{1,0:T(8,128)(2,1)S(1)} %get-tuple-element.28), channel_id=3, replica_groups=mesh['plane'=4,'peer'=8,'tp'=1] {'peer'}, dimensions={0}, use_global_device_ids=true | all-gather | bytes 663552 | tf_op jit(solution)/shard_map/all_gather | solution.py:717
  165.7 3.8 %states.3 = (bf16[8,512,128]{2,1,0:T(8,128)(2,1)S(1)}, f32[8,512,128]{2,1,0:T(8,128)S(1)}, bf16[528,128]{1,0:T(8,128)(2,1)S(1)}) custom-call(f32[8,512,128]{2,1,0:T(8,128)S(1)} %copy-done, bf16[8,144,256]{2,1,0:T(8,128)(2,1)S(1)} %bitcast.20, bf16[8,528,128]{2,1,0:T(8,128)(2,1)S(1)} %all-to-all-done.2.side_ref, f32[8,128]{1,0:T(8,128)S(1)} %broadcast_in_dim.2.rates_ref, ...), custom_call_target="tpu_custom_call" | custom-call | flops 1000000000 | bytes 4000000 | tf_op jit(solution)/shard_map/states/pallas_call | solution.py:671
  169.6 3.0 %collective-permute-start.5 = (bf16[528,128]{1,0:T(8,128)(2,1)S(1)}, bf16[528,128]{1,0:T(8,128)(2,1)S(1)}, u32[]{:S(2)}, u32[]{:S(2)}) collective-permute-start(bf16[528,128]{1,0:T(8,128)(2,1)S(1)} %get-tuple-element.33), channel_id=1, source_target_pairs={{0,8},{8,16},{16,24},{1,9},{9,17},{17,25},{2,10},{10,18},{18,26},{... | collective-permute-start | bytes 405512 | tf_op jit(solution)/shard_map/ppermute | solution.py:590
  172.6 5.3 %collective-permute-start.6 = (bf16[528,128]{1,0:T(8,128)(2,1)S(1)}, bf16[528,128]{1,0:T(8,128)(2,1)S(1)}, u32[]{:S(2)}, u32[]{:S(2)}) collective-permute-start(bf16[528,128]{1,0:T(8,128)(2,1)S(1)} %get-tuple-element.33), channel_id=1, source_target_pairs={{0,16},{8,24},{1,17},{9,25},{2,18},{10,26},{3,19},{11,27},{4,20},{... | collective-permute-start | bytes 405512 | tf_op jit(solution)/shard_map/ppermute | solution.py:590
  177.9 1.3 collective-permute-start.7
  179.2 6.7 %local.3 = (f32[8,512,128]{2,1,0:T(8,128)S(1)}, f32[8,512,128]{2,1,0:T(8,128)S(1)}) custom-call(bf16[8,512,128]{2,1,0:T(8,128)(2,1)S(1)} %get-tuple-element.29.x_ref, bf16[8,144,256]{2,1,0:T(8,128)(2,1)S(1)} %bitcast.21, bf16[8,528,128]{2,1,0:T(8,128)(2,1)S(1)} %all-to-all-done.2.side_ref, f32[8,128]{1,0:T(8,128)S(1)} %broadcast_in_dim.2.rates_ref, ...), custom_call_target="tpu_custom_call" | custom-call | flops 2000000000 | bytes 5000000 | tf_op jit(solution)/shard_map/local/pallas_call | solution.py:680
  185.9 4.1 %gated.3 = bf16[8,512,128]{2,1,0:T(8,128)(2,1)S(1)} custom-call(f32[8,512,128]{2,1,0:T(8,128)S(1)} %get-tuple-element.31.y_ref, f32[8,512,128]{2,1,0:T(8,128)S(1)} %get-tuple-element.32.silu_ref, bf16[8,144,256]{2,1,0:T(8,128)(2,1)S(1)} %bitcast.22, bf16[8,528,128]{2,1,0:T(8,128)(2,1)S(1)} %all-to-all-done.2.side_ref, ...), custom_call_target="tpu_custom_call" | custom-call | flops 1000000000 | bytes 5000000 | tf_op jit(solution)/shard_map/gated/pallas_call | solution.py:687
  190.0 17.9 %all_to_all.31.g_ref = bf16[8,512,128]{2,1,0:T(8,128)(2,1)S(1)} all-to-all(bf16[8,512,128]{2,1,0:T(8,128)(2,1)S(1)} %gated.3), channel_id=1, replica_groups=mesh['plane'=4,'peer'=8,'tp'=1] {'peer'}, dimensions={0} | all-to-all | bytes 2097152 | tf_op jit(solution)/shard_map/all_to_all | solution.py:726
  207.9 1.7 finish_second.1
  (35 shorter events, 3.6 us)
Async XLA Ops:
  0.6 1.0 copy-start.2
  1.6 0.9 copy-start.3
  2.5 14.9 %copy-start.5 = (bf16[128,4096]{1,0:T(8,128)(2,1)S(1)}, bf16[128,4096]{1,0:T(8,128)(2,1)}, u32[]{:S(2)}) copy-start(bf16[128,4096]{1,0:T(8,128)(2,1)} %x_ref.2) | copy-start | bytes 3145732
  18.6 7.2 %copy-start.7 = (s32[128,64]{0,1:T(8,128)S(1)}, s32[128,64]{0,1:T(8,128)}, u32[]{:S(2)}) copy-start(s32[128,64]{0,1:T(8,128)} %param.12) | copy-start | bytes 98308
  18.6 24.1 %copy-start.1 = (bf16[128,4096]{1,0:T(8,128)(2,1)S(1)}, bf16[128,4096]{1,0:T(8,128)(2,1)}, u32[]{:S(2)}) copy-start(bf16[128,4096]{1,0:T(8,128)(2,1)} %x_ref.3) | copy-start | bytes 3145732
  18.6 24.1 %all-to-all-start.1 = ((bf16[8,512,128]{2,1,0:T(8,128)(2,1)}), bf16[8,512,128]{2,1,0:T(8,128)(2,1)S(1)}, u32[]{:S(2)}, u32[]{:S(2)}) async-start(bf16[8,512,128]{2,1,0:T(8,128)(2,1)} %pack_queries.1), calls=%async_computation.1 | async-start | bytes 2097152 | tf_op jit(solution)/shard_map/all_to_all | solution.py:610
  22.3 15.2 %collective-permute-start = (bf16[8,256,128]{2,1,0:T(8,128)(2,1)S(1)}, bf16[8,256,128]{2,1,0:T(8,128)(2,1)S(1)}, u32[]{:S(2)}, u32[]{:S(2)}) collective-permute-start(bf16[8,256,128]{2,1,0:T(8,128)(2,1)S(1)} %all_to_all.30.rest_0_.ko_ref.vo_ref), channel_id=1, source_target_pairs={{0,8},{8,16},{16,24},{1,9},{9,17},{17,25},{2,10},{10,18},{18,26},{... | collective-permute-start | bytes 1572872 | tf_op jit(solution)/shard_map/ppermute | solution.py:590
  37.5 15.2 %collective-permute-start.1 = (bf16[8,256,128]{2,1,0:T(8,128)(2,1)S(1)}, bf16[8,256,128]{2,1,0:T(8,128)(2,1)}, u32[]{:S(2)}, u32[]{:S(2)}) collective-permute-start(bf16[8,256,128]{2,1,0:T(8,128)(2,1)S(1)} %collective-permute-done.k1_ref.v1_ref), channel_id=1, source_target_pairs={{0,8},{8,16},{16,24},{1,9},{9,17},{17,25},{2,10},{10,18},{18,26},{... | collective-permute-start | bytes 1572872 | tf_op jit(solution)/shard_map/ppermute | solution.py:590
  43.9 30.4 %all-to-all-start.2 = ((bf16[8,528,128]{2,1,0:T(8,128)(2,1)}), bf16[8,528,128]{2,1,0:T(8,128)(2,1)S(1)}, u32[]{:S(2)}, u32[]{:S(2)}) async-start(bf16[8,528,128]{2,1,0:T(8,128)(2,1)} %pack_gates.1), calls=%async_computation.2 | async-start | bytes 2162688 | tf_op jit(solution)/shard_map/all_to_all | solution.py:622
  74.9 5.1 %copy-start.8 = (f32[64]{0:T(128)S(1)}, f32[64]{0:T(128)}, u32[]{:S(2)}) copy-start(f32[64]{0:T(128)} %param.11) | copy-start | bytes 772
  75.6 31.9 %copy-start.6 = (bf16[8,512,128]{2,1,0:T(8,128)(2,1)S(1)}, bf16[8,512,128]{2,1,0:T(8,128)(2,1)}, u32[]{:S(2)}) copy-start(bf16[8,512,128]{2,1,0:T(8,128)(2,1)} %get-tuple-element.18.x_ref) | copy-start | bytes 3145732
  75.6 20.5 %all-to-all-start.3 = ((f32[8,136,256]{2,1,0:T(8,128)}), f32[8,136,256]{2,1,0:T(8,128)}, u32[]{:S(2)}, u32[]{:S(2)}) async-start(f32[8,136,256]{2,1,0:T(8,128)} %after.1), calls=%async_computation.3 | async-start | bytes 2228224 | tf_op jit(solution)/shard_map/all_to_all | solution.py:654
  111.3 17.0 %collective-permute-start.2 = (bf16[528,128]{1,0:T(8,128)(2,1)S(1)}, bf16[528,128]{1,0:T(8,128)(2,1)S(1)}, u32[]{:S(2)}, u32[]{:S(2)}) collective-permute-start(bf16[528,128]{1,0:T(8,128)(2,1)S(1)} %get-tuple-element.24), channel_id=1, source_target_pairs={{0,8},{8,16},{16,24},{1,9},{9,17},{17,25},{2,10},{10,18},{18,26},{... | collective-permute-start | bytes 405512 | tf_op jit(solution)/shard_map/ppermute | solution.py:590
  115.8 12.5 %collective-permute-start.3 = (bf16[528,128]{1,0:T(8,128)(2,1)S(1)}, bf16[528,128]{1,0:T(8,128)(2,1)S(1)}, u32[]{:S(2)}, u32[]{:S(2)}) collective-permute-start(bf16[528,128]{1,0:T(8,128)(2,1)S(1)} %get-tuple-element.24), channel_id=1, source_target_pairs={{0,16},{8,24},{1,17},{9,25},{2,18},{10,26},{3,19},{11,27},{4,20},{... | collective-permute-start | bytes 405512 | tf_op jit(solution)/shard_map/ppermute | solution.py:590
  120.3 8.0 %collective-permute-start.4 = (bf16[528,128]{1,0:T(8,128)(2,1)S(1)}, bf16[528,128]{1,0:T(8,128)(2,1)S(1)}, u32[]{:S(2)}, u32[]{:S(2)}) collective-permute-start(bf16[528,128]{1,0:T(8,128)(2,1)S(1)} %get-tuple-element.24), channel_id=1, source_target_pairs={{0,24},{1,25},{2,26},{3,27},{4,28},{5,29},{6,30},{7,31}} | collective-permute-start | bytes 405512 | tf_op jit(solution)/shard_map/ppermute | solution.py:590
  134.1 3.7 %copy-start.4 = (f32[4096]{0:T(1024)S(1)}, f32[4096]{0:T(1024)}, u32[]{:S(2)}) copy-start(f32[4096]{0:T(1024)} %param.14) | copy-start | bytes 49156
  134.1 19.0 %all-to-all-start.4 = ((bf16[8,512,128]{2,1,0:T(8,128)(2,1)}), bf16[8,512,128]{2,1,0:T(8,128)(2,1)S(1)}, u32[]{:S(2)}, u32[]{:S(2)}) async-start(bf16[8,512,128]{2,1,0:T(8,128)(2,1)} %get-tuple-element.25), calls=%async_computation.4 | async-start | bytes 2097152 | tf_op jit(solution)/shard_map/all_to_all | solution.py:716
  153.1 12.7 %copy-start = (f32[8,512,128]{2,1,0:T(8,128)S(1)}, f32[8,512,128]{2,1,0:T(8,128)}, u32[]{:S(2)}) copy-start(f32[8,512,128]{2,1,0:T(8,128)} %get-tuple-element.27.x_ref) | copy-start | bytes 6291460
  169.6 16.3 %collective-permute-start.5 = (bf16[528,128]{1,0:T(8,128)(2,1)S(1)}, bf16[528,128]{1,0:T(8,128)(2,1)S(1)}, u32[]{:S(2)}, u32[]{:S(2)}) collective-permute-start(bf16[528,128]{1,0:T(8,128)(2,1)S(1)} %get-tuple-element.33), channel_id=1, source_target_pairs={{0,8},{8,16},{16,24},{1,9},{9,17},{17,25},{2,10},{10,18},{18,26},{... | collective-permute-start | bytes 405512 | tf_op jit(solution)/shard_map/ppermute | solution.py:590
  172.6 13.3 %collective-permute-start.6 = (bf16[528,128]{1,0:T(8,128)(2,1)S(1)}, bf16[528,128]{1,0:T(8,128)(2,1)S(1)}, u32[]{:S(2)}, u32[]{:S(2)}) collective-permute-start(bf16[528,128]{1,0:T(8,128)(2,1)S(1)} %get-tuple-element.33), channel_id=1, source_target_pairs={{0,16},{8,24},{1,17},{9,25},{2,18},{10,26},{3,19},{11,27},{4,20},{... | collective-permute-start | bytes 405512 | tf_op jit(solution)/shard_map/ppermute | solution.py:590
  177.9 8.0 %collective-permute-start.7 = (bf16[528,128]{1,0:T(8,128)(2,1)S(1)}, bf16[528,128]{1,0:T(8,128)(2,1)S(1)}, u32[]{:S(2)}, u32[]{:S(2)}) collective-permute-start(bf16[528,128]{1,0:T(8,128)(2,1)S(1)} %get-tuple-element.33), channel_id=1, source_target_pairs={{0,24},{1,25},{2,26},{3,27},{4,28},{5,29},{6,30},{7,31}} | collective-permute-start | bytes 405512 | tf_op jit(solution)/shard_map/ppermute | solution.py:590
